TPU v7x, 32 devices: a whole 2x2x4 slice. The times are simulated.
32 devices in a mesh: tm: 4 (over z), gx: 4 (over y, x), gy: 2 (over core).
Axes of the slice: x: 2, y: 2, z: 4, core: 2. Of those that a mesh axis runs over, the one named last changes fastest.
Arguments:
- states: float32 [8, 256, 256], P('tm', 'gx', 'gy'), may hold values from 0.5 to 1.5
- bed: float32 [256, 256], P('gx', 'gy'), may hold values from -3 to 3
- background_state: float32 [256, 256], P('gx', 'gy'), may hold values from 0.5 to 1.5
- ice_mask: int32 [256, 256], P('gx', 'gy'), may hold values 0 or 1
- flow_rate: float32 [256, 256], P('gx', 'gy'), may hold values from 0.02 to 0.1
- obs_cell: int32 [8, 4, 2, 512], P('tm', 'gx', 'gy'), may hold values from 0 to 8191
- obs_value: float32 [8, 4, 2, 512], P('tm', 'gx', 'gy'), may hold values from 0.5 to 1.5
Outputs:
- states_out: float32 [8, 256, 256], P('tm', 'gx', 'gy')
- bed_out: float32 [256, 256], P('gx', 'gy')
All inputs are finite; a program needn't handle non-finite values. No bound on the sum of `ice_mask` on one device may be relied on, other than what follows from the above.
Results may differ from a plain program's by a relative error of at most 0.0001.
Values sent between devices are 32-bit elements; how exact they have to be, the bound alone decides.
No kernel may reach another device: no remote copies, remote signals or barrier semaphores. Data moves between devices by JAX's collectives and lax.ppermute only.
A program may use at most 64 MiB of HBM per device.

v0:
```python
import jax
import jax.numpy as jnp
from jax import lax
from jax.sharding import PartitionSpec as P

STEPS = 4
OUTER = 2


bed_rate = 0.1
state_rate = 0.5


def with_halo(value, sides, width):
    for axis, dim in sides:
        count, length = (lax.axis_size(axis), value.shape[dim])
        up = [(i, (i + 1) % count) for i in range(count - 1)]
        down = [(j, i) for i, j in up]
        last = lax.slice_in_dim(value, length - width, length, axis=dim)
        first = lax.slice_in_dim(value, 0, width, axis=dim)
        before = lax.ppermute(last, axis, up)
        after = lax.ppermute(first, axis, down)
        value = jnp.concatenate([before, value, after], axis=dim)
    return value


def from_behind(block, axis, distance):
    devices = range(lax.axis_size(axis))
    route = [(i - distance, i) for i in devices if i - distance in devices]
    return lax.ppermute(block, axis, route)


def advance(thick, ground, maskf, rate):
    surface = ground + thick
    open_x = maskf[1:, :] * maskf[:-1, :]
    coef_x = 0.5 * (rate[1:, :] + rate[:-1, :]) * open_x
    mean_x = 0.5 * (thick[1:, :] + thick[:-1, :])
    flux_x = coef_x * mean_x * mean_x * (surface[1:, :] - surface[:-1, :])
    open_y = maskf[:, 1:] * maskf[:, :-1]
    coef_y = 0.5 * (rate[:, 1:] + rate[:, :-1]) * open_y
    mean_y = 0.5 * (thick[:, 1:] + thick[:, :-1])
    flux_y = coef_y * mean_y * mean_y * (surface[:, 1:] - surface[:, :-1])
    change = flux_x[1:, 1:-1] - flux_x[:-1, 1:-1] + (flux_y[1:-1, 1:] - flux_y[1:-1, :-1])
    return thick[1:-1, 1:-1] + change


def batch_advance(thick, ground, maskf, rate):
    return jax.vmap(advance, in_axes=(0, None, None, None))(thick, ground, maskf, rate)


def inner(array, width):
    return array[..., width : array.shape[-2] - width, width : array.shape[-1] - width]


def per_device(states, bed, background_state, ice_mask, flow_rate, obs_cell, obs_value):
    slices_here, rows_here, cols_here = states.shape
    maskf = ice_mask.astype(jnp.float32)
    offsets = (jnp.arange(slices_here, dtype=jnp.int32) * (rows_here * cols_here))[:, None]
    cell_index = (obs_cell.reshape(slices_here, -1) + offsets).reshape(-1)
    observed = obs_value.reshape(-1)
    first_device = lax.axis_index("tm") == 0
    reach = 2 * STEPS
    mask_pad, rate_pad = (
        with_halo(maskf, (("gx", 0), ("gy", 1)), reach),
        with_halo(flow_rate, (("gx", 0), ("gy", 1)), reach),
    )
    bed_prior = bed
    for outer in range(OUTER):
        wide_path = []
        stacked = jnp.concatenate([bed[None], states], axis=0)
        wide = with_halo(stacked, (("gx", 1), ("gy", 2)), reach)
        bed_pad = wide[0]
        walker = wide[1:]
        for step in range(STEPS):
            wide_path.append(walker)
            walker = batch_advance(
                walker, inner(bed_pad, step), inner(mask_pad, step), inner(rate_pad, step)
            )
        final = inner(walker, STEPS)
        incoming = from_behind(final[slices_here - 1], "tm", 1)
        start_state = jnp.where(first_device, background_state, incoming)
        previous = jnp.concatenate([start_state[None], final[:-1]], axis=0)
        misfit = states - previous
        later = from_behind(misfit[0], "tm", -1)
        following = jnp.concatenate([misfit[1:], later[None]], axis=0)
        predicted = final.reshape(-1)[cell_index]
        residual = predicted - observed
        spread = (
            jnp.zeros((slices_here * rows_here * cols_here,), jnp.float32)
            .at[cell_index]
            .add(residual)
        )
        adjoint = spread.reshape(slices_here, rows_here, cols_here) - following
        bed_grad = jnp.zeros((rows_here, cols_here), jnp.float32)
        wide_adjoint = with_halo(adjoint, (("gx", 1), ("gy", 2)), STEPS)
        for step in reversed(range(STEPS)):
            radius = step + 1
            thick_in = inner(wide_path[step], reach - step - (radius + 1))
            cut = reach - (radius + 1)
            mask_here = inner(mask_pad, cut)
            rate_here = inner(rate_pad, cut)

            def wide_step(thick_arg, ground_arg):
                return batch_advance(thick_arg, ground_arg, mask_here, rate_here)

            _, pull = jax.vjp(wide_step, thick_in, inner(bed_pad, cut))
            grad_thick, grad_ground = pull(wide_adjoint)
            wide_adjoint = inner(grad_thick, 2)
            bed_grad = bed_grad + inner(grad_ground, radius + 1)
        adjoint = wide_adjoint
        total = lax.psum(bed_grad, "tm")
        bed = bed - bed_rate * (total + (bed - bed_prior))
        states = states - state_rate * (misfit + adjoint)
    return (states, bed)


def solution(mesh):
    placed = (
        P("tm", "gx", "gy"),
        P("gx", "gy"),
        P("gx", "gy"),
        P("gx", "gy"),
        P("gx", "gy"),
        P("tm", "gx", "gy", None),
        P("tm", "gx", "gy", None),
    )
    return jax.shard_map(
        per_device,
        mesh=mesh,
        in_specs=placed,
        out_specs=(P("tm", "gx", "gy"), P("gx", "gy")),
        check_vma=False,
    )
```

profile of v0, /device:TPU:0, one launch (start us, length us, event | category | flops | bytes accessed | tf_op | source)
XLA Modules:
  0.0 171.4 jit_solution(18293389572790365645)
XLA Ops:
  1.4 1.4 collective-permute-start.9
  2.9 5.5 %collective-permute-start.8 = (f32[8,128]{1,0:T(8,128)S(1)}, f32[8,128]{1,0:T(8,128)S(1)}, u32[]{:S(2)}, u32[]{:S(2)}) collective-permute-start(f32[8,128]{1,0:T(8,128)S(1)} %get-tuple-element.140), channel_id=1, source_target_pairs={{0,2},{2,4},{4,6},{1,3},{3,5},{5,7},{8,10},{10,12},{12,14},{9,11},... | collective-permute-start | bytes 12296 | tf_op jit(solution)/shard_map/ppermute | solution.py:21
  9.1 4.8 %collective-permute-start.4 = (f32[8,128]{1,0:T(8,128)S(1)}, f32[8,128]{1,0:T(8,128)S(1)}, u32[]{:S(2)}, u32[]{:S(2)}) collective-permute-start(f32[8,128]{1,0:T(8,128)S(1)} %get-tuple-element.139), channel_id=1, source_target_pairs={{0,2},{2,4},{4,6},{1,3},{3,5},{5,7},{8,10},{10,12},{12,14},{9,11},... | collective-permute-start | bytes 12296 | tf_op jit(solution)/shard_map/ppermute | solution.py:21
  15.2 1.3 collective-permute-start.1
  17.3 5.2 %collective-permute-start = (f32[3,8,128]{2,1,0:T(8,128)S(1)}, f32[3,8,128]{2,1,0:T(8,128)S(1)}, u32[]{:S(2)}, u32[]{:S(2)}) collective-permute-start(f32[3,8,128]{2,1,0:T(8,128)S(1)} %get-tuple-element.120), channel_id=1, source_target_pairs={{0,2},{2,4},{4,6},{1,3},{3,5},{5,7},{8,10},{10,12},{12,14},{9,11},... | collective-permute-start | bytes 36872 | tf_op jit(solution)/shard_map/ppermute | solution.py:21
  23.9 3.0 %collective-permute-start.10 = (f32[80,8]{1,0:T(8,128)S(1)}, f32[80,8]{1,0:T(8,128)S(1)}, u32[]{:S(2)}, u32[]{:S(2)}) collective-permute-start(f32[80,8]{1,0:T(8,128)S(1)} %get-tuple-element.136), channel_id=1, source_target_pairs={{0,1},{2,3},{4,5},{6,7},{8,9},{10,11},{12,13},{14,15},{16,17},{18,... | collective-permute-start | bytes 7688 | tf_op jit(solution)/shard_map/ppermute | solution.py:21
  28.4 3.0 %collective-permute-start.6 = (f32[80,8]{1,0:T(8,128)S(1)}, f32[80,8]{1,0:T(8,128)S(1)}, u32[]{:S(2)}, u32[]{:S(2)}) collective-permute-start(f32[80,8]{1,0:T(8,128)S(1)} %get-tuple-element.134), channel_id=1, source_target_pairs={{0,1},{2,3},{4,5},{6,7},{8,9},{10,11},{12,13},{14,15},{16,17},{18,... | collective-permute-start | bytes 7688 | tf_op jit(solution)/shard_map/ppermute | solution.py:21
  35.5 3.0 %collective-permute-start.2 = (f32[3,80,8]{2,1,0:T(8,128)S(1)}, f32[3,80,8]{2,1,0:T(8,128)S(1)}, u32[]{:S(2)}, u32[]{:S(2)}) collective-permute-start(f32[3,80,8]{2,1,0:T(8,128)S(1)} %get-tuple-element.116), channel_id=1, source_target_pairs={{0,1},{2,3},{4,5},{6,7},{8,9},{10,11},{12,13},{14,15},{16,17},{18,... | collective-permute-start | bytes 23048 | tf_op jit(solution)/shard_map/ppermute | solution.py:21
  42.0 3.5 %collective-permute-start.12 = (f32[64,128]{1,0:T(8,128)S(1)}, f32[64,128]{1,0:T(8,128)S(1)}, u32[]{:S(2)}, u32[]{:S(2)}) collective-permute-start(f32[64,128]{1,0:T(8,128)S(1)} %get-tuple-element.112), channel_id=1, source_target_pairs={{0,8},{8,16},{16,24},{1,9},{9,17},{17,25},{2,10},{10,18},{18,26},{... | collective-permute-start | bytes 98312 | tf_op jit(solution)/shard_map/ppermute | solution.py:30
  45.8 1.3 collective-permute-done.12
  48.7 6.2 %gather_fusion = f32[1024]{0:T(1024)S(1)} fusion(f32[16384]{0:T(1024)S(1)} %bitcast.34, s32[1024]{0:T(1024)S(1)} %broadcast_clamp_fusion), kind=kCustom, calls=%fused_computation | custom fusion | bytes 12288 | tf_op jit(solution)/shard_map/gather | solution.py:86
  54.9 5.9 %scatter_custom_fusion = f32[16384]{0:T(1024)S(1)} fusion(s32[1024]{0:T(1024)S(1)} %bitcast.45, f32[1024]{0:T(1024)S(1)} %sub.189, f32[]{:T(128)} %constant.10.clone.1), kind=kCustom, calls=%fused_computation.342 | custom fusion | flops 1024 | bytes 65540 | tf_op jit(solution)/shard_map/scatter-add | solution.py:91
  62.2 5.4 %collective-permute-start.14 = (f32[2,4,128]{2,1,0:T(4,128)S(1)}, f32[2,4,128]{2,1,0:T(4,128)S(1)}, u32[]{:S(2)}, u32[]{:S(2)}) collective-permute-start(f32[2,4,128]{2,1,0:T(4,128)S(1)} %get-tuple-element.130), channel_id=1, source_target_pairs={{0,2},{2,4},{4,6},{1,3},{3,5},{5,7},{8,10},{10,12},{12,14},{9,11},... | collective-permute-start | bytes 12296 | tf_op jit(solution)/shard_map/ppermute | solution.py:21
  70.4 3.0 %collective-permute-start.16 = (f32[2,72,4]{2,1,0:T(8,128)S(1)}, f32[2,72,4]{2,1,0:T(8,128)S(1)}, u32[]{:S(2)}, u32[]{:S(2)}) collective-permute-start(f32[2,72,4]{2,1,0:T(8,128)S(1)} %get-tuple-element.124), channel_id=1, source_target_pairs={{0,1},{2,3},{4,5},{6,7},{8,9},{10,11},{12,13},{14,15},{16,17},{18,... | collective-permute-start | bytes 6920 | tf_op jit(solution)/shard_map/ppermute | solution.py:21
  77.7 21.1 %psum.14 = f32[64,128]{1,0:T(8,128)S(1)} all-reduce(f32[64,128]{1,0:T(8,128)S(1)} %slice_add_fusion.61), channel_id=1, replica_groups=mesh['tm'=4,'gx'=4,'gy'=2] {'tm'}, use_global_device_ids=true, to_apply=%region_5.6 | all-reduce | flops 8192 | bytes 65536 | tf_op jit(solution)/shard_map/psum | solution.py:111
  100.3 5.4 %collective-permute-start.18 = (f32[3,8,128]{2,1,0:T(8,128)S(1)}, f32[3,8,128]{2,1,0:T(8,128)S(1)}, u32[]{:S(2)}, u32[]{:S(2)}) collective-permute-start(f32[3,8,128]{2,1,0:T(8,128)S(1)} %get-tuple-element.118), channel_id=1, source_target_pairs={{0,2},{2,4},{4,6},{1,3},{3,5},{5,7},{8,10},{10,12},{12,14},{9,11},... | collective-permute-start | bytes 36872 | tf_op jit(solution)/shard_map/ppermute | solution.py:21
  105.8 1.4 collective-permute-done.18
  108.5 3.2 %collective-permute-start.20 = (f32[3,80,8]{2,1,0:T(8,128)S(1)}, f32[3,80,8]{2,1,0:T(8,128)S(1)}, u32[]{:S(2)}, u32[]{:S(2)}) collective-permute-start(f32[3,80,8]{2,1,0:T(8,128)S(1)} %get-tuple-element.114), channel_id=1, source_target_pairs={{0,1},{2,3},{4,5},{6,7},{8,9},{10,11},{12,13},{14,15},{16,17},{18,... | collective-permute-start | bytes 23048 | tf_op jit(solution)/shard_map/ppermute | solution.py:21
  116.4 1.5 collective-permute-done.22
  119.5 6.2 %gather_fusion.1 = f32[1024]{0:T(1024)S(1)} fusion(f32[16384]{0:T(1024)S(1)} %bitcast.33, s32[1024]{0:T(1024)S(1)} %broadcast_clamp_fusion), kind=kCustom, calls=%fused_computation.1 | custom fusion | bytes 12288 | tf_op jit(solution)/shard_map/gather | solution.py:86
  125.7 5.9 %scatter_custom_fusion.1 = f32[16384]{0:T(1024)S(1)} fusion(s32[1024]{0:T(1024)S(1)} %bitcast.46, f32[1024]{0:T(1024)S(1)} %sub.217, f32[]{:T(128)} %constant.10.clone.1), kind=kCustom, calls=%fused_computation.340 | custom fusion | flops 1024 | bytes 65540 | tf_op jit(solution)/shard_map/scatter-add | solution.py:91
  133.0 5.7 %collective-permute-start.24 = (f32[2,4,128]{2,1,0:T(4,128)S(1)}, f32[2,4,128]{2,1,0:T(4,128)S(1)}, u32[]{:S(2)}, u32[]{:S(2)}) collective-permute-start(f32[2,4,128]{2,1,0:T(4,128)S(1)} %get-tuple-element.126), channel_id=1, source_target_pairs={{0,2},{2,4},{4,6},{1,3},{3,5},{5,7},{8,10},{10,12},{12,14},{9,11},... | collective-permute-start | bytes 12296 | tf_op jit(solution)/shard_map/ppermute | solution.py:21
  141.4 3.0 %collective-permute-start.26 = (f32[2,72,4]{2,1,0:T(8,128)S(1)}, f32[2,72,4]{2,1,0:T(8,128)S(1)}, u32[]{:S(2)}, u32[]{:S(2)}) collective-permute-start(f32[2,72,4]{2,1,0:T(8,128)S(1)} %get-tuple-element.122), channel_id=1, source_target_pairs={{0,1},{2,3},{4,5},{6,7},{8,9},{10,11},{12,13},{14,15},{16,17},{18,... | collective-permute-start | bytes 6920 | tf_op jit(solution)/shard_map/ppermute | solution.py:21
  148.8 21.2 %psum.15 = f32[64,128]{1,0:T(8,128)S(1)} all-reduce(f32[64,128]{1,0:T(8,128)S(1)} %slice_add_fusion.58), channel_id=1, replica_groups=mesh['tm'=4,'gx'=4,'gy'=2] {'tm'}, use_global_device_ids=true, to_apply=%region_11.12 | all-reduce | flops 8192 | bytes 65536 | tf_op jit(solution)/shard_map/psum | solution.py:111
  (192 shorter events, 42.2 us)
Async XLA Ops:
  1.4 15.9 %collective-permute-start.9 = (f32[8,128]{1,0:T(8,128)S(1)}, f32[8,128]{1,0:T(8,128)S(1)}, u32[]{:S(2)}, u32[]{:S(2)}) collective-permute-start(f32[8,128]{1,0:T(8,128)S(1)} %get-tuple-element.141), channel_id=1, source_target_pairs={{2,0},{4,2},{6,4},{3,1},{5,3},{7,5},{10,8},{12,10},{14,12},{11,9},... | collective-permute-start | bytes 12296 | tf_op jit(solution)/shard_map/ppermute | solution.py:22
  2.9 19.7 %collective-permute-start.8 = (f32[8,128]{1,0:T(8,128)S(1)}, f32[8,128]{1,0:T(8,128)S(1)}, u32[]{:S(2)}, u32[]{:S(2)}) collective-permute-start(f32[8,128]{1,0:T(8,128)S(1)} %get-tuple-element.140), channel_id=1, source_target_pairs={{0,2},{2,4},{4,6},{1,3},{3,5},{5,7},{8,10},{10,12},{12,14},{9,11},... | collective-permute-start | bytes 12296 | tf_op jit(solution)/shard_map/ppermute | solution.py:21
  9.1 14.9 %collective-permute-start.4 = (f32[8,128]{1,0:T(8,128)S(1)}, f32[8,128]{1,0:T(8,128)S(1)}, u32[]{:S(2)}, u32[]{:S(2)}) collective-permute-start(f32[8,128]{1,0:T(8,128)S(1)} %get-tuple-element.139), channel_id=1, source_target_pairs={{0,2},{2,4},{4,6},{1,3},{3,5},{5,7},{8,10},{10,12},{12,14},{9,11},... | collective-permute-start | bytes 12296 | tf_op jit(solution)/shard_map/ppermute | solution.py:21
  13.9 13.1 %collective-permute-start.5 = (f32[8,128]{1,0:T(8,128)S(1)}, f32[8,128]{1,0:T(8,128)S(1)}, u32[]{:S(2)}, u32[]{:S(2)}) collective-permute-start(f32[8,128]{1,0:T(8,128)S(1)} %get-tuple-element.138), channel_id=1, source_target_pairs={{2,0},{4,2},{6,4},{3,1},{5,3},{7,5},{10,8},{12,10},{14,12},{11,9},... | collective-permute-start | bytes 12296 | tf_op jit(solution)/shard_map/ppermute | solution.py:22
  15.2 18.9 %collective-permute-start.1 = (f32[3,8,128]{2,1,0:T(8,128)S(1)}, f32[3,8,128]{2,1,0:T(8,128)S(1)}, u32[]{:S(2)}, u32[]{:S(2)}) collective-permute-start(f32[3,8,128]{2,1,0:T(8,128)S(1)} %get-tuple-element.121), channel_id=1, source_target_pairs={{2,0},{4,2},{6,4},{3,1},{5,3},{7,5},{10,8},{12,10},{14,12},{11,9},... | collective-permute-start | bytes 36872 | tf_op jit(solution)/shard_map/ppermute | solution.py:22
  17.3 16.8 %collective-permute-start = (f32[3,8,128]{2,1,0:T(8,128)S(1)}, f32[3,8,128]{2,1,0:T(8,128)S(1)}, u32[]{:S(2)}, u32[]{:S(2)}) collective-permute-start(f32[3,8,128]{2,1,0:T(8,128)S(1)} %get-tuple-element.120), channel_id=1, source_target_pairs={{0,2},{2,4},{4,6},{1,3},{3,5},{5,7},{8,10},{10,12},{12,14},{9,11},... | collective-permute-start | bytes 36872 | tf_op jit(solution)/shard_map/ppermute | solution.py:21
  22.6 5.8 %collective-permute-start.11 = (f32[80,8]{1,0:T(8,128)S(1)}, f32[80,8]{1,0:T(8,128)S(1)}, u32[]{:S(2)}, u32[]{:S(2)}) collective-permute-start(f32[80,8]{1,0:T(8,128)S(1)} %get-tuple-element.137), channel_id=1, source_target_pairs={{1,0},{3,2},{5,4},{7,6},{9,8},{11,10},{13,12},{15,14},{17,16},{19,... | collective-permute-start | bytes 7688 | tf_op jit(solution)/shard_map/ppermute | solution.py:22
  23.9 7.5 %collective-permute-start.10 = (f32[80,8]{1,0:T(8,128)S(1)}, f32[80,8]{1,0:T(8,128)S(1)}, u32[]{:S(2)}, u32[]{:S(2)}) collective-permute-start(f32[80,8]{1,0:T(8,128)S(1)} %get-tuple-element.136), channel_id=1, source_target_pairs={{0,1},{2,3},{4,5},{6,7},{8,9},{10,11},{12,13},{14,15},{16,17},{18,... | collective-permute-start | bytes 7688 | tf_op jit(solution)/shard_map/ppermute | solution.py:21
  27.1 4.5 %collective-permute-start.7 = (f32[80,8]{1,0:T(8,128)S(1)}, f32[80,8]{1,0:T(8,128)S(1)}, u32[]{:S(2)}, u32[]{:S(2)}) collective-permute-start(f32[80,8]{1,0:T(8,128)S(1)} %get-tuple-element.135), channel_id=1, source_target_pairs={{1,0},{3,2},{5,4},{7,6},{9,8},{11,10},{13,12},{15,14},{17,16},{19,... | collective-permute-start | bytes 7688 | tf_op jit(solution)/shard_map/ppermute | solution.py:22
  34.2 4.5 %collective-permute-start.3 = (f32[3,80,8]{2,1,0:T(8,128)S(1)}, f32[3,80,8]{2,1,0:T(8,128)S(1)}, u32[]{:S(2)}, u32[]{:S(2)}) collective-permute-start(f32[3,80,8]{2,1,0:T(8,128)S(1)} %get-tuple-element.117), channel_id=1, source_target_pairs={{1,0},{3,2},{5,4},{7,6},{9,8},{11,10},{13,12},{15,14},{17,16},{19,... | collective-permute-start | bytes 23048 | tf_op jit(solution)/shard_map/ppermute | solution.py:22
  35.5 4.0 %collective-permute-start.2 = (f32[3,80,8]{2,1,0:T(8,128)S(1)}, f32[3,80,8]{2,1,0:T(8,128)S(1)}, u32[]{:S(2)}, u32[]{:S(2)}) collective-permute-start(f32[3,80,8]{2,1,0:T(8,128)S(1)} %get-tuple-element.116), channel_id=1, source_target_pairs={{0,1},{2,3},{4,5},{6,7},{8,9},{10,11},{12,13},{14,15},{16,17},{18,... | collective-permute-start | bytes 23048 | tf_op jit(solution)/shard_map/ppermute | solution.py:21
  42.0 5.1 %collective-permute-start.12 = (f32[64,128]{1,0:T(8,128)S(1)}, f32[64,128]{1,0:T(8,128)S(1)}, u32[]{:S(2)}, u32[]{:S(2)}) collective-permute-start(f32[64,128]{1,0:T(8,128)S(1)} %get-tuple-element.112), channel_id=1, source_target_pairs={{0,8},{8,16},{16,24},{1,9},{9,17},{17,25},{2,10},{10,18},{18,26},{... | collective-permute-start | bytes 98312 | tf_op jit(solution)/shard_map/ppermute | solution.py:30
  47.1 13.7 %collective-permute-start.13 = (f32[64,128]{1,0:T(8,128)S(1)}, f32[64,128]{1,0:T(8,128)S(1)}, u32[]{:S(2)}, u32[]{:S(2)}) collective-permute-start(f32[64,128]{1,0:T(8,128)S(1)} %get-tuple-element.133), channel_id=1, source_target_pairs={{8,0},{16,8},{24,16},{9,1},{17,9},{25,17},{10,2},{18,10},{26,18},{... | collective-permute-start | bytes 98312 | tf_op jit(solution)/shard_map/ppermute | solution.py:30
  60.9 7.0 %collective-permute-start.15 = (f32[2,4,128]{2,1,0:T(4,128)S(1)}, f32[2,4,128]{2,1,0:T(4,128)S(1)}, u32[]{:S(2)}, u32[]{:S(2)}) collective-permute-start(f32[2,4,128]{2,1,0:T(4,128)S(1)} %get-tuple-element.131), channel_id=1, source_target_pairs={{2,0},{4,2},{6,4},{3,1},{5,3},{7,5},{10,8},{12,10},{14,12},{11,9},... | collective-permute-start | bytes 12296 | tf_op jit(solution)/shard_map/ppermute | solution.py:22
  62.2 6.8 %collective-permute-start.14 = (f32[2,4,128]{2,1,0:T(4,128)S(1)}, f32[2,4,128]{2,1,0:T(4,128)S(1)}, u32[]{:S(2)}, u32[]{:S(2)}) collective-permute-start(f32[2,4,128]{2,1,0:T(4,128)S(1)} %get-tuple-element.130), channel_id=1, source_target_pairs={{0,2},{2,4},{4,6},{1,3},{3,5},{5,7},{8,10},{10,12},{12,14},{9,11},... | collective-permute-start | bytes 12296 | tf_op jit(solution)/shard_map/ppermute | solution.py:21
  69.1 4.5 %collective-permute-start.17 = (f32[2,72,4]{2,1,0:T(8,128)S(1)}, f32[2,72,4]{2,1,0:T(8,128)S(1)}, u32[]{:S(2)}, u32[]{:S(2)}) collective-permute-start(f32[2,72,4]{2,1,0:T(8,128)S(1)} %get-tuple-element.125), channel_id=1, source_target_pairs={{1,0},{3,2},{5,4},{7,6},{9,8},{11,10},{13,12},{15,14},{17,16},{19,... | collective-permute-start | bytes 6920 | tf_op jit(solution)/shard_map/ppermute | solution.py:22
  99.0 6.8 %collective-permute-start.19 = (f32[3,8,128]{2,1,0:T(8,128)S(1)}, f32[3,8,128]{2,1,0:T(8,128)S(1)}, u32[]{:S(2)}, u32[]{:S(2)}) collective-permute-start(f32[3,8,128]{2,1,0:T(8,128)S(1)} %get-tuple-element.119), channel_id=1, source_target_pairs={{2,0},{4,2},{6,4},{3,1},{5,3},{7,5},{10,8},{12,10},{14,12},{11,9},... | collective-permute-start | bytes 36872 | tf_op jit(solution)/shard_map/ppermute | solution.py:22
  100.3 6.8 %collective-permute-start.18 = (f32[3,8,128]{2,1,0:T(8,128)S(1)}, f32[3,8,128]{2,1,0:T(8,128)S(1)}, u32[]{:S(2)}, u32[]{:S(2)}) collective-permute-start(f32[3,8,128]{2,1,0:T(8,128)S(1)} %get-tuple-element.118), channel_id=1, source_target_pairs={{0,2},{2,4},{4,6},{1,3},{3,5},{5,7},{8,10},{10,12},{12,14},{9,11},... | collective-permute-start | bytes 36872 | tf_op jit(solution)/shard_map/ppermute | solution.py:21
  107.2 4.5 %collective-permute-start.21 = (f32[3,80,8]{2,1,0:T(8,128)S(1)}, f32[3,80,8]{2,1,0:T(8,128)S(1)}, u32[]{:S(2)}, u32[]{:S(2)}) collective-permute-start(f32[3,80,8]{2,1,0:T(8,128)S(1)} %get-tuple-element.115), channel_id=1, source_target_pairs={{1,0},{3,2},{5,4},{7,6},{9,8},{11,10},{13,12},{15,14},{17,16},{19,... | collective-permute-start | bytes 23048 | tf_op jit(solution)/shard_map/ppermute | solution.py:22
  108.5 4.0 %collective-permute-start.20 = (f32[3,80,8]{2,1,0:T(8,128)S(1)}, f32[3,80,8]{2,1,0:T(8,128)S(1)}, u32[]{:S(2)}, u32[]{:S(2)}) collective-permute-start(f32[3,80,8]{2,1,0:T(8,128)S(1)} %get-tuple-element.114), channel_id=1, source_target_pairs={{0,1},{2,3},{4,5},{6,7},{8,9},{10,11},{12,13},{14,15},{16,17},{18,... | collective-permute-start | bytes 23048 | tf_op jit(solution)/shard_map/ppermute | solution.py:21
  117.9 13.7 %collective-permute-start.23 = (f32[64,128]{1,0:T(8,128)S(1)}, f32[64,128]{1,0:T(8,128)S(1)}, u32[]{:S(2)}, u32[]{:S(2)}) collective-permute-start(f32[64,128]{1,0:T(8,128)S(1)} %get-tuple-element.129), channel_id=1, source_target_pairs={{8,0},{16,8},{24,16},{9,1},{17,9},{25,17},{10,2},{18,10},{26,18},{... | collective-permute-start | bytes 98312 | tf_op jit(solution)/shard_map/ppermute | solution.py:30
  131.7 7.2 %collective-permute-start.25 = (f32[2,4,128]{2,1,0:T(4,128)S(1)}, f32[2,4,128]{2,1,0:T(4,128)S(1)}, u32[]{:S(2)}, u32[]{:S(2)}) collective-permute-start(f32[2,4,128]{2,1,0:T(4,128)S(1)} %get-tuple-element.127), channel_id=1, source_target_pairs={{2,0},{4,2},{6,4},{3,1},{5,3},{7,5},{10,8},{12,10},{14,12},{11,9},... | collective-permute-start | bytes 12296 | tf_op jit(solution)/shard_map/ppermute | solution.py:22
  133.0 7.0 %collective-permute-start.24 = (f32[2,4,128]{2,1,0:T(4,128)S(1)}, f32[2,4,128]{2,1,0:T(4,128)S(1)}, u32[]{:S(2)}, u32[]{:S(2)}) collective-permute-start(f32[2,4,128]{2,1,0:T(4,128)S(1)} %get-tuple-element.126), channel_id=1, source_target_pairs={{0,2},{2,4},{4,6},{1,3},{3,5},{5,7},{8,10},{10,12},{12,14},{9,11},... | collective-permute-start | bytes 12296 | tf_op jit(solution)/shard_map/ppermute | solution.py:21
  140.1 4.5 %collective-permute-start.27 = (f32[2,72,4]{2,1,0:T(8,128)S(1)}, f32[2,72,4]{2,1,0:T(8,128)S(1)}, u32[]{:S(2)}, u32[]{:S(2)}) collective-permute-start(f32[2,72,4]{2,1,0:T(8,128)S(1)} %get-tuple-element.123), channel_id=1, source_target_pairs={{1,0},{3,2},{5,4},{7,6},{9,8},{11,10},{13,12},{15,14},{17,16},{19,... | collective-permute-start | bytes 6920 | tf_op jit(solution)/shard_map/ppermute | solution.py:22
  (10 other events, 55.7 us)
where the time goes:
time: 174 us; the launch traced here: 171 us
  starting transfers between devices  73.4 us (42%)
  blocking collectives  42.3 us (24%)
  other arithmetic  27.9 us (16%)
  local copies, waits for them, and re-layouts  15.7 us (9%)
  waiting for transfers between devices  10.2 us (6%)
  between operations  1.91 us (1%)
    ppermute x12, starting transfers between devices, with_halo(): before = lax.ppermute(last, axis, up)  50.5 us
    psum x2, blocking collectives, per_device(): total = lax.psum(bed_grad, 'tm')  42.3 us
    ppermute x12, starting transfers between devices, with_halo(): after = lax.ppermute(first, axis, down)  15.6 us
    gather x2, local copies, waits for them, and re-layouts, per_device(): predicted = final.reshape(-1)[cell_index]  12.3 us
    scatter-add x2, other arithmetic, per_device(): spread = jnp.zeros((slices_here * rows_here * cols_here,), jnp.float32).a...  11.9 us
    ppermute x12, waiting for transfers between devices, with_halo(): before = lax.ppermute(last, axis, up)  7.38 us
    ppermute x4, starting transfers between devices, from_behind(): return lax.ppermute(block, axis, route)  7.36 us
  transfers between devices with their start and end apart: 28, of which 10 were waited for; matrix products, arithmetic and copies ran while one was open for 17% of the time, Pallas kernels for 0%

commit v1 on v0

v1 whole, which is shorter than its diff:
```python
import functools

import jax
import jax.numpy as jnp
from jax import lax
from jax.experimental import pallas as pl
from jax.experimental.pallas import tpu as pltpu
from jax.sharding import PartitionSpec as P

STEPS = 4
OUTER = 2
HALO = 2 * STEPS * OUTER
LANES = 128

bed_rate = 0.1
state_rate = 0.5


def partner(index, shift, count):
    if count & (count - 1) == 0:
        return index ^ shift
    return (index + shift) % count


def source(index, shift, count):
    if count & (count - 1) == 0:
        return index ^ shift
    return (index + count - shift) % count


def exchange(value, axis, shift):
    count = lax.axis_size(axis)
    return lax.ppermute(value, axis, [(i, partner(i, shift, count)) for i in range(count)])


def neighbour_swaps(axis):
    count = lax.axis_size(axis)
    if count == 1:
        return []
    first = [(i, i ^ 1) for i in range(count)]
    if count == 2:
        return [first]
    second = []
    for i in range(1, count, 2):
        j = (i + 1) % count
        second += [(i, j), (j, i)]
    return [first, second]


def call(kernel, out_shape, operands, scratch=()):
    spec = pl.BlockSpec(memory_space=pltpu.VMEM)
    return pl.pallas_call(
        kernel,
        out_shape=out_shape,
        in_specs=[spec] * len(operands),
        out_specs=jax.tree.map(lambda _: spec, out_shape),
        scratch_shapes=list(scratch),
        name=kernel.func.__name__,
    )(*operands)


def lane_of(shape):
    return lax.broadcasted_iota(jnp.int32, shape, len(shape) - 1)


def maps_of(cells, values, rows, cols):
    row = cells // cols
    col = cells % cols
    n = cells.shape[-1]
    at_row = lax.broadcasted_iota(jnp.int32, (rows, n), 0) == row
    at_col = lax.broadcasted_iota(jnp.int32, (cols, n), 0) == col
    left = jnp.where(at_row, 1.0, 0.0).astype(jnp.bfloat16)
    part1 = values.astype(jnp.bfloat16).astype(jnp.float32)
    rest = values - part1
    part2 = rest.astype(jnp.bfloat16).astype(jnp.float32)
    part3 = rest - part2

    def gather(weight):
        right = jnp.where(at_col, weight, 0.0).astype(jnp.bfloat16)
        return lax.dot_general(left, right, (((1,), (1,)), ((), ())), preferred_element_type=jnp.float32)

    return gather(1.0), gather(part1) + (gather(part2) + gather(part3))


def pack_kernel(dims, *refs):
    slices, rows, cols, obs, group, sides, cut, width, lanes = dims
    states, bed, back, mask, rate, cells, values = refs[:7]
    near = refs[7 : 7 + sides]
    blocks = refs[7 + sides : 7 + sides + group]
    statics = refs[7 + sides + group]
    me = lax.axis_index("tm")
    y = lax.axis_index("gy")
    last_y = lax.axis_size("gy") - 1
    lane = lane_of((rows, LANES))
    wide = lane_of((rows, lanes))
    even = (y & 1) == 0

    def beyond(get):
        if sides == 0:
            return jnp.zeros((rows, cols), jnp.float32)
        if sides == 1:
            return get(near[0])
        one, two = get(near[0]), get(near[1])
        return jnp.where((lane < cols // 2) == even, one, two)

    def cut_out(inside, outside, start, offset):
        shift = (offset - start + 4 * LANES) % LANES
        column = lane - offset + start
        picked = jnp.where(
            (column >= 0) & (column < cols),
            pltpu.roll(inside, shift, 1),
            pltpu.roll(outside, shift, 1),
        )
        return picked

    def packed(parts, start):
        out = jnp.zeros((rows, lanes), jnp.float32)
        for s, (inside, outside) in enumerate(parts):
            offset = s * width
            base = offset // LANES * LANES
            piece = cut_out(inside, outside, start, offset - base)
            if lanes != LANES:
                piece = jnp.concatenate([piece] * (lanes // LANES), axis=1)
            out = jnp.where((wide >= offset) & (wide < offset + width), piece, out)
        return out

    kinds = [[], [], []]
    for s in range(slices):
        kinds[0].append((states[s], beyond(lambda r: r[s * rows : (s + 1) * rows])))
        own = maps_of(cells[s : s + 1], values[s : s + 1], rows, cols)
        top = (slices + 4) * rows
        out = []
        for r in near:
            listed = r[top + 2 * s * (obs // LANES) : top + 2 * (s + 1) * (obs // LANES)]
            listed = [
                jnp.concatenate([listed[i * (obs // LANES) + j : i * (obs // LANES) + j + 1] for j in range(obs // LANES)], axis=1)
                for i in (0, 1)
            ]
            out.append(maps_of(listed[0].astype(jnp.int32), listed[1], rows, cols))
        for i in (0, 1):
            if sides == 0:
                outside = jnp.zeros((rows, cols), jnp.float32)
            elif sides == 1:
                outside = out[0][i]
            else:
                outside = jnp.where((lane < cols // 2) == even, out[0][i], out[1][i])
            kinds[1 + i].append((own[i], outside))
    for k in range(group):
        start = partner(me, k, group) * cut - HALO
        for i in range(3):
            blocks[k][i] = packed(kinds[i], start)
    start = me * cut - HALO
    for i, ref in enumerate((bed, back, mask, rate)):
        inside = ref[...]
        outside = beyond(lambda r: r[(slices + i) * rows : (slices + i + 1) * rows])
        if i == 2:
            outside = jnp.where((lane < cols // 2) & (y == last_y), 0.0, outside)
            outside = jnp.where((lane >= cols // 2) & (y == 0), 0.0, outside)
            inside = inside.astype(jnp.float32)
        statics[i] = packed([(inside, outside)] * slices, start)


def edge_kernel(dims, *refs):
    group, rows = dims
    blocks, statics, sends = refs[:group], refs[group], refs[group + 1 :]
    even = (lax.axis_index("gx") & 1) == 0
    for i, send in enumerate(sends):
        lower = even if i == 0 else jnp.logical_not(even)
        start = pl.multiple_of(jnp.where(lower, rows - HALO, 0), 8)
        for k in range(group):
            send[3 * k : 3 * k + 3] = blocks[k][:, pl.ds(start, HALO), :]
        send[3 * group : 3 * group + 4] = statics[:, pl.ds(start, HALO), :]


def main_kernel(dims, *refs):
    slices, rows, group, sides, cut, width, lanes = dims
    blocks, statics = refs[:group], refs[group]
    edges = refs[group + 1 : group + 1 + sides]
    outs = refs[group + 1 + sides : 2 * group + 1 + sides]
    state, count, total, fixed, final, misfit, keep, acc, coef = refs[2 * group + 1 + sides :]
    me = lax.axis_index("tm")
    x = lax.axis_index("gx")
    last_x = lax.axis_size("gx") - 1
    even = (x & 1) == 0
    full = rows + 2 * HALO

    def put(target, main, pieces):
        target[HALO : HALO + rows] = main
        if sides < 2:
            target[0:HALO] = jnp.zeros((HALO, lanes), jnp.float32)
            target[HALO + rows : full] = jnp.zeros((HALO, lanes), jnp.float32)
        for i, piece in enumerate(pieces):
            after = even if i == 0 else jnp.logical_not(even)
            target[pl.ds(pl.multiple_of(jnp.where(after, HALO + rows, 0), 8), HALO)] = piece

    for k in range(group):
        pair = source(me, k, group)
        for i, target in enumerate((state, count, total)):
            put(target.at[pair], blocks[k][i], [e[3 * k + i] for e in edges])
    for i in range(4):
        put(fixed.at[i], statics[i], [e[3 * group + i] for e in edges])

    row = lax.broadcasted_iota(jnp.int32, (full, lanes), 0)
    lane = lane_of((full, lanes))
    outside = ((row < HALO) & (x == 0)) | ((row >= HALO + rows) & (x == last_x))
    mask = jnp.where(outside, 0.0, fixed[2])
    rate = fixed[3]
    down = lambda v: pltpu.roll(v, v.shape[0] - 1, 0)
    up = lambda v: pltpu.roll(v, 1, 0)
    right = lambda v: pltpu.roll(v, lanes - 1, 1)
    left = lambda v: pltpu.roll(v, 1, 1)
    face_x = 0.25 * (rate + down(rate)) * (mask * down(mask))
    face_y = 0.25 * (rate + right(rate)) * (mask * right(mask))
    seam = lane % width == width - 1
    if lanes != slices * width:
        seam = seam | (lane >= slices * width)
    coef[0] = face_x
    coef[1] = jnp.where(seam, 0.0, face_y)
    prior = fixed[0]

    for outer in range(OUTER):
        low = 2 * STEPS * outer
        high = full - low
        size = high - low
        span = pl.ds(low, size)
        bed = fixed[0, span]
        coef[0, span] = jnp.where(row[:size] == size - 1, 0.0, coef[0, span])
        coef[2, span] = down(bed) - bed
        coef[3, span] = right(bed) - bed

        def forward(p, _):
            thick = state[p, span]
            for step in range(STEPS):
                after = thick
                for d, (ahead, behind) in enumerate(((down, up), (right, left))):
                    there = ahead(thick)
                    both = thick + there
                    slope = (there - thick) + coef[2 + d, span]
                    scaled = coef[d, span] * both
                    half = 0.5 * both
                    by_mean = scaled * slope
                    keep[p, step, 2 * d, span] = half * scaled
                    keep[p, step, 2 * d + 1, span] = by_mean
                    flux = half * by_mean
                    after = after + (flux - behind(flux))
                thick = after
            final[p, span] = thick
            return 0

        lax.fori_loop(0, group, forward, 0)
        here = lane[:size]

        def differ(p, _):
            own = final[p, span]
            before = final[jnp.maximum(p - 1, 0), span]
            start = jnp.where(p == 0, fixed[1, span], pltpu.roll(before, (lanes - (slices - 1) * width) % lanes, 1))
            earlier = jnp.where(here < width, start, pltpu.roll(own, width, 1))
            misfit[p, span] = state[p, span] - earlier
            return 0

        lax.fori_loop(0, group, differ, 0)
        acc[...] = jnp.zeros_like(acc)

        def backward(p, _):
            own = misfit[p, span]
            after = misfit[jnp.minimum(p + 1, group - 1), span]
            after = jnp.where(p == group - 1, 0.0, pltpu.roll(after, (slices - 1) * width, 1))
            later = jnp.where(here < (slices - 1) * width, pltpu.roll(own, lanes - width, 1), after)
            pull = count[p, span] * final[p, span] - total[p, span] - later
            for step in reversed(range(STEPS)):
                new = pull
                for d, (ahead, behind) in enumerate(((down, up), (right, left))):
                    jump = pull - ahead(pull)
                    by_slope = keep[p, step, 2 * d, span] * jump
                    by_mean = keep[p, step, 2 * d + 1, span] * jump
                    acc[d, span] = acc[d, span] + by_slope
                    new = new + ((by_mean - by_slope) + behind(by_mean + by_slope))
                pull = new
            state[p, span] = state[p, span] - state_rate * (own + pull)
            return 0

        lax.fori_loop(0, group, backward, 0)
        by_x, by_y = acc[0, span], acc[1, span]
        each = (up(by_x) - by_x) + (left(by_y) - by_y)
        summed = each
        for s in range(1, slices):
            summed = summed + pltpu.roll(each, lanes - s * width, 1)
        grad = summed
        for s in range(1, slices):
            grad = jnp.where(here >= s * width, pltpu.roll(summed, s * width, 1), grad)
        fixed[0, span] = bed - bed_rate * (grad + (bed - prior[low:high]))

    inner = slice(HALO, HALO + rows)
    place = lane_of((rows, LANES))

    def one_tile(value, come, go):
        if lanes != LANES:
            base = come // LANES * LANES
            value = jnp.concatenate([value, value[:, :LANES]], axis=1)
            low = pltpu.roll(value[:, base : base + LANES], (go - come) % LANES, 1)
            high = pltpu.roll(value[:, base + LANES : base + 2 * LANES], (go - come) % LANES, 1)
            return jnp.where(place - go + come - base < LANES, low, high)
        return pltpu.roll(value, (go - come) % LANES, 1)

    ground = one_tile(fixed[0, inner], HALO, slices * cut)
    for k in range(group):
        mine = state[partner(me, k, group), inner]
        out = ground
        for s in range(slices):
            piece = one_tile(mine, s * width + HALO, s * cut)
            out = jnp.where((place >= s * cut) & (place < (s + 1) * cut), piece, out)
        outs[k][...] = out


def join_kernel(dims, *refs):
    slices, rows, group, cut = dims
    pieces, states, bed = refs[:group], refs[group], refs[group + 1]
    me = lax.axis_index("tm")
    lane = lane_of((rows, LANES))
    outs = [jnp.zeros((rows, LANES), jnp.float32)] * (slices + 1)
    for k in range(group):
        block = source(me, k, group)
        here = (lane >= block * cut) & (lane < (block + 1) * cut)
        value = pieces[k][...]
        for s in range(slices + 1):
            shift = (block * cut - s * cut + LANES) % LANES
            outs[s] = jnp.where(here, pltpu.roll(value, shift, 1), outs[s])
    for s in range(slices):
        states[s] = outs[s]
    bed[...] = outs[slices]


def per_device(states, bed, background_state, ice_mask, flow_rate, obs_cell, obs_value):
    slices, rows, cols = states.shape
    obs = obs_cell.shape[-1]
    group = lax.axis_size("tm")
    cut = cols // group
    width = cut + 2 * HALO
    lanes = -(-slices * width // LANES) * LANES
    full = rows + 2 * HALO
    f32 = lambda *shape: jax.ShapeDtypeStruct(shape, jnp.float32)
    vmem = lambda *shape: pltpu.VMEM(shape, jnp.float32)

    cells = obs_cell.reshape(slices, obs)
    values = obs_value.reshape(slices, obs)
    listed = jnp.stack([cells.astype(jnp.float32), values], axis=1)
    raw = jnp.concatenate(
        [
            states.reshape(slices * rows, cols),
            bed,
            background_state,
            ice_mask.astype(jnp.float32),
            flow_rate,
            listed.reshape(-1, LANES),
        ],
        axis=0,
    )
    near = [lax.ppermute(raw, "gy", pairs) for pairs in neighbour_swaps("gy")]
    dims = (slices, rows, cols, obs, group, len(near), cut, width, lanes)
    *blocks, statics = call(
        functools.partial(pack_kernel, dims),
        [f32(3, rows, lanes)] * group + [f32(4, rows, lanes)],
        [states, bed, background_state, ice_mask, flow_rate, cells, values, *near],
    )
    blocks = [blocks[0]] + [exchange(blocks[k], "tm", k) for k in range(1, group)]
    swaps = neighbour_swaps("gx")
    edges = []
    if swaps:
        sends = call(
            functools.partial(edge_kernel, (group, rows)),
            [f32(3 * group + 4, HALO, lanes)] * len(swaps),
            [*blocks, statics],
        )
        edges = [lax.ppermute(send, "gx", pairs) for send, pairs in zip(sends, swaps)]
    packed = call(
        functools.partial(main_kernel, (slices, rows, group, len(edges), cut, width, lanes)),
        [f32(rows, LANES)] * group,
        [*blocks, statics, *edges],
        [vmem(group, full, lanes)] * 3
        + [vmem(4, full, lanes)]
        + [vmem(group, full, lanes)] * 2
        + [vmem(group, STEPS, 4, full, lanes), vmem(2, full, lanes), vmem(4, full, lanes)],
    )
    pieces = [packed[0]] + [exchange(packed[k], "tm", k) for k in range(1, group)]
    return tuple(
        call(
            functools.partial(join_kernel, (slices, rows, group, cut)),
            [f32(slices, rows, cols), f32(rows, cols)],
            pieces,
        )
    )


def solution(mesh):
    placed = (
        P("tm", "gx", "gy"),
        P("gx", "gy"),
        P("gx", "gy"),
        P("gx", "gy"),
        P("gx", "gy"),
        P("tm", "gx", "gy", None),
        P("tm", "gx", "gy", None),
    )
    return jax.shard_map(
        per_device,
        mesh=mesh,
        in_specs=placed,
        out_specs=(P("tm", "gx", "gy"), P("gx", "gy")),
        check_vma=False,
    )
```

time: 174 us -> 59.5 us (0.34); the launches traced: 171 us -> 59 us
  starting transfers between devices: 73.4 us -> 13.7 us
  blocking collectives: 42.3 us -> 0 us
  other arithmetic: 27.9 us -> 0.71 us
  Pallas kernels: 0 us -> 19.5 us
  local copies, waits for them, and re-layouts: 15.7 us -> 7.06 us
  waiting for transfers between devices: 10.2 us -> 17.2 us
    ppermute x28 -> x9, starting transfers between devices: 73.4 us -> 13.7 us  [the longest x6 10.2 us: exchange(): lax.ppermute(value, axis, [(i, partner(i, shift, count)) for i in range(c...]
    psum x2 -> x0, blocking collectives: 42.3 us -> none  [per_device(): total = lax.psum(bed_grad, 'tm')]
    pallas_call x0 -> x4, Pallas kernels: none -> 19.5 us  [call(): pl.pallas_call(kernel, out_shape=out_shape, in_specs=[spec] * len(operand...]
    gather x2 -> x0, local copies, waits for them, and re-layouts: 12.3 us -> none  [per_device(): predicted = final.reshape(-1)[cell_index]]
    scatter-add x2 -> x0, other arithmetic: 11.9 us -> none  [per_device(): spread = jnp.zeros((slices_here * rows_here * cols_here,), jnp.float32).a...]
    ppermute x28 -> x9, waiting for transfers between devices: 10.2 us -> 17.2 us  [the longest x6 12.6 us: exchange(): lax.ppermute(value, axis, [(i, partner(i, shift, count)) for i in range(c...]
    unnamed x16 -> x36, local copies, waits for them, and re-layouts: 0.79 us -> 7.04 us
    neg x24 -> x0, other arithmetic: 5.54 us -> none  [the longest x8 2.07 us: advance(): flux_y[1:-1, 1:] - flux_y[1:-1, :-1]]
  transfers between devices with their start and end apart: 28 -> 9, of which waited for: 10 -> 6; matrix products, arithmetic and copies ran while one was open for 17% -> 2% of each run, Pallas kernels for 0% -> 0%
where the time goes in v1:
time: 59.5 us; the launch traced here: 59 us
  Pallas kernels  19.5 us (33%)
  waiting for transfers between devices  17.2 us (29%)
  starting transfers between devices  13.7 us (23%)
  local copies, waits for them, and re-layouts  7.06 us (12%)
  other arithmetic  0.71 us (1%)
  between operations  0.7 us (1%)
    pallas_call x4, Pallas kernels, call(): pl.pallas_call(kernel, out_shape=out_shape, in_specs=[spec] * len(operand...  19.5 us
    ppermute x6, waiting for transfers between devices, exchange(): lax.ppermute(value, axis, [(i, partner(i, shift, count)) for i in range(c...  12.6 us
    ppermute x6, starting transfers between devices, exchange(): lax.ppermute(value, axis, [(i, partner(i, shift, count)) for i in range(c...  10.2 us
    unnamed x36, local copies, waits for them, and re-layouts  7.04 us
    ppermute x2, waiting for transfers between devices, per_device(): lax.ppermute(send, 'gx', pairs)  4.58 us
    ppermute x2, starting transfers between devices, per_device(): lax.ppermute(send, 'gx', pairs)  2.98 us
  transfers between devices with their start and end apart: 9, of which 6 were waited for; matrix products, arithmetic and copies ran while one was open for 2% of the time, Pallas kernels for 0%

profile of v1, /device:TPU:0, one launch (start us, length us, event | category | flops | bytes accessed | tf_op | source)
XLA Modules:
  0.0 59.0 jit_solution(1866584192417155923)
XLA Ops:
  0.6 0.7 %fusion = f32[2,1,512]{2,1,0:T(1,128)S(1)} fusion(s32[2,1,1,512]{3,2,1,0:T(1,128)} %param.12), kind=kLoop, calls=%fused_computation.10 | loop fusion | flops 1024 | bytes 8192 | tf_op jit(solution)/shard_map/convert_element_type | solution.py:346
  1.4 0.9 %constant_dynamic-update-slice_fusion.4 = f32[400,128]{1,0:T(8,128)S(1)} fusion(f32[128,128]{1,0:T(8,128)} %bitcast.14), kind=kLoop, calls=%fused_computation.5 | loop fusion | bytes 131072
  2.3 0.7 %copy-done.5 = f32[64,128]{1,0:T(8,128)S(1)} copy-done((f32[64,128]{1,0:T(8,128)S(1)}, f32[64,128]{1,0:T(8,128)}, u32[]{:S(2)}) %copy-start.5) | copy-done | bytes 32792
  3.0 0.8 %copy-done.6 = s32[64,128]{1,0:T(8,128)S(1)} copy-done((s32[64,128]{1,0:T(8,128)S(1)}, s32[64,128]{1,0:T(8,128)}, u32[]{:S(2)}) %copy-start.6) | copy-done | bytes 32792
  3.8 0.8 %copy-done.7 = f32[64,128]{1,0:T(8,128)S(1)} copy-done((f32[64,128]{1,0:T(8,128)S(1)}, f32[64,128]{1,0:T(8,128)}, u32[]{:S(2)}) %copy-start.7) | copy-done | bytes 32792
  6.4 0.7 %copy-done.3 = f32[400,128]{1,0:T(8,128)} copy-done((f32[400,128]{1,0:T(8,128)}, f32[400,128]{1,0:T(8,128)S(1)}, u32[]{:S(2)}) %copy-start.3) | copy-done | bytes 204824
  7.1 2.9 %pack_kernel.1 = (f32[3,64,128]{2,1,0:T(8,128)}, f32[3,64,128]{2,1,0:T(8,128)}, f32[3,64,128]{2,1,0:T(8,128)}, f32[3,64,128]{2,1,0:T(8,128)}, f32[4,64,128]{2,1,0:T(8,128)}) custom-call(f32[2,64,128]{2,1,0:T(8,128)} %refs_0_.1, f32[64,128]{1,0:T(8,128)} %refs_1_.1, f32[64,128]{1,0:T(8,128)} %refs_2_.1, s32[64,128]{1,0:T(8,128)} %refs_3_.1, ...), custom_call_target="tpu_custom_call" | custom-call | tf_op jit(solution)/shard_map/pack_kernel/pallas_call | solution.py:52
  9.9 3.1 %collective-permute-start.1 = (f32[3,64,128]{2,1,0:T(8,128)}, f32[3,64,128]{2,1,0:T(8,128)S(1)}, u32[]{:S(2)}, u32[]{:S(2)}) collective-permute-start(f32[3,64,128]{2,1,0:T(8,128)} %get-tuple-element.14), channel_id=1, source_target_pairs={{0,8},{8,0},{16,24},{24,16},{1,9},{9,1},{17,25},{25,17},{2,10},{10... | collective-permute-start | bytes 294920 | tf_op jit(solution)/shard_map/ppermute | solution.py:33
  13.0 2.6 %collective-permute-start.2 = (f32[3,64,128]{2,1,0:T(8,128)}, f32[3,64,128]{2,1,0:T(8,128)S(1)}, u32[]{:S(2)}, u32[]{:S(2)}) collective-permute-start(f32[3,64,128]{2,1,0:T(8,128)} %get-tuple-element.15), channel_id=1, source_target_pairs={{0,16},{8,24},{16,0},{24,8},{1,17},{9,25},{17,1},{25,9},{2,18},{10... | collective-permute-start | bytes 294920 | tf_op jit(solution)/shard_map/ppermute | solution.py:33
  16.1 7.7 %collective-permute-done.2.refs_2_ = f32[3,64,128]{2,1,0:T(8,128)S(1)} collective-permute-done((f32[3,64,128]{2,1,0:T(8,128)}, f32[3,64,128]{2,1,0:T(8,128)S(1)}, u32[]{:S(2)}, u32[]{:S(2)}) %collective-permute-start.2) | collective-permute-done | bytes 98336 | tf_op jit(solution)/shard_map/ppermute | solution.py:33
  23.7 0.6 %copy-done.1 = f32[3,64,128]{2,1,0:T(8,128)} copy-done((f32[3,64,128]{2,1,0:T(8,128)}, f32[3,64,128]{2,1,0:T(8,128)S(1)}, u32[]{:S(2)}) %copy-start.1) | copy-done | bytes 98328
  24.4 1.8 %edge_kernel.1 = (f32[16,16,128]{2,1,0:T(8,128)}, f32[16,16,128]{2,1,0:T(8,128)}) custom-call(f32[3,64,128]{2,1,0:T(8,128)} %get-tuple-element.13.refs_0_, f32[3,64,128]{2,1,0:T(8,128)} %copy-done, f32[3,64,128]{2,1,0:T(8,128)} %copy-done.1, f32[3,64,128]{2,1,0:T(8,128)} %copy-done.2, f32[4,64,128]{2,1,0:T(8,128)} %get-tuple-element.17.refs_4_), custom_call_target="tpu_custom_call" | custom-call | tf_op jit(solution)/shard_map/edge_kernel/pallas_call | solution.py:52
  26.2 1.5 %collective-permute-start.4 = (f32[16,16,128]{2,1,0:T(8,128)}, f32[16,16,128]{2,1,0:T(8,128)S(1)}, u32[]{:S(2)}, u32[]{:S(2)}) collective-permute-start(f32[16,16,128]{2,1,0:T(8,128)} %get-tuple-element.18), channel_id=1, source_target_pairs={{0,2},{2,0},{4,6},{6,4},{1,3},{3,1},{5,7},{7,5},{8,10},{10,8},{12,... | collective-permute-start | bytes 393224 | tf_op jit(solution)/shard_map/ppermute | solution.py:374
  27.7 1.5 %collective-permute-start.5 = (f32[16,16,128]{2,1,0:T(8,128)}, f32[16,16,128]{2,1,0:T(8,128)S(1)}, u32[]{:S(2)}, u32[]{:S(2)}) collective-permute-start(f32[16,16,128]{2,1,0:T(8,128)} %get-tuple-element.19), channel_id=1, source_target_pairs={{2,4},{4,2},{6,0},{0,6},{3,5},{5,3},{7,1},{1,7},{10,12},{12,10},{1... | collective-permute-start | bytes 393224 | tf_op jit(solution)/shard_map/ppermute | solution.py:374
  29.2 2.8 %collective-permute-done.4.refs_5_ = f32[16,16,128]{2,1,0:T(8,128)S(1)} collective-permute-done((f32[16,16,128]{2,1,0:T(8,128)}, f32[16,16,128]{2,1,0:T(8,128)S(1)}, u32[]{:S(2)}, u32[]{:S(2)}) %collective-permute-start.4) | collective-permute-done | bytes 131104 | tf_op jit(solution)/shard_map/ppermute | solution.py:374
  32.0 1.8 %collective-permute-done.5.refs_6_ = f32[16,16,128]{2,1,0:T(8,128)S(1)} collective-permute-done((f32[16,16,128]{2,1,0:T(8,128)}, f32[16,16,128]{2,1,0:T(8,128)S(1)}, u32[]{:S(2)}, u32[]{:S(2)}) %collective-permute-start.5) | collective-permute-done | bytes 131104 | tf_op jit(solution)/shard_map/ppermute | solution.py:374
  33.8 0.7 %copy-done.9 = f32[16,16,128]{2,1,0:T(8,128)} copy-done((f32[16,16,128]{2,1,0:T(8,128)}, f32[16,16,128]{2,1,0:T(8,128)S(1)}, u32[]{:S(2)}) %copy-start.9) | copy-done | bytes 131096
  34.4 13.2 %main_kernel.1 = (f32[64,128]{1,0:T(8,128)}, f32[64,128]{1,0:T(8,128)}, f32[64,128]{1,0:T(8,128)}, f32[64,128]{1,0:T(8,128)}) custom-call(f32[3,64,128]{2,1,0:T(8,128)} %get-tuple-element.13.refs_0_, f32[3,64,128]{2,1,0:T(8,128)} %copy-done, f32[3,64,128]{2,1,0:T(8,128)} %copy-done.1, f32[3,64,128]{2,1,0:T(8,128)} %copy-done.2, ...), custom_call_target="tpu_custom_call" | custom-call | tf_op jit(solution)/shard_map/main_kernel/pallas_call | solution.py:52
  47.7 2.1 %collective-permute-start.6 = (f32[64,128]{1,0:T(8,128)}, f32[64,128]{1,0:T(8,128)S(1)}, u32[]{:S(2)}, u32[]{:S(2)}) collective-permute-start(f32[64,128]{1,0:T(8,128)} %get-tuple-element.21), channel_id=1, source_target_pairs={{0,8},{8,0},{16,24},{24,16},{1,9},{9,1},{17,25},{25,17},{2,10},{10... | collective-permute-start | bytes 98312 | tf_op jit(solution)/shard_map/ppermute | solution.py:33
  49.8 1.0 %collective-permute-start.7 = (f32[64,128]{1,0:T(8,128)}, f32[64,128]{1,0:T(8,128)S(1)}, u32[]{:S(2)}, u32[]{:S(2)}) collective-permute-start(f32[64,128]{1,0:T(8,128)} %get-tuple-element.22), channel_id=1, source_target_pairs={{0,16},{8,24},{16,0},{24,8},{1,17},{9,25},{17,1},{25,9},{2,18},{10... | collective-permute-start | bytes 98312 | tf_op jit(solution)/shard_map/ppermute | solution.py:33
  50.8 1.4 %collective-permute-start.8 = (f32[64,128]{1,0:T(8,128)}, f32[64,128]{1,0:T(8,128)S(1)}, u32[]{:S(2)}, u32[]{:S(2)}) collective-permute-start(f32[64,128]{1,0:T(8,128)} %get-tuple-element.23), channel_id=1, source_target_pairs={{0,24},{8,16},{16,8},{24,0},{1,25},{9,17},{17,9},{25,1},{2,26},{10... | collective-permute-start | bytes 98312 | tf_op jit(solution)/shard_map/ppermute | solution.py:33
  52.2 2.8 %collective-permute-done.7.refs_2_ = f32[64,128]{1,0:T(8,128)S(1)} collective-permute-done((f32[64,128]{1,0:T(8,128)}, f32[64,128]{1,0:T(8,128)S(1)}, u32[]{:S(2)}, u32[]{:S(2)}) %collective-permute-start.7) | collective-permute-done | bytes 32800 | tf_op jit(solution)/shard_map/ppermute | solution.py:33
  55.0 1.7 %collective-permute-done.8.refs_3_ = f32[64,128]{1,0:T(8,128)S(1)} collective-permute-done((f32[64,128]{1,0:T(8,128)}, f32[64,128]{1,0:T(8,128)S(1)}, u32[]{:S(2)}, u32[]{:S(2)}) %collective-permute-start.8) | collective-permute-done | bytes 32800 | tf_op jit(solution)/shard_map/ppermute | solution.py:33
  57.3 1.6 %join_kernel.1 = (f32[2,64,128]{2,1,0:T(8,128)}, f32[64,128]{1,0:T(8,128)}) custom-call(f32[64,128]{1,0:T(8,128)} %get-tuple-element.20.refs_0_, f32[64,128]{1,0:T(8,128)} %copy-done.10, f32[64,128]{1,0:T(8,128)} %copy-done.11, f32[64,128]{1,0:T(8,128)} %copy-done.12), custom_call_target="tpu_custom_call" | custom-call | tf_op jit(solution)/shard_map/join_kernel/pallas_call | solution.py:52
  (39 shorter events, 3.1 us)
Async XLA Ops:
  0.6 0.7 %copy-start.14 = (f32[2,1,1,512]{3,2,1,0:T(1,128)S(1)}, f32[2,1,1,512]{3,2,1,0:T(1,128)}, u32[]{:S(2)}) copy-start(f32[2,1,1,512]{3,2,1,0:T(1,128)} %param.13) | copy-start | bytes 12292
  1.4 0.9 %copy-start.4 = (f32[64,128]{1,0:T(8,128)S(1)}, f32[64,128]{1,0:T(8,128)}, u32[]{:S(2)}) copy-start(f32[64,128]{1,0:T(8,128)} %refs_1_.1) | copy-start | bytes 98308
  2.2 0.8 %copy-start.5 = (f32[64,128]{1,0:T(8,128)S(1)}, f32[64,128]{1,0:T(8,128)}, u32[]{:S(2)}) copy-start(f32[64,128]{1,0:T(8,128)} %refs_2_.1) | copy-start | bytes 98308
  3.0 0.8 %copy-start.6 = (s32[64,128]{1,0:T(8,128)S(1)}, s32[64,128]{1,0:T(8,128)}, u32[]{:S(2)}) copy-start(s32[64,128]{1,0:T(8,128)} %refs_3_.1) | copy-start | bytes 98308
  3.8 0.8 %copy-start.7 = (f32[64,128]{1,0:T(8,128)S(1)}, f32[64,128]{1,0:T(8,128)}, u32[]{:S(2)}) copy-start(f32[64,128]{1,0:T(8,128)} %refs_4_.1) | copy-start | bytes 98308
  4.5 0.7 %copy-start.13 = (s32[2,1,1,512]{3,2,1,0:T(1,128)S(1)}, s32[2,1,1,512]{3,2,1,0:T(1,128)}, u32[]{:S(2)}) copy-start(s32[2,1,1,512]{3,2,1,0:T(1,128)} %param.12) | copy-start | bytes 12292
  4.5 1.9 %collective-permute-start = (f32[400,128]{1,0:T(8,128)S(1)}, f32[400,128]{1,0:T(8,128)S(1)}, u32[]{:S(2)}, u32[]{:S(2)}) collective-permute-start(f32[400,128]{1,0:T(8,128)S(1)} %constant_dynamic-update-slice_fusion), channel_id=1, source_target_pairs={{0,1},{1,0},{2,3},{3,2},{4,5},{5,4},{6,7},{7,6},{8,9},{9,8},{10,11... | collective-permute-start | bytes 614408 | tf_op jit(solution)/shard_map/ppermute | solution.py:358
  6.4 0.7 %copy-start.3 = (f32[400,128]{1,0:T(8,128)}, f32[400,128]{1,0:T(8,128)S(1)}, u32[]{:S(2)}) copy-start(f32[400,128]{1,0:T(8,128)S(1)} %collective-permute-done.refs_7_) | copy-start | bytes 614404
  9.9 6.1 %collective-permute-start.1 = (f32[3,64,128]{2,1,0:T(8,128)}, f32[3,64,128]{2,1,0:T(8,128)S(1)}, u32[]{:S(2)}, u32[]{:S(2)}) collective-permute-start(f32[3,64,128]{2,1,0:T(8,128)} %get-tuple-element.14), channel_id=1, source_target_pairs={{0,8},{8,0},{16,24},{24,16},{1,9},{9,1},{17,25},{25,17},{2,10},{10... | collective-permute-start | bytes 294920 | tf_op jit(solution)/shard_map/ppermute | solution.py:33
  13.0 10.7 %collective-permute-start.2 = (f32[3,64,128]{2,1,0:T(8,128)}, f32[3,64,128]{2,1,0:T(8,128)S(1)}, u32[]{:S(2)}, u32[]{:S(2)}) collective-permute-start(f32[3,64,128]{2,1,0:T(8,128)} %get-tuple-element.15), channel_id=1, source_target_pairs={{0,16},{8,24},{16,0},{24,8},{1,17},{9,25},{17,1},{25,9},{2,18},{10... | collective-permute-start | bytes 294920 | tf_op jit(solution)/shard_map/ppermute | solution.py:33
  15.6 8.1 %collective-permute-start.3 = (f32[3,64,128]{2,1,0:T(8,128)}, f32[3,64,128]{2,1,0:T(8,128)S(1)}, u32[]{:S(2)}, u32[]{:S(2)}) collective-permute-start(f32[3,64,128]{2,1,0:T(8,128)} %get-tuple-element.16), channel_id=1, source_target_pairs={{0,24},{8,16},{16,8},{24,0},{1,25},{9,17},{17,9},{25,1},{2,26},{10... | collective-permute-start | bytes 294920 | tf_op jit(solution)/shard_map/ppermute | solution.py:33
  16.1 7.7 %copy-start = (f32[3,64,128]{2,1,0:T(8,128)}, f32[3,64,128]{2,1,0:T(8,128)S(1)}, u32[]{:S(2)}) copy-start(f32[3,64,128]{2,1,0:T(8,128)S(1)} %collective-permute-done.1.refs_1_) | copy-start | bytes 294916
  23.7 0.6 %copy-start.1 = (f32[3,64,128]{2,1,0:T(8,128)}, f32[3,64,128]{2,1,0:T(8,128)S(1)}, u32[]{:S(2)}) copy-start(f32[3,64,128]{2,1,0:T(8,128)S(1)} %collective-permute-done.2.refs_2_) | copy-start | bytes 294916
  23.7 0.7 %copy-start.2 = (f32[3,64,128]{2,1,0:T(8,128)}, f32[3,64,128]{2,1,0:T(8,128)S(1)}, u32[]{:S(2)}) copy-start(f32[3,64,128]{2,1,0:T(8,128)S(1)} %collective-permute-done.3.refs_3_) | copy-start | bytes 294916
  26.2 5.8 %collective-permute-start.4 = (f32[16,16,128]{2,1,0:T(8,128)}, f32[16,16,128]{2,1,0:T(8,128)S(1)}, u32[]{:S(2)}, u32[]{:S(2)}) collective-permute-start(f32[16,16,128]{2,1,0:T(8,128)} %get-tuple-element.18), channel_id=1, source_target_pairs={{0,2},{2,0},{4,6},{6,4},{1,3},{3,1},{5,7},{7,5},{8,10},{10,8},{12,... | collective-permute-start | bytes 393224 | tf_op jit(solution)/shard_map/ppermute | solution.py:374
  27.7 6.1 %collective-permute-start.5 = (f32[16,16,128]{2,1,0:T(8,128)}, f32[16,16,128]{2,1,0:T(8,128)S(1)}, u32[]{:S(2)}, u32[]{:S(2)}) collective-permute-start(f32[16,16,128]{2,1,0:T(8,128)} %get-tuple-element.19), channel_id=1, source_target_pairs={{2,4},{4,2},{6,0},{0,6},{3,5},{5,3},{7,1},{1,7},{10,12},{12,10},{1... | collective-permute-start | bytes 393224 | tf_op jit(solution)/shard_map/ppermute | solution.py:374
  32.0 1.8 %copy-start.8 = (f32[16,16,128]{2,1,0:T(8,128)}, f32[16,16,128]{2,1,0:T(8,128)S(1)}, u32[]{:S(2)}) copy-start(f32[16,16,128]{2,1,0:T(8,128)S(1)} %collective-permute-done.4.refs_5_) | copy-start | bytes 393220
  33.8 0.7 %copy-start.9 = (f32[16,16,128]{2,1,0:T(8,128)}, f32[16,16,128]{2,1,0:T(8,128)S(1)}, u32[]{:S(2)}) copy-start(f32[16,16,128]{2,1,0:T(8,128)S(1)} %collective-permute-done.5.refs_6_) | copy-start | bytes 393220
  47.7 4.5 %collective-permute-start.6 = (f32[64,128]{1,0:T(8,128)}, f32[64,128]{1,0:T(8,128)S(1)}, u32[]{:S(2)}, u32[]{:S(2)}) collective-permute-start(f32[64,128]{1,0:T(8,128)} %get-tuple-element.21), channel_id=1, source_target_pairs={{0,8},{8,0},{16,24},{24,16},{1,9},{9,1},{17,25},{25,17},{2,10},{10... | collective-permute-start | bytes 98312 | tf_op jit(solution)/shard_map/ppermute | solution.py:33
  49.8 5.2 %collective-permute-start.7 = (f32[64,128]{1,0:T(8,128)}, f32[64,128]{1,0:T(8,128)S(1)}, u32[]{:S(2)}, u32[]{:S(2)}) collective-permute-start(f32[64,128]{1,0:T(8,128)} %get-tuple-element.22), channel_id=1, source_target_pairs={{0,16},{8,24},{16,0},{24,8},{1,17},{9,25},{17,1},{25,9},{2,18},{10... | collective-permute-start | bytes 98312 | tf_op jit(solution)/shard_map/ppermute | solution.py:33
  50.8 5.9 %collective-permute-start.8 = (f32[64,128]{1,0:T(8,128)}, f32[64,128]{1,0:T(8,128)S(1)}, u32[]{:S(2)}, u32[]{:S(2)}) collective-permute-start(f32[64,128]{1,0:T(8,128)} %get-tuple-element.23), channel_id=1, source_target_pairs={{0,24},{8,16},{16,8},{24,0},{1,25},{9,17},{17,9},{25,1},{2,26},{10... | collective-permute-start | bytes 98312 | tf_op jit(solution)/shard_map/ppermute | solution.py:33
  52.2 4.5 %copy-start.10 = (f32[64,128]{1,0:T(8,128)}, f32[64,128]{1,0:T(8,128)S(1)}, u32[]{:S(2)}) copy-start(f32[64,128]{1,0:T(8,128)S(1)} %collective-permute-done.6.refs_1_) | copy-start | bytes 98308
  55.0 1.7 %copy-start.11 = (f32[64,128]{1,0:T(8,128)}, f32[64,128]{1,0:T(8,128)S(1)}, u32[]{:S(2)}) copy-start(f32[64,128]{1,0:T(8,128)S(1)} %collective-permute-done.7.refs_2_) | copy-start | bytes 98308
  56.7 0.6 %copy-start.12 = (f32[64,128]{1,0:T(8,128)}, f32[64,128]{1,0:T(8,128)S(1)}, u32[]{:S(2)}) copy-start(f32[64,128]{1,0:T(8,128)S(1)} %collective-permute-done.8.refs_3_) | copy-start | bytes 98308

commit v2 on v1

--- a/solution.py
+++ b/solution.py
@@ -56,6 +56,7 @@
         out_specs=jax.tree.map(lambda _: spec, out_shape),
         scratch_shapes=list(scratch),
         name=kernel.func.__name__,
+        compiler_params=pltpu.CompilerParams(vmem_limit_bytes=16 << 20),
     )(*operands)
 
 

time: 59.5 us -> 50.1 us (0.84)
  Pallas kernels: 19.5 us -> 13.2 us
  local copies, waits for them, and re-layouts: 7.06 us -> 3.29 us
  starting transfers between devices: 13.7 us -> 14.4 us
    pallas_call x4, Pallas kernels: 19.5 us -> 13.2 us  [call(): pl.pallas_call(kernel, out_shape=out_shape, in_specs=[spec] * len(operand...]
    unnamed x36 -> x20, local copies, waits for them, and re-layouts: 7.04 us -> 3.28 us
    ppermute x1, waiting for transfers between devices: 0.01 us -> 0.93 us  [per_device(): near = [lax.ppermute(raw, 'gy', pairs) for pairs in neighbour_swaps('gy')]]
  transfers between devices with their start and end apart: 9 -> 9, of which waited for: 6 -> 7; matrix products, arithmetic and copies ran while one was open for 2% -> 0% of each run, Pallas kernels for 0% -> 0%
where the time goes in v2:
time: 50.1 us; the launch traced here: 49.6 us
  waiting for transfers between devices  17.4 us (35%)
  starting transfers between devices  14.4 us (29%)
  Pallas kernels  13.2 us (26%)
  local copies, waits for them, and re-layouts  3.29 us (7%)
  other arithmetic  0.71 us (1%)
  between operations  0.71 us (1%)
    pallas_call x4, Pallas kernels, call(): pl.pallas_call(kernel, out_shape=out_shape, in_specs=[spec] * len(operand...  13.2 us
    ppermute x6, waiting for transfers between devices, exchange(): lax.ppermute(value, axis, [(i, partner(i, shift, count)) for i in range(c...  12.1 us
    ppermute x6, starting transfers between devices, exchange(): lax.ppermute(value, axis, [(i, partner(i, shift, count)) for i in range(c...  10.8 us
    ppermute x2, waiting for transfers between devices, per_device(): lax.ppermute(send, 'gx', pairs)  4.37 us
    unnamed x20, local copies, waits for them, and re-layouts  3.28 us
    ppermute x2, starting transfers between devices, per_device(): lax.ppermute(send, 'gx', pairs)  3.05 us
  transfers between devices with their start and end apart: 9, of which 7 were waited for; matrix products, arithmetic and copies ran while one was open for 0% of the time, Pallas kernels for 0%

profile of v2, /device:TPU:0, one launch (start us, length us, event | category | flops | bytes accessed | tf_op | source)
XLA Modules:
  0.0 49.6 jit_solution(622854508510330157)
XLA Ops:
  0.6 0.7 %fusion = f32[2,1,512]{2,1,0:T(1,128)S(1)} fusion(s32[2,1,1,512]{3,2,1,0:T(1,128)} %param.12), kind=kLoop, calls=%fused_computation.10 | loop fusion | flops 1024 | bytes 8192 | tf_op jit(solution)/shard_map/convert_element_type | solution.py:347
  1.4 0.9 %constant_dynamic-update-slice_fusion.4 = f32[400,128]{1,0:T(8,128)S(1)} fusion(f32[128,128]{1,0:T(8,128)} %bitcast.14), kind=kLoop, calls=%fused_computation.5 | loop fusion | bytes 131072
  2.3 0.7 %copy-done.2 = f32[64,128]{1,0:T(8,128)S(1)} copy-done((f32[64,128]{1,0:T(8,128)S(1)}, f32[64,128]{1,0:T(8,128)}, u32[]{:S(2)}) %copy-start.2) | copy-done | bytes 32792
  3.0 0.8 %copy-done.3 = s32[64,128]{1,0:T(8,128)S(1)} copy-done((s32[64,128]{1,0:T(8,128)S(1)}, s32[64,128]{1,0:T(8,128)}, u32[]{:S(2)}) %copy-start.3) | copy-done | bytes 32792
  3.8 0.8 %copy-done.4 = f32[64,128]{1,0:T(8,128)S(1)} copy-done((f32[64,128]{1,0:T(8,128)S(1)}, f32[64,128]{1,0:T(8,128)}, u32[]{:S(2)}) %copy-start.4) | copy-done | bytes 32792
  4.5 0.6 %collective-permute-start = (f32[400,128]{1,0:T(8,128)S(1)}, f32[400,128]{1,0:T(8,128)S(1)}, u32[]{:S(2)}, u32[]{:S(2)}) collective-permute-start(f32[400,128]{1,0:T(8,128)S(1)} %constant_dynamic-update-slice_fusion), channel_id=1, source_target_pairs={{0,1},{1,0},{2,3},{3,2},{4,5},{5,4},{6,7},{7,6},{8,9},{9,8},{10,11... | collective-permute-start | bytes 614408 | tf_op jit(solution)/shard_map/ppermute | solution.py:359
  5.1 0.1 copy-done.5
  5.2 0.9 %collective-permute-done.refs_7_ = f32[400,128]{1,0:T(8,128)S(1)} collective-permute-done((f32[400,128]{1,0:T(8,128)S(1)}, f32[400,128]{1,0:T(8,128)S(1)}, u32[]{:S(2)}, u32[]{:S(2)}) %collective-permute-start) | collective-permute-done | bytes 204832 | tf_op jit(solution)/shard_map/ppermute | solution.py:359
  6.2 1.0 %pack_kernel.1 = (f32[3,64,128]{2,1,0:T(8,128)S(1)}, f32[3,64,128]{2,1,0:T(8,128)S(1)}, f32[3,64,128]{2,1,0:T(8,128)S(1)}, f32[3,64,128]{2,1,0:T(8,128)S(1)}, f32[4,64,128]{2,1,0:T(8,128)S(1)}) custom-call(f32[2,64,128]{2,1,0:T(8,128)S(1)} %copy-done, f32[64,128]{1,0:T(8,128)S(1)} %copy-done.1, f32[64,128]{1,0:T(8,128)S(1)} %copy-done.2, ...), custom_call_target="tpu_custom_call" | custom-call | tf_op jit(solution)/shard_map/pack_kernel/pallas_call | solution.py:52
  7.2 3.0 %collective-permute-start.1 = (f32[3,64,128]{2,1,0:T(8,128)S(1)}, f32[3,64,128]{2,1,0:T(8,128)S(1)}, u32[]{:S(2)}, u32[]{:S(2)}) collective-permute-start(f32[3,64,128]{2,1,0:T(8,128)S(1)} %get-tuple-element.14), channel_id=1, source_target_pairs={{0,8},{8,0},{16,24},{24,16},{1,9},{9,1},{17,25},{25,17},{2,10},{10... | collective-permute-start | bytes 294920 | tf_op jit(solution)/shard_map/ppermute | solution.py:33
  10.2 2.6 %collective-permute-start.2 = (f32[3,64,128]{2,1,0:T(8,128)S(1)}, f32[3,64,128]{2,1,0:T(8,128)S(1)}, u32[]{:S(2)}, u32[]{:S(2)}) collective-permute-start(f32[3,64,128]{2,1,0:T(8,128)S(1)} %get-tuple-element.15), channel_id=1, source_target_pairs={{0,16},{8,24},{16,0},{24,8},{1,17},{9,25},{17,1},{25,9},{2,18},{10... | collective-permute-start | bytes 294920 | tf_op jit(solution)/shard_map/ppermute | solution.py:33
  12.8 0.5 %collective-permute-done.1.refs_1_ = f32[3,64,128]{2,1,0:T(8,128)S(1)} collective-permute-done((f32[3,64,128]{2,1,0:T(8,128)S(1)}, f32[3,64,128]{2,1,0:T(8,128)S(1)}, u32[]{:S(2)}, u32[]{:S(2)}) %collective-permute-start.1) | collective-permute-done | bytes 98336 | tf_op jit(solution)/shard_map/ppermute | solution.py:33
  13.3 7.6 %collective-permute-done.2.refs_2_ = f32[3,64,128]{2,1,0:T(8,128)S(1)} collective-permute-done((f32[3,64,128]{2,1,0:T(8,128)S(1)}, f32[3,64,128]{2,1,0:T(8,128)S(1)}, u32[]{:S(2)}, u32[]{:S(2)}) %collective-permute-start.2) | collective-permute-done | bytes 98336 | tf_op jit(solution)/shard_map/ppermute | solution.py:33
  20.9 1.6 %collective-permute-start.4 = (f32[16,16,128]{2,1,0:T(8,128)S(1)}, f32[16,16,128]{2,1,0:T(8,128)S(1)}, u32[]{:S(2)}, u32[]{:S(2)}) collective-permute-start(f32[16,16,128]{2,1,0:T(8,128)S(1)} %get-tuple-element.18), channel_id=1, source_target_pairs={{0,2},{2,0},{4,6},{6,4},{1,3},{3,1},{5,7},{7,5},{8,10},{10,8},{12,... | collective-permute-start | bytes 393224 | tf_op jit(solution)/shard_map/ppermute | solution.py:375
  22.4 1.5 %collective-permute-start.5 = (f32[16,16,128]{2,1,0:T(8,128)S(1)}, f32[16,16,128]{2,1,0:T(8,128)S(1)}, u32[]{:S(2)}, u32[]{:S(2)}) collective-permute-start(f32[16,16,128]{2,1,0:T(8,128)S(1)} %get-tuple-element.19), channel_id=1, source_target_pairs={{2,4},{4,2},{6,0},{0,6},{3,5},{5,3},{7,1},{1,7},{10,12},{12,10},{1... | collective-permute-start | bytes 393224 | tf_op jit(solution)/shard_map/ppermute | solution.py:375
  23.9 2.7 %collective-permute-done.4.refs_5_ = f32[16,16,128]{2,1,0:T(8,128)S(1)} collective-permute-done((f32[16,16,128]{2,1,0:T(8,128)S(1)}, f32[16,16,128]{2,1,0:T(8,128)S(1)}, u32[]{:S(2)}, u32[]{:S(2)}) %collective-permute-start.4) | collective-permute-done | bytes 131104 | tf_op jit(solution)/shard_map/ppermute | solution.py:375
  26.6 1.7 %collective-permute-done.5.refs_6_ = f32[16,16,128]{2,1,0:T(8,128)S(1)} collective-permute-done((f32[16,16,128]{2,1,0:T(8,128)S(1)}, f32[16,16,128]{2,1,0:T(8,128)S(1)}, u32[]{:S(2)}, u32[]{:S(2)}) %collective-permute-start.5) | collective-permute-done | bytes 131104 | tf_op jit(solution)/shard_map/ppermute | solution.py:375
  28.3 11.4 %main_kernel.1 = (f32[64,128]{1,0:T(8,128)S(1)}, f32[64,128]{1,0:T(8,128)S(1)}, f32[64,128]{1,0:T(8,128)S(1)}, f32[64,128]{1,0:T(8,128)S(1)}) custom-call(f32[3,64,128]{2,1,0:T(8,128)S(1)} %get-tuple-element.13.refs_0_, f32[3,64,128]{2,1,0:T(8,128)S(1)} %collective-permute-done.1.refs_1_, f32[3,64,128]{2,1,0:T(8,128)S(1)} %collective-permute-done.2.refs_2_, ...), custom_call_target="tpu_custom_call" | custom-call | tf_op jit(solution)/shard_map/main_kernel/pallas_call | solution.py:52
  39.7 2.7 %collective-permute-start.6 = (f32[64,128]{1,0:T(8,128)S(1)}, f32[64,128]{1,0:T(8,128)S(1)}, u32[]{:S(2)}, u32[]{:S(2)}) collective-permute-start(f32[64,128]{1,0:T(8,128)S(1)} %get-tuple-element.21), channel_id=1, source_target_pairs={{0,8},{8,0},{16,24},{24,16},{1,9},{9,1},{17,25},{25,17},{2,10},{10... | collective-permute-start | bytes 98312 | tf_op jit(solution)/shard_map/ppermute | solution.py:33
  42.4 0.7 %collective-permute-start.7 = (f32[64,128]{1,0:T(8,128)S(1)}, f32[64,128]{1,0:T(8,128)S(1)}, u32[]{:S(2)}, u32[]{:S(2)}) collective-permute-start(f32[64,128]{1,0:T(8,128)S(1)} %get-tuple-element.22), channel_id=1, source_target_pairs={{0,16},{8,24},{16,0},{24,8},{1,17},{9,25},{17,1},{25,9},{2,18},{10... | collective-permute-start | bytes 98312 | tf_op jit(solution)/shard_map/ppermute | solution.py:33
  43.1 1.7 %collective-permute-start.8 = (f32[64,128]{1,0:T(8,128)S(1)}, f32[64,128]{1,0:T(8,128)S(1)}, u32[]{:S(2)}, u32[]{:S(2)}) collective-permute-start(f32[64,128]{1,0:T(8,128)S(1)} %get-tuple-element.23), channel_id=1, source_target_pairs={{0,24},{8,16},{16,8},{24,0},{1,25},{9,17},{17,9},{25,1},{2,26},{10... | collective-permute-start | bytes 98312 | tf_op jit(solution)/shard_map/ppermute | solution.py:33
  44.9 2.4 %collective-permute-done.7.refs_2_ = f32[64,128]{1,0:T(8,128)S(1)} collective-permute-done((f32[64,128]{1,0:T(8,128)S(1)}, f32[64,128]{1,0:T(8,128)S(1)}, u32[]{:S(2)}, u32[]{:S(2)}) %collective-permute-start.7) | collective-permute-done | bytes 32800 | tf_op jit(solution)/shard_map/ppermute | solution.py:33
  47.2 1.6 %collective-permute-done.8.refs_3_ = f32[64,128]{1,0:T(8,128)S(1)} collective-permute-done((f32[64,128]{1,0:T(8,128)S(1)}, f32[64,128]{1,0:T(8,128)S(1)}, u32[]{:S(2)}, u32[]{:S(2)}) %collective-permute-start.8) | collective-permute-done | bytes 32800 | tf_op jit(solution)/shard_map/ppermute | solution.py:33
  48.8 0.8 %join_kernel.1 = (f32[2,64,128]{2,1,0:T(8,128)}, f32[64,128]{1,0:T(8,128)}) custom-call(f32[64,128]{1,0:T(8,128)S(1)} %get-tuple-element.20.refs_0_, f32[64,128]{1,0:T(8,128)S(1)} %collective-permute-done.6.refs_1_, f32[64,128]{1,0:T(8,128)S(1)} %collective-permute-done.7.refs_2_, f32[64,128]{1,0:T(8,128)S(1)} %collective-permute-done.8.refs_3_), custom_call_target="tpu_custom_call" | custom-call | tf_op jit(solution)/shard_map/join_kernel/pallas_call | solution.py:52
  (23 shorter events, 0.1 us)
Async XLA Ops:
  0.6 0.7 %copy-start.6 = (f32[2,1,1,512]{3,2,1,0:T(1,128)S(1)}, f32[2,1,1,512]{3,2,1,0:T(1,128)}, u32[]{:S(2)}) copy-start(f32[2,1,1,512]{3,2,1,0:T(1,128)} %param.13) | copy-start | bytes 12292
  1.4 0.9 %copy-start.1 = (f32[64,128]{1,0:T(8,128)S(1)}, f32[64,128]{1,0:T(8,128)}, u32[]{:S(2)}) copy-start(f32[64,128]{1,0:T(8,128)} %refs_1_.1) | copy-start | bytes 98308
  2.2 0.8 %copy-start.2 = (f32[64,128]{1,0:T(8,128)S(1)}, f32[64,128]{1,0:T(8,128)}, u32[]{:S(2)}) copy-start(f32[64,128]{1,0:T(8,128)} %refs_2_.1) | copy-start | bytes 98308
  3.0 0.8 %copy-start.3 = (s32[64,128]{1,0:T(8,128)S(1)}, s32[64,128]{1,0:T(8,128)}, u32[]{:S(2)}) copy-start(s32[64,128]{1,0:T(8,128)} %refs_3_.1) | copy-start | bytes 98308
  3.8 0.8 %copy-start.4 = (f32[64,128]{1,0:T(8,128)S(1)}, f32[64,128]{1,0:T(8,128)}, u32[]{:S(2)}) copy-start(f32[64,128]{1,0:T(8,128)} %refs_4_.1) | copy-start | bytes 98308
  4.5 1.7 %copy-start = (f32[2,64,128]{2,1,0:T(8,128)S(1)}, f32[2,64,128]{2,1,0:T(8,128)}, u32[]{:S(2)}) copy-start(f32[2,64,128]{2,1,0:T(8,128)} %refs_0_.1) | copy-start | bytes 196612
  4.5 0.7 %copy-start.5 = (s32[2,1,1,512]{3,2,1,0:T(1,128)S(1)}, s32[2,1,1,512]{3,2,1,0:T(1,128)}, u32[]{:S(2)}) copy-start(s32[2,1,1,512]{3,2,1,0:T(1,128)} %param.12) | copy-start | bytes 12292
  4.5 1.6 %collective-permute-start = (f32[400,128]{1,0:T(8,128)S(1)}, f32[400,128]{1,0:T(8,128)S(1)}, u32[]{:S(2)}, u32[]{:S(2)}) collective-permute-start(f32[400,128]{1,0:T(8,128)S(1)} %constant_dynamic-update-slice_fusion), channel_id=1, source_target_pairs={{0,1},{1,0},{2,3},{3,2},{4,5},{5,4},{6,7},{7,6},{8,9},{9,8},{10,11... | collective-permute-start | bytes 614408 | tf_op jit(solution)/shard_map/ppermute | solution.py:359
  7.2 6.1 %collective-permute-start.1 = (f32[3,64,128]{2,1,0:T(8,128)S(1)}, f32[3,64,128]{2,1,0:T(8,128)S(1)}, u32[]{:S(2)}, u32[]{:S(2)}) collective-permute-start(f32[3,64,128]{2,1,0:T(8,128)S(1)} %get-tuple-element.14), channel_id=1, source_target_pairs={{0,8},{8,0},{16,24},{24,16},{1,9},{9,1},{17,25},{25,17},{2,10},{10... | collective-permute-start | bytes 294920 | tf_op jit(solution)/shard_map/ppermute | solution.py:33
  10.2 10.7 %collective-permute-start.2 = (f32[3,64,128]{2,1,0:T(8,128)S(1)}, f32[3,64,128]{2,1,0:T(8,128)S(1)}, u32[]{:S(2)}, u32[]{:S(2)}) collective-permute-start(f32[3,64,128]{2,1,0:T(8,128)S(1)} %get-tuple-element.15), channel_id=1, source_target_pairs={{0,16},{8,24},{16,0},{24,8},{1,17},{9,25},{17,1},{25,9},{2,18},{10... | collective-permute-start | bytes 294920 | tf_op jit(solution)/shard_map/ppermute | solution.py:33
  12.8 8.1 %collective-permute-start.3 = (f32[3,64,128]{2,1,0:T(8,128)S(1)}, f32[3,64,128]{2,1,0:T(8,128)S(1)}, u32[]{:S(2)}, u32[]{:S(2)}) collective-permute-start(f32[3,64,128]{2,1,0:T(8,128)S(1)} %get-tuple-element.16), channel_id=1, source_target_pairs={{0,24},{8,16},{16,8},{24,0},{1,25},{9,17},{17,9},{25,1},{2,26},{10... | collective-permute-start | bytes 294920 | tf_op jit(solution)/shard_map/ppermute | solution.py:33
  20.9 5.8 %collective-permute-start.4 = (f32[16,16,128]{2,1,0:T(8,128)S(1)}, f32[16,16,128]{2,1,0:T(8,128)S(1)}, u32[]{:S(2)}, u32[]{:S(2)}) collective-permute-start(f32[16,16,128]{2,1,0:T(8,128)S(1)} %get-tuple-element.18), channel_id=1, source_target_pairs={{0,2},{2,0},{4,6},{6,4},{1,3},{3,1},{5,7},{7,5},{8,10},{10,8},{12,... | collective-permute-start | bytes 393224 | tf_op jit(solution)/shard_map/ppermute | solution.py:375
  22.4 5.9 %collective-permute-start.5 = (f32[16,16,128]{2,1,0:T(8,128)S(1)}, f32[16,16,128]{2,1,0:T(8,128)S(1)}, u32[]{:S(2)}, u32[]{:S(2)}) collective-permute-start(f32[16,16,128]{2,1,0:T(8,128)S(1)} %get-tuple-element.19), channel_id=1, source_target_pairs={{2,4},{4,2},{6,0},{0,6},{3,5},{5,3},{7,1},{1,7},{10,12},{12,10},{1... | collective-permute-start | bytes 393224 | tf_op jit(solution)/shard_map/ppermute | solution.py:375
  39.7 5.2 %collective-permute-start.6 = (f32[64,128]{1,0:T(8,128)S(1)}, f32[64,128]{1,0:T(8,128)S(1)}, u32[]{:S(2)}, u32[]{:S(2)}) collective-permute-start(f32[64,128]{1,0:T(8,128)S(1)} %get-tuple-element.21), channel_id=1, source_target_pairs={{0,8},{8,0},{16,24},{24,16},{1,9},{9,1},{17,25},{25,17},{2,10},{10... | collective-permute-start | bytes 98312 | tf_op jit(solution)/shard_map/ppermute | solution.py:33
  42.4 4.8 %collective-permute-start.7 = (f32[64,128]{1,0:T(8,128)S(1)}, f32[64,128]{1,0:T(8,128)S(1)}, u32[]{:S(2)}, u32[]{:S(2)}) collective-permute-start(f32[64,128]{1,0:T(8,128)S(1)} %get-tuple-element.22), channel_id=1, source_target_pairs={{0,16},{8,24},{16,0},{24,8},{1,17},{9,25},{17,1},{25,9},{2,18},{10... | collective-permute-start | bytes 98312 | tf_op jit(solution)/shard_map/ppermute | solution.py:33
  43.1 5.7 %collective-permute-start.8 = (f32[64,128]{1,0:T(8,128)S(1)}, f32[64,128]{1,0:T(8,128)S(1)}, u32[]{:S(2)}, u32[]{:S(2)}) collective-permute-start(f32[64,128]{1,0:T(8,128)S(1)} %get-tuple-element.23), channel_id=1, source_target_pairs={{0,24},{8,16},{16,8},{24,0},{1,25},{9,17},{17,9},{25,1},{2,26},{10... | collective-permute-start | bytes 98312 | tf_op jit(solution)/shard_map/ppermute | solution.py:33

commit v3 on v0

v3 whole, which is shorter than its diff:
```python
import functools

import jax
import jax.numpy as jnp
from jax import lax
from jax.experimental import pallas as pl
from jax.experimental.pallas import tpu as pltpu
from jax.sharding import PartitionSpec as P

STEPS = 4
OUTER = 2
HALO = 2 * STEPS * OUTER
LANES = 128

bed_rate = 0.1
state_rate = 0.5


def partner(index, shift, count):
    if count & (count - 1) == 0:
        return index ^ shift
    return (index + shift) % count


def source(index, shift, count):
    if count & (count - 1) == 0:
        return index ^ shift
    return (index + count - shift) % count


def exchange(value, axis, shift):
    count = lax.axis_size(axis)
    return lax.ppermute(value, axis, [(i, partner(i, shift, count)) for i in range(count)])


def neighbour_swaps(axis):
    count = lax.axis_size(axis)
    if count == 1:
        return []
    first = [(i, i ^ 1) for i in range(count)]
    if count == 2:
        return [first]
    second = []
    for i in range(1, count, 2):
        j = (i + 1) % count
        second += [(i, j), (j, i)]
    return [first, second]


def call(kernel, out_shape, operands, scratch=(), inputs=pltpu.VMEM):
    spec = pl.BlockSpec(memory_space=pltpu.VMEM)
    return pl.pallas_call(
        kernel,
        out_shape=out_shape,
        in_specs=[pl.BlockSpec(memory_space=inputs)] * len(operands),
        out_specs=jax.tree.map(lambda _: spec, out_shape),
        scratch_shapes=list(scratch),
        name=kernel.func.__name__,
        compiler_params=pltpu.CompilerParams(vmem_limit_bytes=16 << 20),
    )(*operands)


def lane_of(shape):
    return lax.broadcasted_iota(jnp.int32, shape, len(shape) - 1)


def near_first(even, number):
    return even if number == 0 else jnp.logical_not(even)


def copy_kernel(dims, *refs):
    slices, rows, cols, lists, sides = dims
    states, bed, back, mask, rate, cells, values = refs[:7]
    own = refs[7]
    sends = refs[8 : 8 + sides]
    mask_in, cells_in, sems = refs[8 + sides :]
    top = (slices + 4) * rows
    pairs = [(states.at[s], own.at[s * rows : (s + 1) * rows]) for s in range(slices)]
    for i, ref in ((0, bed), (1, back), (3, rate)):
        pairs.append((ref, own.at[(slices + i) * rows : (slices + i + 1) * rows]))
    pairs += [(mask, mask_in), (cells, cells_in), (values, own.at[top + lists : top + 2 * lists])]
    copies = [pltpu.make_async_copy(a, b, sems.at[i]) for i, (a, b) in enumerate(pairs)]
    for copy in copies:
        copy.start()
    for copy in copies:
        copy.wait()
    own[(slices + 2) * rows : (slices + 3) * rows] = mask_in[...].astype(jnp.float32)
    own[top : top + lists] = cells_in[...].astype(jnp.float32)
    even = (lax.axis_index("gy") & 1) == 0
    lane = lane_of((rows, LANES))
    for i, send in enumerate(sends):
        first = jnp.where(near_first(even, i), cols - HALO, 0)
        out = jnp.zeros((rows, LANES), jnp.float32)
        for j in range(slices + 4):
            shift = (HALO * j - first + 2 * LANES) % LANES
            moved = pltpu.roll(own[j * rows : (j + 1) * rows], shift, 1)
            out = jnp.where((lane >= HALO * j) & (lane < HALO * (j + 1)), moved, out)
        send[0:rows] = out
        send[rows : rows + 2 * lists] = own[top : top + 2 * lists]


def pack_kernel(dims, *refs):
    slices, rows, cols, lists, group, sides, cut, width = dims
    own = refs[0]
    near = refs[1 : 1 + sides]
    blocks = refs[1 + sides : 1 + sides + group]
    statics = refs[1 + sides + group]
    me = lax.axis_index("tm")
    y = lax.axis_index("gy")
    last_y = lax.axis_size("gy") - 1
    lane = lane_of((rows, LANES))
    even = (y & 1) == 0
    top = (slices + 4) * rows

    def placed(number, start, offset):
        column = lane - offset + start
        shift = offset - start + 4 * LANES
        value = pltpu.roll(own[number * rows : (number + 1) * rows], shift % LANES, 1)
        for i, ref in enumerate(near):
            after = near_first(even, i)
            there = pltpu.roll(ref[0:rows], (shift - HALO * number + jnp.where(after, cols, -HALO)) % LANES, 1)
            if sides == 1:
                beyond = (column < 0) | (column >= cols)
            else:
                beyond = ((column >= cols) & after) | ((column < 0) & jnp.logical_not(after))
            value = jnp.where(beyond, there, value)
        if number == slices + 2:
            left = (column < 0) & (y == 0)
            right = (column >= cols) & (y == last_y)
            value = jnp.where(left | right, 0.0, value)
        return value

    def packed(numbers, start):
        out = placed(numbers[0], start, 0)
        for s, number in enumerate(numbers[1:], 1):
            out = jnp.where(lane >= s * width, placed(number, start, s * width), out)
        return out

    for k in range(group):
        start = partner(me, k, group) * cut - HALO
        blocks[k][0:rows] = packed(list(range(slices)), start)
        blocks[k][rows : rows + 2 * lists] = own[top : top + 2 * lists]
        for i, ref in enumerate(near):
            low = rows + 2 * lists * (i + 1)
            blocks[k][low : low + 2 * lists] = ref[rows : rows + 2 * lists]
    start = me * cut - HALO
    statics[0] = packed([slices, slices + 1], start)
    statics[1] = packed([slices + 2, slices + 3], start)


def maps_kernel(dims, *refs):
    slices, rows, cols, lists, group, sides, cut, width = dims
    blocks, statics = refs[:group], refs[group]
    maps = refs[group + 1]
    sends = refs[group + 2 :]
    start = lax.axis_index("tm") * cut - HALO
    even = (lax.axis_index("gy") & 1) == 0
    each = lists // slices
    for k in range(group):
        found = [[], []]
        for s in range(slices):
            row, col, value = [], [], []
            for side in range(1 + sides):
                low = rows + 2 * lists * side + each * s
                shift = -start
                if side:
                    shift = shift + jnp.where(near_first(even, side - 1), cols, -cols)
                for j in range(each):
                    cell = blocks[k][low + j : low + j + 1].astype(jnp.int32)
                    row.append(cell // cols)
                    col.append(cell % cols + shift)
                    value.append(blocks[k][low + lists + j : low + lists + j + 1])
            row, col, value = (jnp.concatenate(v, axis=1) for v in (row, col, value))
            n = row.shape[1]
            at_row = lax.broadcasted_iota(jnp.int32, (rows, n), 0) == row
            at_col = lax.broadcasted_iota(jnp.int32, (width, n), 0) == col
            left = jnp.where(at_row, 1.0, 0.0).astype(jnp.bfloat16)
            part1 = value.astype(jnp.bfloat16).astype(jnp.float32)
            rest = value - part1
            part2 = rest.astype(jnp.bfloat16).astype(jnp.float32)
            weights = (jnp.ones_like(value), part1, part2, rest - part2)
            right = jnp.concatenate([jnp.where(at_col, w, 0.0).astype(jnp.bfloat16) for w in weights], axis=0)
            out = lax.dot_general(left, right, (((1,), (1,)), ((), ())), preferred_element_type=jnp.float32)
            found[0].append(out[:, 0:width])
            found[1].append(out[:, width : 2 * width] + (out[:, 2 * width : 3 * width] + out[:, 3 * width : 4 * width]))
        for i in range(2):
            parts = found[i]
            if slices * width < LANES:
                parts = parts + [jnp.zeros((rows, LANES - slices * width), jnp.float32)]
            maps[2 * k + i] = jnp.concatenate(parts, axis=1)
    even = (lax.axis_index("gx") & 1) == 0
    for i, send in enumerate(sends):
        low = pl.multiple_of(jnp.where(near_first(even, i), rows - HALO, 0), 8)
        for k in range(group):
            send[k] = blocks[k][pl.ds(low, HALO)]
        send[group : 3 * group] = maps[:, pl.ds(low, HALO)]
        send[3 * group : 3 * group + 2] = statics[:, pl.ds(low, HALO)]


def main_kernel(dims, *refs):
    slices, rows, group, sides, cut, width = dims
    blocks, statics, maps = refs[:group], refs[group], refs[group + 1]
    edges = refs[group + 2 : group + 2 + sides]
    outs = refs[group + 2 + sides : 2 * group + 2 + sides]
    state, count, total, fixed, final, misfit, keep, coef = refs[2 * group + 2 + sides :]
    me = lax.axis_index("tm")
    x = lax.axis_index("gx")
    last_x = lax.axis_size("gx") - 1
    even = (x & 1) == 0
    full = rows + 2 * HALO
    wrap = (slices - 1) * width

    def put(target, main, pieces):
        target[HALO : HALO + rows] = main
        if sides < 2:
            target[0:HALO] = jnp.zeros((HALO, LANES), jnp.float32)
            target[HALO + rows : full] = jnp.zeros((HALO, LANES), jnp.float32)
        for i, piece in enumerate(pieces):
            after = near_first(even, i)
            target[pl.ds(pl.multiple_of(jnp.where(after, HALO + rows, 0), 8), HALO)] = piece

    for k in range(group):
        pair = source(me, k, group)
        put(state.at[pair], blocks[k][0:rows], [e[k] for e in edges])
        put(count.at[pair], maps[2 * k], [e[group + 2 * k] for e in edges])
        put(total.at[pair], maps[2 * k + 1], [e[group + 2 * k + 1] for e in edges])
    for i in range(2):
        put(fixed.at[i], statics[i], [e[3 * group + i] for e in edges])

    row = lax.broadcasted_iota(jnp.int32, (full, LANES), 0)
    lane = lane_of((full, LANES))
    down = lambda v: pltpu.roll(v, v.shape[0] - 1, 0)
    up = lambda v: pltpu.roll(v, 1, 0)
    right = lambda v: pltpu.roll(v, LANES - 1, 1)
    left = lambda v: pltpu.roll(v, 1, 1)
    moves = ((down, up), (right, left))

    def spread(value):
        out = value
        for s in range(1, slices):
            out = jnp.where(lane[: value.shape[0]] >= s * width, pltpu.roll(value, s * width, 1), out)
        return out

    second = lambda v: pltpu.roll(v, LANES - width, 1)
    outside = ((row < HALO) & (x == 0)) | ((row >= HALO + rows) & (x == last_x))
    mask = jnp.where(outside, 0.0, spread(fixed[1]))
    rate = spread(second(fixed[1]))
    prior = spread(fixed[0])
    background = second(fixed[0])
    seam = lane % width == width - 1
    if LANES != slices * width:
        seam = seam | (lane >= slices * width)
    coef[0] = 0.25 * (rate + down(rate)) * (mask * down(mask))
    coef[1] = jnp.where(seam, 0.0, 0.25 * (rate + right(rate)) * (mask * right(mask)))
    fixed[0] = prior
    fixed[1] = background
    fixed[2] = prior

    pairs = range(group)
    for outer in range(OUTER):
        low = 2 * STEPS * outer
        high = full - low
        size = high - low
        span = pl.ds(low, size)
        here = lane[:size]
        bed = fixed[2, span]
        coef[0, span] = jnp.where(row[:size] == size - 1, 0.0, coef[0, span])
        coef[2, span] = down(bed) - bed
        coef[3, span] = right(bed) - bed

        thick = [state[p, span] for p in pairs]
        for step in range(STEPS):
            fluxes = []
            for d, (ahead, behind) in enumerate(moves):
                there = [ahead(v) for v in thick]
                flux = []
                for p in pairs:
                    both = thick[p] + there[p]
                    slope = (there[p] - thick[p]) + coef[2 + d, span]
                    scaled = coef[d, span] * both
                    half = 0.5 * both
                    by_mean = scaled * slope
                    keep[p, step, 2 * d, span] = half * scaled
                    keep[p, step, 2 * d + 1, span] = by_mean
                    flux.append(half * by_mean)
                fluxes.append((flux, [behind(v) for v in flux]))
            thick = [
                thick[p] + ((fluxes[0][0][p] - fluxes[0][1][p]) + (fluxes[1][0][p] - fluxes[1][1][p])) for p in pairs
            ]
        for p in pairs:
            final[p, span] = thick[p]

        for p in pairs:
            own = final[p, span]
            start = pltpu.roll(final[p - 1, span], (LANES - wrap) % LANES, 1) if p else fixed[1, span]
            earlier = jnp.where(here < width, start, pltpu.roll(own, width, 1))
            misfit[p, span] = state[p, span] - earlier
        pull = []
        for p in pairs:
            later = pltpu.roll(misfit[p, span], LANES - width, 1)
            after = pltpu.roll(misfit[p + 1, span], wrap, 1) if p + 1 < group else 0.0
            later = jnp.where(here < wrap, later, after)
            pull.append(count[p, span] * final[p, span] - total[p, span] - later)

        sums = [None, None]
        for step in reversed(range(STEPS)):
            parts = []
            for d, (ahead, behind) in enumerate(moves):
                jump = [v - ahead(v) for v in pull]
                own, passed = [], []
                for p in pairs:
                    by_slope = keep[p, step, 2 * d, span] * jump[p]
                    by_mean = keep[p, step, 2 * d + 1, span] * jump[p]
                    sums[d] = by_slope if sums[d] is None else sums[d] + by_slope
                    own.append(by_mean - by_slope)
                    passed.append(by_mean + by_slope)
                parts.append((own, [behind(v) for v in passed]))
            pull = [pull[p] + ((parts[0][0][p] + parts[0][1][p]) + (parts[1][0][p] + parts[1][1][p])) for p in pairs]
        for p in pairs:
            state[p, span] = state[p, span] - state_rate * (misfit[p, span] + pull[p])
        by_x, by_y = sums
        each = (up(by_x) - by_x) + (left(by_y) - by_y)
        summed = each
        for s in range(1, slices):
            summed = summed + pltpu.roll(each, LANES - s * width, 1)
        fixed[2, span] = bed - bed_rate * (spread(summed) + (bed - prior[low:high]))

    inner = slice(HALO, HALO + rows)

    def fold(value, used):
        parts = LANES // used
        height = value.shape[0] // parts
        out = value[0:height]
        place = lane_of((height, LANES))
        for i in range(1, parts):
            moved = pltpu.roll(value[i * height : (i + 1) * height], i * used, 1)
            out = jnp.where(place >= i * used, moved, out)
        return out

    place = lane_of((rows, LANES))
    ground = fold(pltpu.roll(fixed[2, inner], LANES - HALO, 1), cut)
    for k in range(group):
        mine = state[partner(me, k, group), inner]
        out = pltpu.roll(mine, LANES - HALO, 1)
        for s in range(1, slices):
            out = jnp.where(place >= s * cut, pltpu.roll(mine, (s * cut - s * width - HALO) % LANES, 1), out)
        folded = fold(out, slices * cut)
        outs[k][0 : folded.shape[0]] = folded
        outs[k][folded.shape[0] :] = ground


def join_kernel(dims, *refs):
    slices, rows, group, cut = dims
    pieces, states, bed = refs[:group], refs[group], refs[group + 1]
    me = lax.axis_index("tm")
    height = rows * slices * cut // LANES
    for target, used, low, count in [(states.at[s], slices * cut, s * cut, height) for s in range(slices)] + [
        (bed, cut, 0, rows * cut // LANES)
    ]:
        base = 0 if count == height and target is not bed else height
        lane = lane_of((count, LANES))
        for i in range(LANES // used):
            out = jnp.zeros((count, LANES), jnp.float32)
            for k in range(group):
                first = source(me, k, group) * cut
                moved = pltpu.roll(pieces[k][base : base + count], (first - i * used - low + 2 * LANES) % LANES, 1)
                out = jnp.where((lane >= first) & (lane < first + cut), moved, out)
            target[i * count : (i + 1) * count] = out


def per_device(states, bed, background_state, ice_mask, flow_rate, obs_cell, obs_value):
    slices, rows, cols = states.shape
    group = lax.axis_size("tm")
    cut = cols // group
    width = cut + 2 * HALO
    full = rows + 2 * HALO
    lists = slices * obs_cell.shape[-1] // LANES
    f32 = lambda *shape: jax.ShapeDtypeStruct(shape, jnp.float32)
    vmem = lambda *shape: pltpu.VMEM(shape, jnp.float32)

    swaps_y = neighbour_swaps("gy")
    sides = len(swaps_y)
    own, *sends = call(
        functools.partial(copy_kernel, (slices, rows, cols, lists, sides)),
        [f32((slices + 4) * rows + 2 * lists, cols)] + [f32(rows + 2 * lists, LANES)] * sides,
        [pltpu.with_memory_space_constraint(v, pltpu.HBM) for v in (states, bed, background_state, ice_mask, flow_rate, obs_cell.reshape(lists, LANES), obs_value.reshape(lists, LANES))],
        [pltpu.VMEM((rows, cols), jnp.int32), pltpu.VMEM((lists, LANES), jnp.int32), pltpu.SemaphoreType.DMA((slices + 6,))],
        inputs=pltpu.HBM,
    )
    near = [lax.ppermute(send, "gy", pairs) for send, pairs in zip(sends, swaps_y)]
    dims = (slices, rows, cols, lists, group, sides, cut, width)
    *blocks, statics = call(
        functools.partial(pack_kernel, dims),
        [f32(rows + 2 * lists * (1 + sides), LANES)] * group + [f32(2, rows, LANES)],
        [own, *near],
    )
    blocks = [blocks[0]] + [exchange(blocks[k], "tm", k) for k in range(1, group)]
    swaps_x = neighbour_swaps("gx")
    maps, *sends = call(
        functools.partial(maps_kernel, dims),
        [f32(2 * group, rows, LANES)] + [f32(3 * group + 2, HALO, LANES)] * len(swaps_x),
        [*blocks, statics],
    )
    edges = [lax.ppermute(send, "gx", pairs) for send, pairs in zip(sends, swaps_x)]
    packed = call(
        functools.partial(main_kernel, (slices, rows, group, len(edges), cut, width)),
        [f32(rows * (slices + 1) * cut // LANES, LANES)] * group,
        [*blocks, statics, maps, *edges],
        [vmem(group, full, LANES)] * 3
        + [vmem(3, full, LANES)]
        + [vmem(group, full, LANES)] * 2
        + [vmem(group, STEPS, 4, full, LANES), vmem(4, full, LANES)],
    )
    pieces = [packed[0]] + [exchange(packed[k], "tm", k) for k in range(1, group)]
    return tuple(
        call(
            functools.partial(join_kernel, (slices, rows, group, cut)),
            [f32(slices, rows, cols), f32(rows, cols)],
            pieces,
        )
    )


def solution(mesh):
    placed = (
        P("tm", "gx", "gy"),
        P("gx", "gy"),
        P("gx", "gy"),
        P("gx", "gy"),
        P("gx", "gy"),
        P("tm", "gx", "gy", None),
        P("tm", "gx", "gy", None),
    )
    return jax.shard_map(
        per_device,
        mesh=mesh,
        in_specs=placed,
        out_specs=(P("tm", "gx", "gy"), P("gx", "gy")),
        check_vma=False,
    )
```

time: 174 us -> 35.6 us (0.20); the launches traced: 171 us -> 35.4 us
  starting transfers between devices: 73.4 us -> 13.6 us
  blocking collectives: 42.3 us -> 0 us
  other arithmetic: 27.9 us -> 0 us
  local copies, waits for them, and re-layouts: 15.7 us -> 0 us
  Pallas kernels: 0 us -> 7.33 us
  waiting for transfers between devices: 10.2 us -> 13.8 us
    ppermute x28 -> x9, starting transfers between devices: 73.4 us -> 13.6 us  [the longest x6 9.99 us: exchange(): lax.ppermute(value, axis, [(i, partner(i, shift, count)) for i in range(c...]
    psum x2 -> x0, blocking collectives: 42.3 us -> none  [per_device(): total = lax.psum(bed_grad, 'tm')]
    gather x2 -> x0, local copies, waits for them, and re-layouts: 12.3 us -> none  [per_device(): predicted = final.reshape(-1)[cell_index]]
    scatter-add x2 -> x0, other arithmetic: 11.9 us -> none  [per_device(): spread = jnp.zeros((slices_here * rows_here * cols_here,), jnp.float32).a...]
    pallas_call x0 -> x5, Pallas kernels: none -> 7.33 us  [call(): pl.pallas_call(kernel, out_shape=out_shape, in_specs=[pl.BlockSpec(memory...]
    neg x24 -> x0, other arithmetic: 5.54 us -> none  [the longest x8 2.07 us: advance(): flux_y[1:-1, 1:] - flux_y[1:-1, :-1]]
    mul x31 -> x0, other arithmetic: 3.65 us -> none  [the longest x15 2.23 us: advance(): flux_y = coef_y * mean_y * mean_y * (surface[:, 1:] - surface[:, :-1])]
    ppermute x28 -> x9, waiting for transfers between devices: 10.2 us -> 13.8 us  [the longest x6 8.75 us: exchange(): lax.ppermute(value, axis, [(i, partner(i, shift, count)) for i in range(c...]
  transfers between devices with their start and end apart: 28 -> 9, of which waited for: 10 -> 7; matrix products, arithmetic and copies ran while one was open for 17% -> 0% of each run, Pallas kernels for 0% -> 0%
where the time goes in v3:
time: 35.6 us; the launch traced here: 35.4 us
  waiting for transfers between devices  13.8 us (39%)
  starting transfers between devices  13.6 us (38%)
  Pallas kernels  7.33 us (21%)
  between operations  0.67 us (2%)
    ppermute x6, starting transfers between devices, exchange(): lax.ppermute(value, axis, [(i, partner(i, shift, count)) for i in range(c...  9.99 us
    ppermute x6, waiting for transfers between devices, exchange(): lax.ppermute(value, axis, [(i, partner(i, shift, count)) for i in range(c...  8.75 us
    pallas_call x5, Pallas kernels, call(): pl.pallas_call(kernel, out_shape=out_shape, in_specs=[pl.BlockSpec(memory...  7.33 us
    ppermute x2, waiting for transfers between devices, per_device(): lax.ppermute(send, 'gx', pairs)  4.2 us
    ppermute x2, starting transfers between devices, per_device(): lax.ppermute(send, 'gx', pairs)  3.05 us
    ppermute x1, waiting for transfers between devices, per_device(): lax.ppermute(send, 'gy', pairs)  0.87 us
  transfers between devices with their start and end apart: 9, of which 7 were waited for; matrix products, arithmetic and copies ran while one was open for 0% of the time, Pallas kernels for 0%

profile of v3, /device:TPU:0, one launch (start us, length us, event | category | flops | bytes accessed | tf_op | source)
XLA Modules:
  0.0 35.4 jit_solution(7481498939557065818)
XLA Ops:
  0.6 1.0 %copy_kernel.1 = (f32[400,128]{1,0:T(8,128)S(1)}, f32[80,128]{1,0:T(8,128)S(1)}) custom-call(f32[2,64,128]{2,1,0:T(8,128)} %refs_0_.1, f32[64,128]{1,0:T(8,128)} %refs_1_.1, f32[64,128]{1,0:T(8,128)} %refs_2_.1, s32[64,128]{1,0:T(8,128)} %refs_3_.1, f32[64,128]{1,0:T(8,128)} %refs_4_.1, s32[8,128]{1,0:T(8,128)} %bitcast.2, f32[8,128]{1,0:T(8,128)} %bitcast.3), custom_call_target="tpu_custom_call" | custom-call | tf_op jit(solution)/shard_map/copy_kernel/pallas_call | solution.py:52
  1.7 0.6 %collective-permute-start = (f32[80,128]{1,0:T(8,128)S(1)}, f32[80,128]{1,0:T(8,128)S(1)}, u32[]{:S(2)}, u32[]{:S(2)}) collective-permute-start(f32[80,128]{1,0:T(8,128)S(1)} %get-tuple-element.17), channel_id=1, source_target_pairs={{0,1},{1,0},{2,3},{3,2},{4,5},{5,4},{6,7},{7,6},{8,9},{9,8},{10,11... | collective-permute-start | bytes 122888 | tf_op jit(solution)/shard_map/ppermute | solution.py:390
  2.2 0.9 %collective-permute-done.refs_1_ = f32[80,128]{1,0:T(8,128)S(1)} collective-permute-done((f32[80,128]{1,0:T(8,128)S(1)}, f32[80,128]{1,0:T(8,128)S(1)}, u32[]{:S(2)}, u32[]{:S(2)}) %collective-permute-start) | collective-permute-done | bytes 40992 | tf_op jit(solution)/shard_map/ppermute | solution.py:390
  3.1 0.3 pack_kernel.1
  3.4 3.0 %collective-permute-start.1 = (f32[96,128]{1,0:T(8,128)S(1)}, f32[96,128]{1,0:T(8,128)S(1)}, u32[]{:S(2)}, u32[]{:S(2)}) collective-permute-start(f32[96,128]{1,0:T(8,128)S(1)} %get-tuple-element.19), channel_id=1, source_target_pairs={{0,8},{8,0},{16,24},{24,16},{1,9},{9,1},{17,25},{25,17},{2,10},{10... | collective-permute-start | bytes 147464 | tf_op jit(solution)/shard_map/ppermute | solution.py:33
  6.4 2.6 %collective-permute-start.2 = (f32[96,128]{1,0:T(8,128)S(1)}, f32[96,128]{1,0:T(8,128)S(1)}, u32[]{:S(2)}, u32[]{:S(2)}) collective-permute-start(f32[96,128]{1,0:T(8,128)S(1)} %get-tuple-element.20), channel_id=1, source_target_pairs={{0,16},{8,24},{16,0},{24,8},{1,17},{9,25},{17,1},{25,9},{2,18},{10... | collective-permute-start | bytes 147464 | tf_op jit(solution)/shard_map/ppermute | solution.py:33
  9.0 0.0 collective-permute-start.3
  9.0 0.0 collective-permute-done.1.refs_1_
  9.0 3.3 %collective-permute-done.2.refs_2_ = f32[96,128]{1,0:T(8,128)S(1)} collective-permute-done((f32[96,128]{1,0:T(8,128)S(1)}, f32[96,128]{1,0:T(8,128)S(1)}, u32[]{:S(2)}, u32[]{:S(2)}) %collective-permute-start.2) | collective-permute-done | bytes 49184 | tf_op jit(solution)/shard_map/ppermute | solution.py:33
  12.2 2.6 %collective-permute-done.3.refs_3_ = f32[96,128]{1,0:T(8,128)S(1)} collective-permute-done((f32[96,128]{1,0:T(8,128)S(1)}, f32[96,128]{1,0:T(8,128)S(1)}, u32[]{:S(2)}, u32[]{:S(2)}) %collective-permute-start.3) | collective-permute-done | bytes 49184 | tf_op jit(solution)/shard_map/ppermute | solution.py:33
  14.8 1.6 %maps_kernel.1 = (f32[8,64,128]{2,1,0:T(8,128)S(1)}, f32[14,16,128]{2,1,0:T(8,128)S(1)}, f32[14,16,128]{2,1,0:T(8,128)S(1)}) custom-call(f32[96,128]{1,0:T(8,128)S(1)} %get-tuple-element.18.refs_0_, f32[96,128]{1,0:T(8,128)S(1)} %collective-permute-done.1.refs_1_, f32[96,128]{1,0:T(8,128)S(1)} %collective-permute-done.2.refs_2_, ...), custom_call_target="tpu_custom_call" | custom-call | tf_op jit(solution)/shard_map/maps_kernel/pallas_call | solution.py:52
  16.5 1.6 %collective-permute-start.4 = (f32[14,16,128]{2,1,0:T(8,128)S(1)}, f32[14,16,128]{2,1,0:T(8,128)S(1)}, u32[]{:S(2)}, u32[]{:S(2)}) collective-permute-start(f32[14,16,128]{2,1,0:T(8,128)S(1)} %get-tuple-element.24), channel_id=1, source_target_pairs={{0,2},{2,0},{4,6},{6,4},{1,3},{3,1},{5,7},{7,5},{8,10},{10,8},{12,... | collective-permute-start | bytes 344072 | tf_op jit(solution)/shard_map/ppermute | solution.py:404
  18.0 1.5 %collective-permute-start.5 = (f32[14,16,128]{2,1,0:T(8,128)S(1)}, f32[14,16,128]{2,1,0:T(8,128)S(1)}, u32[]{:S(2)}, u32[]{:S(2)}) collective-permute-start(f32[14,16,128]{2,1,0:T(8,128)S(1)} %get-tuple-element.25), channel_id=1, source_target_pairs={{2,4},{4,2},{6,0},{0,6},{3,5},{5,3},{7,1},{1,7},{10,12},{12,10},{1... | collective-permute-start | bytes 344072 | tf_op jit(solution)/shard_map/ppermute | solution.py:404
  19.5 2.7 %collective-permute-done.4.refs_6_ = f32[14,16,128]{2,1,0:T(8,128)S(1)} collective-permute-done((f32[14,16,128]{2,1,0:T(8,128)S(1)}, f32[14,16,128]{2,1,0:T(8,128)S(1)}, u32[]{:S(2)}, u32[]{:S(2)}) %collective-permute-start.4) | collective-permute-done | bytes 114720 | tf_op jit(solution)/shard_map/ppermute | solution.py:404
  22.2 1.5 %collective-permute-done.5.refs_7_ = f32[14,16,128]{2,1,0:T(8,128)S(1)} collective-permute-done((f32[14,16,128]{2,1,0:T(8,128)S(1)}, f32[14,16,128]{2,1,0:T(8,128)S(1)}, u32[]{:S(2)}, u32[]{:S(2)}) %collective-permute-start.5) | collective-permute-done | bytes 114720 | tf_op jit(solution)/shard_map/ppermute | solution.py:404
  23.7 3.6 %main_kernel.1 = (f32[48,128]{1,0:T(8,128)S(1)}, f32[48,128]{1,0:T(8,128)S(1)}, f32[48,128]{1,0:T(8,128)S(1)}, f32[48,128]{1,0:T(8,128)S(1)}) custom-call(f32[96,128]{1,0:T(8,128)S(1)} %get-tuple-element.18.refs_0_, f32[96,128]{1,0:T(8,128)S(1)} %collective-permute-done.1.refs_1_, f32[96,128]{1,0:T(8,128)S(1)} %collective-permute-done.2.refs_2_, ...), custom_call_target="tpu_custom_call" | custom-call | tf_op jit(solution)/shard_map/main_kernel/pallas_call | solution.py:52
  27.3 0.1 collective-permute-start.6
  27.4 1.6 %collective-permute-start.7 = (f32[48,128]{1,0:T(8,128)S(1)}, f32[48,128]{1,0:T(8,128)S(1)}, u32[]{:S(2)}, u32[]{:S(2)}) collective-permute-start(f32[48,128]{1,0:T(8,128)S(1)} %get-tuple-element.28), channel_id=1, source_target_pairs={{0,16},{8,24},{16,0},{24,8},{1,17},{9,25},{17,1},{25,9},{2,18},{10... | collective-permute-start | bytes 73736 | tf_op jit(solution)/shard_map/ppermute | solution.py:33
  29.0 2.8 %collective-permute-start.8 = (f32[48,128]{1,0:T(8,128)S(1)}, f32[48,128]{1,0:T(8,128)S(1)}, u32[]{:S(2)}, u32[]{:S(2)}) collective-permute-start(f32[48,128]{1,0:T(8,128)S(1)} %get-tuple-element.29), channel_id=1, source_target_pairs={{0,24},{8,16},{16,8},{24,0},{1,25},{9,17},{17,9},{25,1},{2,26},{10... | collective-permute-start | bytes 73736 | tf_op jit(solution)/shard_map/ppermute | solution.py:33
  31.7 0.0 collective-permute-done.6.refs_1_
  31.7 0.4 %collective-permute-done.7.refs_2_ = f32[48,128]{1,0:T(8,128)S(1)} collective-permute-done((f32[48,128]{1,0:T(8,128)S(1)}, f32[48,128]{1,0:T(8,128)S(1)}, u32[]{:S(2)}, u32[]{:S(2)}) %collective-permute-start.7) | collective-permute-done | bytes 24608 | tf_op jit(solution)/shard_map/ppermute | solution.py:33
  32.2 2.4 %collective-permute-done.8.refs_3_ = f32[48,128]{1,0:T(8,128)S(1)} collective-permute-done((f32[48,128]{1,0:T(8,128)S(1)}, f32[48,128]{1,0:T(8,128)S(1)}, u32[]{:S(2)}, u32[]{:S(2)}) %collective-permute-start.8) | collective-permute-done | bytes 24608 | tf_op jit(solution)/shard_map/ppermute | solution.py:33
  34.6 0.8 %join_kernel.1 = (f32[2,64,128]{2,1,0:T(8,128)}, f32[64,128]{1,0:T(8,128)}) custom-call(f32[48,128]{1,0:T(8,128)S(1)} %get-tuple-element.26.refs_0_, f32[48,128]{1,0:T(8,128)S(1)} %collective-permute-done.6.refs_1_, f32[48,128]{1,0:T(8,128)S(1)} %collective-permute-done.7.refs_2_, f32[48,128]{1,0:T(8,128)S(1)} %collective-permute-done.8.refs_3_), custom_call_target="tpu_custom_call" | custom-call | tf_op jit(solution)/shard_map/join_kernel/pallas_call | solution.py:52
Async XLA Ops:
  1.7 1.4 %collective-permute-start = (f32[80,128]{1,0:T(8,128)S(1)}, f32[80,128]{1,0:T(8,128)S(1)}, u32[]{:S(2)}, u32[]{:S(2)}) collective-permute-start(f32[80,128]{1,0:T(8,128)S(1)} %get-tuple-element.17), channel_id=1, source_target_pairs={{0,1},{1,0},{2,3},{3,2},{4,5},{5,4},{6,7},{7,6},{8,9},{9,8},{10,11... | collective-permute-start | bytes 122888 | tf_op jit(solution)/shard_map/ppermute | solution.py:390
  3.4 5.6 %collective-permute-start.1 = (f32[96,128]{1,0:T(8,128)S(1)}, f32[96,128]{1,0:T(8,128)S(1)}, u32[]{:S(2)}, u32[]{:S(2)}) collective-permute-start(f32[96,128]{1,0:T(8,128)S(1)} %get-tuple-element.19), channel_id=1, source_target_pairs={{0,8},{8,0},{16,24},{24,16},{1,9},{9,1},{17,25},{25,17},{2,10},{10... | collective-permute-start | bytes 147464 | tf_op jit(solution)/shard_map/ppermute | solution.py:33
  6.4 5.9 %collective-permute-start.2 = (f32[96,128]{1,0:T(8,128)S(1)}, f32[96,128]{1,0:T(8,128)S(1)}, u32[]{:S(2)}, u32[]{:S(2)}) collective-permute-start(f32[96,128]{1,0:T(8,128)S(1)} %get-tuple-element.20), channel_id=1, source_target_pairs={{0,16},{8,24},{16,0},{24,8},{1,17},{9,25},{17,1},{25,9},{2,18},{10... | collective-permute-start | bytes 147464 | tf_op jit(solution)/shard_map/ppermute | solution.py:33
  9.0 5.9 %collective-permute-start.3 = (f32[96,128]{1,0:T(8,128)S(1)}, f32[96,128]{1,0:T(8,128)S(1)}, u32[]{:S(2)}, u32[]{:S(2)}) collective-permute-start(f32[96,128]{1,0:T(8,128)S(1)} %get-tuple-element.21), channel_id=1, source_target_pairs={{0,24},{8,16},{16,8},{24,0},{1,25},{9,17},{17,9},{25,1},{2,26},{10... | collective-permute-start | bytes 147464 | tf_op jit(solution)/shard_map/ppermute | solution.py:33
  16.5 5.7 %collective-permute-start.4 = (f32[14,16,128]{2,1,0:T(8,128)S(1)}, f32[14,16,128]{2,1,0:T(8,128)S(1)}, u32[]{:S(2)}, u32[]{:S(2)}) collective-permute-start(f32[14,16,128]{2,1,0:T(8,128)S(1)} %get-tuple-element.24), channel_id=1, source_target_pairs={{0,2},{2,0},{4,6},{6,4},{1,3},{3,1},{5,7},{7,5},{8,10},{10,8},{12,... | collective-permute-start | bytes 344072 | tf_op jit(solution)/shard_map/ppermute | solution.py:404
  18.0 5.7 %collective-permute-start.5 = (f32[14,16,128]{2,1,0:T(8,128)S(1)}, f32[14,16,128]{2,1,0:T(8,128)S(1)}, u32[]{:S(2)}, u32[]{:S(2)}) collective-permute-start(f32[14,16,128]{2,1,0:T(8,128)S(1)} %get-tuple-element.25), channel_id=1, source_target_pairs={{2,4},{4,2},{6,0},{0,6},{3,5},{5,3},{7,1},{1,7},{10,12},{12,10},{1... | collective-permute-start | bytes 344072 | tf_op jit(solution)/shard_map/ppermute | solution.py:404
  27.3 4.4 %collective-permute-start.6 = (f32[48,128]{1,0:T(8,128)S(1)}, f32[48,128]{1,0:T(8,128)S(1)}, u32[]{:S(2)}, u32[]{:S(2)}) collective-permute-start(f32[48,128]{1,0:T(8,128)S(1)} %get-tuple-element.27), channel_id=1, source_target_pairs={{0,8},{8,0},{16,24},{24,16},{1,9},{9,1},{17,25},{25,17},{2,10},{10... | collective-permute-start | bytes 73736 | tf_op jit(solution)/shard_map/ppermute | solution.py:33
  27.4 4.8 %collective-permute-start.7 = (f32[48,128]{1,0:T(8,128)S(1)}, f32[48,128]{1,0:T(8,128)S(1)}, u32[]{:S(2)}, u32[]{:S(2)}) collective-permute-start(f32[48,128]{1,0:T(8,128)S(1)} %get-tuple-element.28), channel_id=1, source_target_pairs={{0,16},{8,24},{16,0},{24,8},{1,17},{9,25},{17,1},{25,9},{2,18},{10... | collective-permute-start | bytes 73736 | tf_op jit(solution)/shard_map/ppermute | solution.py:33
  29.0 5.6 %collective-permute-start.8 = (f32[48,128]{1,0:T(8,128)S(1)}, f32[48,128]{1,0:T(8,128)S(1)}, u32[]{:S(2)}, u32[]{:S(2)}) collective-permute-start(f32[48,128]{1,0:T(8,128)S(1)} %get-tuple-element.29), channel_id=1, source_target_pairs={{0,24},{8,16},{16,8},{24,0},{1,25},{9,17},{17,9},{25,1},{2,26},{10... | collective-permute-start | bytes 73736 | tf_op jit(solution)/shard_map/ppermute | solution.py:33

commit v4 on v3

--- a/solution.py
+++ b/solution.py
@@ -7,6 +7,7 @@
 from jax.experimental.pallas import tpu as pltpu
 from jax.sharding import PartitionSpec as P
 
+
 STEPS = 4
 OUTER = 2
 HALO = 2 * STEPS * OUTER
@@ -16,38 +17,58 @@
 state_rate = 0.5
 
 
-def partner(index, shift, count):
+def partner(index, number, count):
+    shift = (count - number) % count
     if count & (count - 1) == 0:
         return index ^ shift
     return (index + shift) % count
 
 
-def source(index, shift, count):
+def source(index, number, count):
+    shift = (count - number) % count
     if count & (count - 1) == 0:
         return index ^ shift
     return (index + count - shift) % count
 
 
-def exchange(value, axis, shift):
+def exchange(value, axis, number):
     count = lax.axis_size(axis)
-    return lax.ppermute(value, axis, [(i, partner(i, shift, count)) for i in range(count)])
+    return lax.ppermute(value, axis, [(i, partner(i, number, count)) for i in range(count)])
 
 
 def neighbour_swaps(axis):
     count = lax.axis_size(axis)
     if count == 1:
         return []
-    first = [(i, i ^ 1) for i in range(count)]
+    near = [(i, i ^ 1) for i in range(count)]
     if count == 2:
-        return [first]
-    second = []
+        return [near]
+    far = []
     for i in range(1, count, 2):
         j = (i + 1) % count
-        second += [(i, j), (j, i)]
-    return [first, second]
-
-
-def call(kernel, out_shape, operands, scratch=(), inputs=pltpu.VMEM):
+        far += [(i, j), (j, i)]
+    return [far, near]
+
+
+def reaches_after(index, number, swaps):
+    return (index & 1) == (0 if number == swaps - 1 else 1)
+
+
+def exchange_all(values):
+    out = list(values)
+    for k in range(1, len(values)):
+        out[k] = exchange(values[k], "tm", k)
+    return out
+
+
+def swap_all(values, axis):
+    out = []
+    for value, pairs in zip(values, neighbour_swaps(axis)):
+        out.append(lax.ppermute(value, axis, pairs))
+    return out
+
+
+def call(kernel, out_shape, operands, scratch=(), inputs=pltpu.VMEM, cost=None):
     spec = pl.BlockSpec(memory_space=pltpu.VMEM)
     return pl.pallas_call(
         kernel,
@@ -55,17 +76,13 @@
         in_specs=[pl.BlockSpec(memory_space=inputs)] * len(operands),
         out_specs=jax.tree.map(lambda _: spec, out_shape),
         scratch_shapes=list(scratch),
-        name=kernel.func.__name__,
+        cost_estimate=cost,
         compiler_params=pltpu.CompilerParams(vmem_limit_bytes=16 << 20),
     )(*operands)
 
 
 def lane_of(shape):
     return lax.broadcasted_iota(jnp.int32, shape, len(shape) - 1)
-
-
-def near_first(even, number):
-    return even if number == 0 else jnp.logical_not(even)
 
 
 def copy_kernel(dims, *refs):
@@ -86,10 +103,10 @@
         copy.wait()
     own[(slices + 2) * rows : (slices + 3) * rows] = mask_in[...].astype(jnp.float32)
     own[top : top + lists] = cells_in[...].astype(jnp.float32)
-    even = (lax.axis_index("gy") & 1) == 0
+    y = lax.axis_index("gy")
     lane = lane_of((rows, LANES))
     for i, send in enumerate(sends):
-        first = jnp.where(near_first(even, i), cols - HALO, 0)
+        first = jnp.where(reaches_after(y, i, sides), cols - HALO, 0)
         out = jnp.zeros((rows, LANES), jnp.float32)
         for j in range(slices + 4):
             shift = (HALO * j - first + 2 * LANES) % LANES
@@ -109,7 +126,6 @@
     y = lax.axis_index("gy")
     last_y = lax.axis_size("gy") - 1
     lane = lane_of((rows, LANES))
-    even = (y & 1) == 0
     top = (slices + 4) * rows
 
     def placed(number, start, offset):
@@ -117,7 +133,7 @@
         shift = offset - start + 4 * LANES
         value = pltpu.roll(own[number * rows : (number + 1) * rows], shift % LANES, 1)
         for i, ref in enumerate(near):
-            after = near_first(even, i)
+            after = reaches_after(y, i, sides)
             there = pltpu.roll(ref[0:rows], (shift - HALO * number + jnp.where(after, cols, -HALO)) % LANES, 1)
             if sides == 1:
                 beyond = (column < 0) | (column >= cols)
@@ -148,65 +164,67 @@
     statics[1] = packed([slices + 2, slices + 3], start)
 
 
-def maps_kernel(dims, *refs):
-    slices, rows, cols, lists, group, sides, cut, width = dims
+def maps_kernel(dims, block, maps):
+    slices, rows, cols, lists, _, sides, cut, width = dims
+    start = lax.axis_index("tm") * cut - HALO
+    y = lax.axis_index("gy")
+    each = lists // slices
+    found = [[], []]
+    for s in range(slices):
+        row, col, value = [], [], []
+        for side in range(1 + sides):
+            low = rows + 2 * lists * side + each * s
+            shift = -start
+            if side:
+                shift = shift + jnp.where(reaches_after(y, side - 1, sides), cols, -cols)
+            for j in range(each):
+                cell = block[low + j : low + j + 1].astype(jnp.int32)
+                row.append(cell // cols)
+                col.append(cell % cols + shift)
+                value.append(block[low + lists + j : low + lists + j + 1])
+        row, col, value = (jnp.concatenate(v, axis=1) for v in (row, col, value))
+        n = row.shape[1]
+        at_row = lax.broadcasted_iota(jnp.int32, (rows, n), 0) == row
+        at_col = lax.broadcasted_iota(jnp.int32, (width, n), 0) == col
+        left = jnp.where(at_row, 1.0, 0.0).astype(jnp.bfloat16)
+        part1 = value.astype(jnp.bfloat16).astype(jnp.float32)
+        rest = value - part1
+        part2 = rest.astype(jnp.bfloat16).astype(jnp.float32)
+        weights = (jnp.ones_like(value), part1, part2, rest - part2)
+        right = jnp.concatenate([jnp.where(at_col, w, 0.0).astype(jnp.bfloat16) for w in weights], axis=0)
+        out = lax.dot_general(left, right, (((1,), (1,)), ((), ())), preferred_element_type=jnp.float32)
+        found[0].append(out[:, 0:width])
+        found[1].append(out[:, width : 2 * width] + (out[:, 2 * width : 3 * width] + out[:, 3 * width : 4 * width]))
+    for i in range(2):
+        parts = found[i]
+        if slices * width < LANES:
+            parts = parts + [jnp.zeros((rows, LANES - slices * width), jnp.float32)]
+        maps[i] = jnp.concatenate(parts, axis=1)
+
+
+def edge_kernel(dims, *refs):
+    rows, group = dims
     blocks, statics = refs[:group], refs[group]
-    maps = refs[group + 1]
-    sends = refs[group + 2 :]
-    start = lax.axis_index("tm") * cut - HALO
-    even = (lax.axis_index("gy") & 1) == 0
-    each = lists // slices
-    for k in range(group):
-        found = [[], []]
-        for s in range(slices):
-            row, col, value = [], [], []
-            for side in range(1 + sides):
-                low = rows + 2 * lists * side + each * s
-                shift = -start
-                if side:
-                    shift = shift + jnp.where(near_first(even, side - 1), cols, -cols)
-                for j in range(each):
-                    cell = blocks[k][low + j : low + j + 1].astype(jnp.int32)
-                    row.append(cell // cols)
-                    col.append(cell % cols + shift)
-                    value.append(blocks[k][low + lists + j : low + lists + j + 1])
-            row, col, value = (jnp.concatenate(v, axis=1) for v in (row, col, value))
-            n = row.shape[1]
-            at_row = lax.broadcasted_iota(jnp.int32, (rows, n), 0) == row
-            at_col = lax.broadcasted_iota(jnp.int32, (width, n), 0) == col
-            left = jnp.where(at_row, 1.0, 0.0).astype(jnp.bfloat16)
-            part1 = value.astype(jnp.bfloat16).astype(jnp.float32)
-            rest = value - part1
-            part2 = rest.astype(jnp.bfloat16).astype(jnp.float32)
-            weights = (jnp.ones_like(value), part1, part2, rest - part2)
-            right = jnp.concatenate([jnp.where(at_col, w, 0.0).astype(jnp.bfloat16) for w in weights], axis=0)
-            out = lax.dot_general(left, right, (((1,), (1,)), ((), ())), preferred_element_type=jnp.float32)
-            found[0].append(out[:, 0:width])
-            found[1].append(out[:, width : 2 * width] + (out[:, 2 * width : 3 * width] + out[:, 3 * width : 4 * width]))
-        for i in range(2):
-            parts = found[i]
-            if slices * width < LANES:
-                parts = parts + [jnp.zeros((rows, LANES - slices * width), jnp.float32)]
-            maps[2 * k + i] = jnp.concatenate(parts, axis=1)
-    even = (lax.axis_index("gx") & 1) == 0
+    maps = refs[group + 1 : 2 * group + 1]
+    sends = refs[2 * group + 1 :]
+    x = lax.axis_index("gx")
     for i, send in enumerate(sends):
-        low = pl.multiple_of(jnp.where(near_first(even, i), rows - HALO, 0), 8)
+        low = pl.multiple_of(jnp.where(reaches_after(x, i, len(sends)), rows - HALO, 0), 8)
         for k in range(group):
             send[k] = blocks[k][pl.ds(low, HALO)]
-        send[group : 3 * group] = maps[:, pl.ds(low, HALO)]
+            send[group + 2 * k : group + 2 * k + 2] = maps[k][:, pl.ds(low, HALO)]
         send[3 * group : 3 * group + 2] = statics[:, pl.ds(low, HALO)]
 
 
 def main_kernel(dims, *refs):
     slices, rows, group, sides, cut, width = dims
-    blocks, statics, maps = refs[:group], refs[group], refs[group + 1]
-    edges = refs[group + 2 : group + 2 + sides]
-    outs = refs[group + 2 + sides : 2 * group + 2 + sides]
-    state, count, total, fixed, final, misfit, keep, coef = refs[2 * group + 2 + sides :]
+    blocks, statics, maps = refs[:group], refs[group], refs[group + 1 : 2 * group + 1]
+    edges = refs[2 * group + 1 : 2 * group + 1 + sides]
+    outs = refs[2 * group + 1 + sides : 3 * group + 1 + sides]
+    state, count, total, fixed, final, misfit, keep, coef = refs[3 * group + 1 + sides :]
     me = lax.axis_index("tm")
     x = lax.axis_index("gx")
     last_x = lax.axis_size("gx") - 1
-    even = (x & 1) == 0
     full = rows + 2 * HALO
     wrap = (slices - 1) * width
 
@@ -216,14 +234,14 @@
             target[0:HALO] = jnp.zeros((HALO, LANES), jnp.float32)
             target[HALO + rows : full] = jnp.zeros((HALO, LANES), jnp.float32)
         for i, piece in enumerate(pieces):
-            after = near_first(even, i)
+            after = reaches_after(x, i, sides)
             target[pl.ds(pl.multiple_of(jnp.where(after, HALO + rows, 0), 8), HALO)] = piece
 
     for k in range(group):
         pair = source(me, k, group)
         put(state.at[pair], blocks[k][0:rows], [e[k] for e in edges])
-        put(count.at[pair], maps[2 * k], [e[group + 2 * k] for e in edges])
-        put(total.at[pair], maps[2 * k + 1], [e[group + 2 * k + 1] for e in edges])
+        put(count.at[pair], maps[k][0], [e[group + 2 * k] for e in edges])
+        put(total.at[pair], maps[k][1], [e[group + 2 * k + 1] for e in edges])
     for i in range(2):
         put(fixed.at[i], statics[i], [e[3 * group + i] for e in edges])
 
@@ -368,7 +386,7 @@
             target[i * count : (i + 1) * count] = out
 
 
-def per_device(states, bed, background_state, ice_mask, flow_rate, obs_cell, obs_value):
+def step(states, bed, background_state, ice_mask, flow_rate, obs_cell, obs_value):
     slices, rows, cols = states.shape
     group = lax.axis_size("tm")
     cut = cols // group
@@ -387,31 +405,42 @@
         [pltpu.VMEM((rows, cols), jnp.int32), pltpu.VMEM((lists, LANES), jnp.int32), pltpu.SemaphoreType.DMA((slices + 6,))],
         inputs=pltpu.HBM,
     )
-    near = [lax.ppermute(send, "gy", pairs) for send, pairs in zip(sends, swaps_y)]
+    near = swap_all(sends, "gy")
     dims = (slices, rows, cols, lists, group, sides, cut, width)
     *blocks, statics = call(
         functools.partial(pack_kernel, dims),
         [f32(rows + 2 * lists * (1 + sides), LANES)] * group + [f32(2, rows, LANES)],
         [own, *near],
     )
-    blocks = [blocks[0]] + [exchange(blocks[k], "tm", k) for k in range(1, group)]
+    blocks = exchange_all(blocks)
     swaps_x = neighbour_swaps("gx")
-    maps, *sends = call(
-        functools.partial(maps_kernel, dims),
-        [f32(2 * group, rows, LANES)] + [f32(3 * group + 2, HALO, LANES)] * len(swaps_x),
-        [*blocks, statics],
-    )
-    edges = [lax.ppermute(send, "gx", pairs) for send, pairs in zip(sends, swaps_x)]
+    flops = 2 * rows * (lists * LANES * (1 + sides)) * 4 * width
+    maps = []
+    for block in blocks:
+        maps.append(
+            call(
+                functools.partial(maps_kernel, dims),
+                f32(2, rows, LANES),
+                [block],
+                cost=pl.CostEstimate(flops=flops, bytes_accessed=1 << 20, transcendentals=0),
+            )
+        )
+    sends = call(
+        functools.partial(edge_kernel, (rows, group)),
+        [f32(3 * group + 2, HALO, LANES)] * len(swaps_x),
+        [*blocks, statics, *maps],
+    ) if swaps_x else []
+    edges = swap_all(sends, "gx")
     packed = call(
         functools.partial(main_kernel, (slices, rows, group, len(edges), cut, width)),
         [f32(rows * (slices + 1) * cut // LANES, LANES)] * group,
-        [*blocks, statics, maps, *edges],
+        [*blocks, statics, *maps, *edges],
         [vmem(group, full, LANES)] * 3
         + [vmem(3, full, LANES)]
         + [vmem(group, full, LANES)] * 2
         + [vmem(group, STEPS, 4, full, LANES), vmem(4, full, LANES)],
     )
-    pieces = [packed[0]] + [exchange(packed[k], "tm", k) for k in range(1, group)]
+    pieces = exchange_all(packed)
     return tuple(
         call(
             functools.partial(join_kernel, (slices, rows, group, cut)),
@@ -432,7 +461,7 @@
         P("tm", "gx", "gy", None),
     )
     return jax.shard_map(
-        per_device,
+        step,
         mesh=mesh,
         in_specs=placed,
         out_specs=(P("tm", "gx", "gy"), P("gx", "gy")),

time: 35.6 us -> 33.9 us (0.952)
  waiting for transfers between devices: 13.8 us -> 11.1 us
  Pallas kernels: 7.33 us -> 8.32 us
    ppermute x9, waiting for transfers between devices: 13.8 us -> 11.1 us  [the longest x6 5.99 us: exchange(): lax.ppermute(value, axis, [(i, partner(i, number, count)) for i in range(...]
    pallas_call x5 -> x9, Pallas kernels: 7.33 us -> 8.32 us  [call(): pl.pallas_call(kernel, out_shape=out_shape, in_specs=[pl.BlockSpec(memory...]
  transfers between devices with their start and end apart: 9 -> 9, of which waited for: 7 -> 7; matrix products, arithmetic and copies ran while one was open for 0% -> 0% of each run, Pallas kernels for 0% -> 6%
where the time goes in v4:
time: 33.9 us; the launch traced here: 33.7 us
  starting transfers between devices  13.6 us (40%)
  waiting for transfers between devices  11.1 us (33%)
  Pallas kernels  8.32 us (25%)
  between operations  0.68 us (2%)
    ppermute x6, starting transfers between devices, exchange(): lax.ppermute(value, axis, [(i, partner(i, number, count)) for i in range(...  10 us
    pallas_call x9, Pallas kernels, call(): pl.pallas_call(kernel, out_shape=out_shape, in_specs=[pl.BlockSpec(memory...  8.32 us
    ppermute x6, waiting for transfers between devices, exchange(): lax.ppermute(value, axis, [(i, partner(i, number, count)) for i in range(...  5.99 us
    ppermute x3, waiting for transfers between devices, swap_all(): out.append(lax.ppermute(value, axis, pairs))  5.13 us
    ppermute x3, starting transfers between devices, swap_all(): out.append(lax.ppermute(value, axis, pairs))  3.6 us
  transfers between devices with their start and end apart: 9, of which 7 were waited for; matrix products, arithmetic and copies ran while one was open for 0% of the time, Pallas kernels for 6%

profile of v4, /device:TPU:0, one launch (start us, length us, event | category | flops | bytes accessed | tf_op | source)
XLA Modules:
  0.0 33.7 jit_solution(12339344914068018862)
XLA Ops:
  0.6 1.0 %shard_map.86 = (f32[400,128]{1,0:T(8,128)S(1)}, f32[80,128]{1,0:T(8,128)S(1)}) custom-call(f32[2,64,128]{2,1,0:T(8,128)} %refs_0_.1, f32[64,128]{1,0:T(8,128)} %refs_1_.1, f32[64,128]{1,0:T(8,128)} %refs_2_.1, s32[64,128]{1,0:T(8,128)} %refs_3_.1, f32[64,128]{1,0:T(8,128)} %refs_4_.1, s32[8,128]{1,0:T(8,128)} %bitcast.2, f32[8,128]{1,0:T(8,128)} %bitcast.3), custom_call_target="tpu_custom_call" | custom-call | tf_op jit(solution)/shard_map/pallas_call | solution.py:73
  1.7 0.6 %collective-permute-start = (f32[80,128]{1,0:T(8,128)S(1)}, f32[80,128]{1,0:T(8,128)S(1)}, u32[]{:S(2)}, u32[]{:S(2)}) collective-permute-start(f32[80,128]{1,0:T(8,128)S(1)} %get-tuple-element.16), channel_id=1, source_target_pairs={{0,1},{1,0},{2,3},{3,2},{4,5},{5,4},{6,7},{7,6},{8,9},{9,8},{10,11... | collective-permute-start | bytes 122888 | tf_op jit(solution)/shard_map/ppermute | solution.py:67
  2.2 0.9 %collective-permute-done.refs_1_ = f32[80,128]{1,0:T(8,128)S(1)} collective-permute-done((f32[80,128]{1,0:T(8,128)S(1)}, f32[80,128]{1,0:T(8,128)S(1)}, u32[]{:S(2)}, u32[]{:S(2)}) %collective-permute-start) | collective-permute-done | bytes 40992 | tf_op jit(solution)/shard_map/ppermute | solution.py:67
  3.1 0.3 shard_map.87
  3.4 3.0 %collective-permute-start.3 = (f32[96,128]{1,0:T(8,128)S(1)}, f32[96,128]{1,0:T(8,128)S(1)}, u32[]{:S(2)}, u32[]{:S(2)}) collective-permute-start(f32[96,128]{1,0:T(8,128)S(1)} %get-tuple-element.20), channel_id=1, source_target_pairs={{0,8},{8,0},{16,24},{24,16},{1,9},{9,1},{17,25},{25,17},{2,10},{10... | collective-permute-start | bytes 147464 | tf_op jit(solution)/shard_map/ppermute | solution.py:36
  6.4 2.6 %collective-permute-start.2 = (f32[96,128]{1,0:T(8,128)S(1)}, f32[96,128]{1,0:T(8,128)S(1)}, u32[]{:S(2)}, u32[]{:S(2)}) collective-permute-start(f32[96,128]{1,0:T(8,128)S(1)} %get-tuple-element.19), channel_id=1, source_target_pairs={{0,16},{8,24},{16,0},{24,8},{1,17},{9,25},{17,1},{25,9},{2,18},{10... | collective-permute-start | bytes 147464 | tf_op jit(solution)/shard_map/ppermute | solution.py:36
  9.0 0.7 %shard_map.88.refs_5_ = f32[2,64,128]{2,1,0:T(8,128)S(1)} custom-call(f32[96,128]{1,0:T(8,128)S(1)} %get-tuple-element.17.block.refs_0_), custom_call_target="tpu_custom_call" | custom-call | flops 67108864 | bytes 1048576 | tf_op jit(solution)/shard_map/pallas_call | solution.py:73
  9.6 0.0 collective-permute-done.3.block.refs_3_
  9.6 0.6 %shard_map.91.refs_8_ = f32[2,64,128]{2,1,0:T(8,128)S(1)} custom-call(f32[96,128]{1,0:T(8,128)S(1)} %collective-permute-done.3.block.refs_3_), custom_call_target="tpu_custom_call" | custom-call | flops 67108864 | bytes 1048576 | tf_op jit(solution)/shard_map/pallas_call | solution.py:73
  10.3 2.0 %collective-permute-done.2.block.refs_2_ = f32[96,128]{1,0:T(8,128)S(1)} collective-permute-done((f32[96,128]{1,0:T(8,128)S(1)}, f32[96,128]{1,0:T(8,128)S(1)}, u32[]{:S(2)}, u32[]{:S(2)}) %collective-permute-start.2) | collective-permute-done | bytes 49184 | tf_op jit(solution)/shard_map/ppermute | solution.py:36
  12.2 0.7 %shard_map.90.refs_7_ = f32[2,64,128]{2,1,0:T(8,128)S(1)} custom-call(f32[96,128]{1,0:T(8,128)S(1)} %collective-permute-done.2.block.refs_2_), custom_call_target="tpu_custom_call" | custom-call | flops 67108864 | bytes 1048576 | tf_op jit(solution)/shard_map/pallas_call | solution.py:73
  12.9 2.0 %collective-permute-done.1.block.refs_1_ = f32[96,128]{1,0:T(8,128)S(1)} collective-permute-done((f32[96,128]{1,0:T(8,128)S(1)}, f32[96,128]{1,0:T(8,128)S(1)}, u32[]{:S(2)}, u32[]{:S(2)}) %collective-permute-start.1) | collective-permute-done | bytes 49184 | tf_op jit(solution)/shard_map/ppermute | solution.py:36
  14.8 0.6 %shard_map.89.refs_6_ = f32[2,64,128]{2,1,0:T(8,128)S(1)} custom-call(f32[96,128]{1,0:T(8,128)S(1)} %collective-permute-done.1.block.refs_1_), custom_call_target="tpu_custom_call" | custom-call | flops 67108864 | bytes 1048576 | tf_op jit(solution)/shard_map/pallas_call | solution.py:73
  15.5 2.5 %collective-permute-start.4 = (f32[14,16,128]{2,1,0:T(8,128)S(1)}, f32[14,16,128]{2,1,0:T(8,128)S(1)}, u32[]{:S(2)}, u32[]{:S(2)}) collective-permute-start(f32[14,16,128]{2,1,0:T(8,128)S(1)} %get-tuple-element.22), channel_id=1, source_target_pairs={{2,4},{4,2},{6,0},{0,6},{3,5},{5,3},{7,1},{1,7},{10,12},{12,10},{1... | collective-permute-start | bytes 344072 | tf_op jit(solution)/shard_map/ppermute | solution.py:67
  18.0 0.5 %collective-permute-start.5 = (f32[14,16,128]{2,1,0:T(8,128)S(1)}, f32[14,16,128]{2,1,0:T(8,128)S(1)}, u32[]{:S(2)}, u32[]{:S(2)}) collective-permute-start(f32[14,16,128]{2,1,0:T(8,128)S(1)} %get-tuple-element.23), channel_id=1, source_target_pairs={{0,2},{2,0},{4,6},{6,4},{1,3},{3,1},{5,7},{7,5},{8,10},{10,8},{12,... | collective-permute-start | bytes 344072 | tf_op jit(solution)/shard_map/ppermute | solution.py:67
  18.6 2.7 %collective-permute-done.4.refs_9_ = f32[14,16,128]{2,1,0:T(8,128)S(1)} collective-permute-done((f32[14,16,128]{2,1,0:T(8,128)S(1)}, f32[14,16,128]{2,1,0:T(8,128)S(1)}, u32[]{:S(2)}, u32[]{:S(2)}) %collective-permute-start.4) | collective-permute-done | bytes 114720 | tf_op jit(solution)/shard_map/ppermute | solution.py:67
  21.3 1.5 %collective-permute-done.5.refs_10_ = f32[14,16,128]{2,1,0:T(8,128)S(1)} collective-permute-done((f32[14,16,128]{2,1,0:T(8,128)S(1)}, f32[14,16,128]{2,1,0:T(8,128)S(1)}, u32[]{:S(2)}, u32[]{:S(2)}) %collective-permute-start.5) | collective-permute-done | bytes 114720 | tf_op jit(solution)/shard_map/ppermute | solution.py:67
  22.8 3.6 %shard_map.93 = (f32[48,128]{1,0:T(8,128)S(1)}, f32[48,128]{1,0:T(8,128)S(1)}, f32[48,128]{1,0:T(8,128)S(1)}, f32[48,128]{1,0:T(8,128)S(1)}) custom-call(f32[96,128]{1,0:T(8,128)S(1)} %get-tuple-element.17.block.refs_0_, f32[96,128]{1,0:T(8,128)S(1)} %collective-permute-done.1.block.refs_1_, f32[96,128]{1,0:T(8,128)S(1)} %collective-permute-done.2.block.refs_2_, ...), custom_call_target="tpu_custom_call" | custom-call | tf_op jit(solution)/shard_map/pallas_call | solution.py:73
  26.4 1.8 %collective-permute-start.6 = (f32[48,128]{1,0:T(8,128)S(1)}, f32[48,128]{1,0:T(8,128)S(1)}, u32[]{:S(2)}, u32[]{:S(2)}) collective-permute-start(f32[48,128]{1,0:T(8,128)S(1)} %get-tuple-element.25), channel_id=1, source_target_pairs={{0,24},{8,16},{16,8},{24,0},{1,25},{9,17},{17,9},{25,1},{2,26},{10... | collective-permute-start | bytes 73736 | tf_op jit(solution)/shard_map/ppermute | solution.py:36
  28.2 2.7 %collective-permute-start.8 = (f32[48,128]{1,0:T(8,128)S(1)}, f32[48,128]{1,0:T(8,128)S(1)}, u32[]{:S(2)}, u32[]{:S(2)}) collective-permute-start(f32[48,128]{1,0:T(8,128)S(1)} %get-tuple-element.27), channel_id=1, source_target_pairs={{0,8},{8,0},{16,24},{24,16},{1,9},{9,1},{17,25},{25,17},{2,10},{10... | collective-permute-start | bytes 73736 | tf_op jit(solution)/shard_map/ppermute | solution.py:36
  30.8 1.2 %collective-permute-done.6.refs_1_ = f32[48,128]{1,0:T(8,128)S(1)} collective-permute-done((f32[48,128]{1,0:T(8,128)S(1)}, f32[48,128]{1,0:T(8,128)S(1)}, u32[]{:S(2)}, u32[]{:S(2)}) %collective-permute-start.6) | collective-permute-done | bytes 24608 | tf_op jit(solution)/shard_map/ppermute | solution.py:36
  32.1 0.8 %collective-permute-done.7.refs_2_ = f32[48,128]{1,0:T(8,128)S(1)} collective-permute-done((f32[48,128]{1,0:T(8,128)S(1)}, f32[48,128]{1,0:T(8,128)S(1)}, u32[]{:S(2)}, u32[]{:S(2)}) %collective-permute-start.7) | collective-permute-done | bytes 24608 | tf_op jit(solution)/shard_map/ppermute | solution.py:36
  32.9 0.0 collective-permute-done.8.refs_3_
  32.9 0.8 %shard_map.94 = (f32[2,64,128]{2,1,0:T(8,128)}, f32[64,128]{1,0:T(8,128)}) custom-call(f32[48,128]{1,0:T(8,128)S(1)} %get-tuple-element.24.refs_0_, f32[48,128]{1,0:T(8,128)S(1)} %collective-permute-done.6.refs_1_, f32[48,128]{1,0:T(8,128)S(1)} %collective-permute-done.7.refs_2_, f32[48,128]{1,0:T(8,128)S(1)} %collective-permute-done.8.refs_3_), custom_call_target="tpu_custom_call" | custom-call | tf_op jit(solution)/shard_map/pallas_call | solution.py:73
  (3 shorter events, 0.0 us)
Async XLA Ops:
  1.7 1.4 %collective-permute-start = (f32[80,128]{1,0:T(8,128)S(1)}, f32[80,128]{1,0:T(8,128)S(1)}, u32[]{:S(2)}, u32[]{:S(2)}) collective-permute-start(f32[80,128]{1,0:T(8,128)S(1)} %get-tuple-element.16), channel_id=1, source_target_pairs={{0,1},{1,0},{2,3},{3,2},{4,5},{5,4},{6,7},{7,6},{8,9},{9,8},{10,11... | collective-permute-start | bytes 122888 | tf_op jit(solution)/shard_map/ppermute | solution.py:67
  3.4 6.2 %collective-permute-start.3 = (f32[96,128]{1,0:T(8,128)S(1)}, f32[96,128]{1,0:T(8,128)S(1)}, u32[]{:S(2)}, u32[]{:S(2)}) collective-permute-start(f32[96,128]{1,0:T(8,128)S(1)} %get-tuple-element.20), channel_id=1, source_target_pairs={{0,8},{8,0},{16,24},{24,16},{1,9},{9,1},{17,25},{25,17},{2,10},{10... | collective-permute-start | bytes 147464 | tf_op jit(solution)/shard_map/ppermute | solution.py:36
  6.4 5.9 %collective-permute-start.2 = (f32[96,128]{1,0:T(8,128)S(1)}, f32[96,128]{1,0:T(8,128)S(1)}, u32[]{:S(2)}, u32[]{:S(2)}) collective-permute-start(f32[96,128]{1,0:T(8,128)S(1)} %get-tuple-element.19), channel_id=1, source_target_pairs={{0,16},{8,24},{16,0},{24,8},{1,17},{9,25},{17,1},{25,9},{2,18},{10... | collective-permute-start | bytes 147464 | tf_op jit(solution)/shard_map/ppermute | solution.py:36
  9.0 5.9 %collective-permute-start.1 = (f32[96,128]{1,0:T(8,128)S(1)}, f32[96,128]{1,0:T(8,128)S(1)}, u32[]{:S(2)}, u32[]{:S(2)}) collective-permute-start(f32[96,128]{1,0:T(8,128)S(1)} %get-tuple-element.18), channel_id=1, source_target_pairs={{0,24},{8,16},{16,8},{24,0},{1,25},{9,17},{17,9},{25,1},{2,26},{10... | collective-permute-start | bytes 147464 | tf_op jit(solution)/shard_map/ppermute | solution.py:36
  15.5 5.8 %collective-permute-start.4 = (f32[14,16,128]{2,1,0:T(8,128)S(1)}, f32[14,16,128]{2,1,0:T(8,128)S(1)}, u32[]{:S(2)}, u32[]{:S(2)}) collective-permute-start(f32[14,16,128]{2,1,0:T(8,128)S(1)} %get-tuple-element.22), channel_id=1, source_target_pairs={{2,4},{4,2},{6,0},{0,6},{3,5},{5,3},{7,1},{1,7},{10,12},{12,10},{1... | collective-permute-start | bytes 344072 | tf_op jit(solution)/shard_map/ppermute | solution.py:67
  18.0 4.8 %collective-permute-start.5 = (f32[14,16,128]{2,1,0:T(8,128)S(1)}, f32[14,16,128]{2,1,0:T(8,128)S(1)}, u32[]{:S(2)}, u32[]{:S(2)}) collective-permute-start(f32[14,16,128]{2,1,0:T(8,128)S(1)} %get-tuple-element.23), channel_id=1, source_target_pairs={{0,2},{2,0},{4,6},{6,4},{1,3},{3,1},{5,7},{7,5},{8,10},{10,8},{12,... | collective-permute-start | bytes 344072 | tf_op jit(solution)/shard_map/ppermute | solution.py:67
  26.4 5.7 %collective-permute-start.6 = (f32[48,128]{1,0:T(8,128)S(1)}, f32[48,128]{1,0:T(8,128)S(1)}, u32[]{:S(2)}, u32[]{:S(2)}) collective-permute-start(f32[48,128]{1,0:T(8,128)S(1)} %get-tuple-element.25), channel_id=1, source_target_pairs={{0,24},{8,16},{16,8},{24,0},{1,25},{9,17},{17,9},{25,1},{2,26},{10... | collective-permute-start | bytes 73736 | tf_op jit(solution)/shard_map/ppermute | solution.py:36
  28.2 4.7 %collective-permute-start.7 = (f32[48,128]{1,0:T(8,128)S(1)}, f32[48,128]{1,0:T(8,128)S(1)}, u32[]{:S(2)}, u32[]{:S(2)}) collective-permute-start(f32[48,128]{1,0:T(8,128)S(1)} %get-tuple-element.26), channel_id=1, source_target_pairs={{0,16},{8,24},{16,0},{24,8},{1,17},{9,25},{17,1},{25,9},{2,18},{10... | collective-permute-start | bytes 73736 | tf_op jit(solution)/shard_map/ppermute | solution.py:36
  28.2 4.7 %collective-permute-start.8 = (f32[48,128]{1,0:T(8,128)S(1)}, f32[48,128]{1,0:T(8,128)S(1)}, u32[]{:S(2)}, u32[]{:S(2)}) collective-permute-start(f32[48,128]{1,0:T(8,128)S(1)} %get-tuple-element.27), channel_id=1, source_target_pairs={{0,8},{8,0},{16,24},{24,16},{1,9},{9,1},{17,25},{25,17},{2,10},{10... | collective-permute-start | bytes 73736 | tf_op jit(solution)/shard_map/ppermute | solution.py:36

commit v5 on v4

--- a/solution.py
+++ b/solution.py
@@ -11,6 +11,7 @@
 STEPS = 4
 OUTER = 2
 HALO = 2 * STEPS * OUTER
+REACH = HALO - STEPS
 LANES = 128
 
 bed_rate = 0.1
@@ -68,7 +69,7 @@
     return out
 
 
-def call(kernel, out_shape, operands, scratch=(), inputs=pltpu.VMEM, cost=None):
+def call(kernel, out_shape, operands, scratch=(), inputs=pltpu.VMEM):
     spec = pl.BlockSpec(memory_space=pltpu.VMEM)
     return pl.pallas_call(
         kernel,
@@ -76,7 +77,6 @@
         in_specs=[pl.BlockSpec(memory_space=inputs)] * len(operands),
         out_specs=jax.tree.map(lambda _: spec, out_shape),
         scratch_shapes=list(scratch),
-        cost_estimate=cost,
         compiler_params=pltpu.CompilerParams(vmem_limit_bytes=16 << 20),
     )(*operands)
 
@@ -164,86 +164,117 @@
     statics[1] = packed([slices + 2, slices + 3], start)
 
 
-def maps_kernel(dims, block, maps):
+def maps_kernel(dims, *refs):
     slices, rows, cols, lists, _, sides, cut, width = dims
+    blocks, maps = refs[: len(refs) // 2], refs[len(refs) // 2 :]
     start = lax.axis_index("tm") * cut - HALO
     y = lax.axis_index("gy")
     each = lists // slices
-    found = [[], []]
-    for s in range(slices):
-        row, col, value = [], [], []
+    rounded = lambda v: v.astype(jnp.bfloat16)
+    n = lists // slices * LANES * (1 + sides)
+    narrow = lambda v: v.astype(jnp.int16)
+    down = narrow(lax.broadcasted_iota(jnp.int32, (rows, n), 0))
+    across = narrow(lax.broadcasted_iota(jnp.int32, (width, n), 0))
+
+    def chosen(where, weight):
+        weight = rounded(jnp.broadcast_to(weight, (1, n)))
+        return jnp.where(where, jnp.broadcast_to(weight, where.shape), jnp.zeros(where.shape, jnp.bfloat16))
+
+    for block, target in zip(blocks, maps):
+        row, col, parts = [], [], []
         for side in range(1 + sides):
-            low = rows + 2 * lists * side + each * s
+            low = rows + 2 * lists * side
             shift = -start
             if side:
                 shift = shift + jnp.where(reaches_after(y, side - 1, sides), cols, -cols)
-            for j in range(each):
-                cell = block[low + j : low + j + 1].astype(jnp.int32)
+            cell = block[low : low + lists].astype(jnp.int32)
+            value = block[low + lists : low + 2 * lists]
+            part1 = rounded(value).astype(jnp.float32)
+            part2 = rounded(value - part1).astype(jnp.float32)
+            if cols & (cols - 1) == 0:
+                row.append(cell >> (cols.bit_length() - 1))
+                col.append((cell & (cols - 1)) + shift)
+            else:
                 row.append(cell // cols)
                 col.append(cell % cols + shift)
-                value.append(block[low + lists + j : low + lists + j + 1])
-        row, col, value = (jnp.concatenate(v, axis=1) for v in (row, col, value))
-        n = row.shape[1]
-        at_row = lax.broadcasted_iota(jnp.int32, (rows, n), 0) == row
-        at_col = lax.broadcasted_iota(jnp.int32, (width, n), 0) == col
-        left = jnp.where(at_row, 1.0, 0.0).astype(jnp.bfloat16)
-        part1 = value.astype(jnp.bfloat16).astype(jnp.float32)
-        rest = value - part1
-        part2 = rest.astype(jnp.bfloat16).astype(jnp.float32)
-        weights = (jnp.ones_like(value), part1, part2, rest - part2)
-        right = jnp.concatenate([jnp.where(at_col, w, 0.0).astype(jnp.bfloat16) for w in weights], axis=0)
-        out = lax.dot_general(left, right, (((1,), (1,)), ((), ())), preferred_element_type=jnp.float32)
-        found[0].append(out[:, 0:width])
-        found[1].append(out[:, width : 2 * width] + (out[:, 2 * width : 3 * width] + out[:, 3 * width : 4 * width]))
-    for i in range(2):
-        parts = found[i]
-        if slices * width < LANES:
-            parts = parts + [jnp.zeros((rows, LANES - slices * width), jnp.float32)]
-        maps[i] = jnp.concatenate(parts, axis=1)
+            parts.append((part1, part2, value - part1 - part2))
+
+        def line(arrays, s):
+            return jnp.concatenate([v[j : j + 1] for v in arrays for j in range(s * each, (s + 1) * each)], axis=1)
+
+        found = [[], []]
+        for s in range(slices):
+            at_row = down == narrow(line(row, s))
+            at_col = across == narrow(line(col, s))
+            left = chosen(at_row, 1.0)
+            weights = [1.0] + [line([p[i] for p in parts], s) for i in range(3)]
+            right = jnp.concatenate([chosen(at_col, w) for w in weights], axis=0)
+            out = lax.dot_general(left, right, (((1,), (1,)), ((), ())), preferred_element_type=jnp.float32)
+            found[0].append(out[:, 0:width])
+            found[1].append(
+                out[:, width : 2 * width] + (out[:, 2 * width : 3 * width] + out[:, 3 * width : 4 * width])
+            )
+        for i in range(2):
+            pieces = found[i]
+            if slices * width < LANES:
+                pieces = pieces + [jnp.zeros((rows, LANES - slices * width), jnp.float32)]
+            target[i] = jnp.concatenate(pieces, axis=1)
 
 
 def edge_kernel(dims, *refs):
-    rows, group = dims
-    blocks, statics = refs[:group], refs[group]
-    maps = refs[group + 1 : 2 * group + 1]
-    sends = refs[2 * group + 1 :]
+    rows, count, swaps = dims
+    blocks, maps = refs[:count], refs[count : 2 * count]
+    statics, sends = refs[2 * count : -swaps], refs[-swaps:]
     x = lax.axis_index("gx")
     for i, send in enumerate(sends):
-        low = pl.multiple_of(jnp.where(reaches_after(x, i, len(sends)), rows - HALO, 0), 8)
-        for k in range(group):
-            send[k] = blocks[k][pl.ds(low, HALO)]
-            send[group + 2 * k : group + 2 * k + 2] = maps[k][:, pl.ds(low, HALO)]
-        send[3 * group : 3 * group + 2] = statics[:, pl.ds(low, HALO)]
+        lower = reaches_after(x, i, swaps)
+        low = pl.multiple_of(jnp.where(lower, rows - HALO, 0), 8)
+        for k in range(count):
+            base = k * (HALO + 2 * REACH)
+            send[base : base + HALO] = blocks[k][pl.ds(low, HALO)]
+            for j in range(2):
+                first = base + HALO + j * REACH
+                send[first : first + REACH] = jnp.where(lower, maps[k][j, rows - REACH : rows], maps[k][j, 0:REACH])
+        for ref in statics:
+            for j in range(2):
+                first = count * (HALO + 2 * REACH) + j * HALO
+                send[first : first + HALO] = ref[j, pl.ds(low, HALO)]
 
 
 def main_kernel(dims, *refs):
     slices, rows, group, sides, cut, width = dims
     blocks, statics, maps = refs[:group], refs[group], refs[group + 1 : 2 * group + 1]
-    edges = refs[2 * group + 1 : 2 * group + 1 + sides]
-    outs = refs[2 * group + 1 + sides : 3 * group + 1 + sides]
-    state, count, total, fixed, final, misfit, keep, coef = refs[3 * group + 1 + sides :]
+    refs = refs[2 * group + 1 :]
+    early, late, outs = refs[:sides], refs[sides : 2 * sides], refs[2 * sides : 2 * sides + group]
+    state, count, total, fixed, final, misfit, keep, coef, slide = refs[2 * sides + group :]
     me = lax.axis_index("tm")
     x = lax.axis_index("gx")
     last_x = lax.axis_size("gx") - 1
     full = rows + 2 * HALO
     wrap = (slices - 1) * width
 
-    def put(target, main, pieces):
+    def put(target, main, pieces, reach):
+        after = reaches_after(x, 0, sides) if sides else None
+        zero = jnp.zeros((reach, LANES), jnp.float32)
+        one, two = (list(pieces) + [zero, zero])[:2]
+        if reach < HALO:
+            target[0:8] = jnp.zeros((8, LANES), jnp.float32)
+            target[full - 8 : full] = jnp.zeros((8, LANES), jnp.float32)
+        target[HALO - reach : HALO] = jnp.where(after, two, one) if sides else zero
         target[HALO : HALO + rows] = main
-        if sides < 2:
-            target[0:HALO] = jnp.zeros((HALO, LANES), jnp.float32)
-            target[HALO + rows : full] = jnp.zeros((HALO, LANES), jnp.float32)
-        for i, piece in enumerate(pieces):
-            after = reaches_after(x, i, sides)
-            target[pl.ds(pl.multiple_of(jnp.where(after, HALO + rows, 0), 8), HALO)] = piece
-
+        target[HALO + rows : HALO + rows + reach] = jnp.where(after, one, two) if sides else zero
+
+    stride = HALO + 2 * REACH
     for k in range(group):
         pair = source(me, k, group)
-        put(state.at[pair], blocks[k][0:rows], [e[k] for e in edges])
-        put(count.at[pair], maps[k][0], [e[group + 2 * k] for e in edges])
-        put(total.at[pair], maps[k][1], [e[group + 2 * k + 1] for e in edges])
-    for i in range(2):
-        put(fixed.at[i], statics[i], [e[3 * group + i] for e in edges])
+        edges, base = (late, (k - 1) * stride) if k else (early, 0)
+        put(state.at[pair], blocks[k][0:rows], [e[base : base + HALO] for e in edges], HALO)
+        for j, target in enumerate((count, total)):
+            first = base + HALO + j * REACH
+            put(target.at[pair], maps[k][j], [e[first : first + REACH] for e in edges], REACH)
+    for j in range(2):
+        first = stride + j * HALO
+        put(fixed.at[j], statics[j], [e[first : first + HALO] for e in early], HALO)
 
     row = lax.broadcasted_iota(jnp.int32, (full, LANES), 0)
     lane = lane_of((full, LANES))
@@ -251,7 +282,8 @@
     up = lambda v: pltpu.roll(v, 1, 0)
     right = lambda v: pltpu.roll(v, LANES - 1, 1)
     left = lambda v: pltpu.roll(v, 1, 1)
-    moves = ((down, up), (right, left))
+    slide[:, :, 0:8] = jnp.zeros((2, group, 8, LANES), jnp.float32)
+    slide[:, :, full + 8 : full + 16] = jnp.zeros((2, group, 8, LANES), jnp.float32)
 
     def spread(value):
         out = value
@@ -281,6 +313,16 @@
         size = high - low
         span = pl.ds(low, size)
         here = lane[:size]
+
+        def slid(number, values, by):
+            for p in pairs:
+                slide[number, p, 8 + low : 8 + high] = values[p]
+            return [slide[number, p, 8 + low + by : 8 + high + by] for p in pairs]
+
+        moves = (
+            (lambda v: slid(0, v, 1), lambda v: slid(1, v, -1)),
+            (lambda v: [right(w) for w in v], lambda v: [left(w) for w in v]),
+        )
         bed = fixed[2, span]
         coef[0, span] = jnp.where(row[:size] == size - 1, 0.0, coef[0, span])
         coef[2, span] = down(bed) - bed
@@ -290,7 +332,7 @@
         for step in range(STEPS):
             fluxes = []
             for d, (ahead, behind) in enumerate(moves):
-                there = [ahead(v) for v in thick]
+                there = ahead(thick)
                 flux = []
                 for p in pairs:
                     both = thick[p] + there[p]
@@ -301,7 +343,7 @@
                     keep[p, step, 2 * d, span] = half * scaled
                     keep[p, step, 2 * d + 1, span] = by_mean
                     flux.append(half * by_mean)
-                fluxes.append((flux, [behind(v) for v in flux]))
+                fluxes.append((flux, behind(flux)))
             thick = [
                 thick[p] + ((fluxes[0][0][p] - fluxes[0][1][p]) + (fluxes[1][0][p] - fluxes[1][1][p])) for p in pairs
             ]
@@ -324,7 +366,7 @@
         for step in reversed(range(STEPS)):
             parts = []
             for d, (ahead, behind) in enumerate(moves):
-                jump = [v - ahead(v) for v in pull]
+                jump = [v - w for v, w in zip(pull, ahead(pull))]
                 own, passed = [], []
                 for p in pairs:
                     by_slope = keep[p, step, 2 * d, span] * jump[p]
@@ -332,7 +374,7 @@
                     sums[d] = by_slope if sums[d] is None else sums[d] + by_slope
                     own.append(by_mean - by_slope)
                     passed.append(by_mean + by_slope)
-                parts.append((own, [behind(v) for v in passed]))
+                parts.append((own, behind(passed)))
             pull = [pull[p] + ((parts[0][0][p] + parts[0][1][p]) + (parts[1][0][p] + parts[1][1][p])) for p in pairs]
         for p in pairs:
             state[p, span] = state[p, span] - state_rate * (misfit[p, span] + pull[p])
@@ -413,32 +455,36 @@
         [own, *near],
     )
     blocks = exchange_all(blocks)
-    swaps_x = neighbour_swaps("gx")
-    flops = 2 * rows * (lists * LANES * (1 + sides)) * 4 * width
     maps = []
-    for block in blocks:
-        maps.append(
-            call(
-                functools.partial(maps_kernel, dims),
-                f32(2, rows, LANES),
-                [block],
-                cost=pl.CostEstimate(flops=flops, bytes_accessed=1 << 20, transcendentals=0),
+    for part in (blocks[:1], blocks[1:]):
+        if part:
+            maps += call(functools.partial(maps_kernel, dims), [f32(2, rows, LANES)] * len(part), part)
+    early, late = [], []
+    swaps = len(neighbour_swaps("gx"))
+    stride = HALO + 2 * REACH
+    if swaps:
+        sends = call(
+            functools.partial(edge_kernel, (rows, 1, swaps)),
+            [f32(stride + 2 * HALO, LANES)] * swaps,
+            [blocks[0], maps[0], statics],
+        )
+        early = swap_all(sends, "gx")
+        late = early
+        if group > 1:
+            sends = call(
+                functools.partial(edge_kernel, (rows, group - 1, swaps)),
+                [f32((group - 1) * stride, LANES)] * swaps,
+                [*blocks[1:], *maps[1:]],
             )
-        )
-    sends = call(
-        functools.partial(edge_kernel, (rows, group)),
-        [f32(3 * group + 2, HALO, LANES)] * len(swaps_x),
-        [*blocks, statics, *maps],
-    ) if swaps_x else []
-    edges = swap_all(sends, "gx")
+            late = swap_all(sends, "gx")
     packed = call(
-        functools.partial(main_kernel, (slices, rows, group, len(edges), cut, width)),
+        functools.partial(main_kernel, (slices, rows, group, swaps, cut, width)),
         [f32(rows * (slices + 1) * cut // LANES, LANES)] * group,
-        [*blocks, statics, *maps, *edges],
+        [*blocks, statics, *maps, *early, *late],
         [vmem(group, full, LANES)] * 3
         + [vmem(3, full, LANES)]
         + [vmem(group, full, LANES)] * 2
-        + [vmem(group, STEPS, 4, full, LANES), vmem(4, full, LANES)],
+        + [vmem(group, STEPS, 4, full, LANES), vmem(4, full, LANES), vmem(2, group, full + 16, LANES)],
     )
     pieces = exchange_all(packed)
     return tuple(

time: 33.9 us -> 35.6 us (1.050)
  starting transfers between devices: 13.6 us -> 15.7 us
  Pallas kernels: 8.32 us -> 7.72 us
    ppermute x3 -> x5, starting transfers between devices: 3.6 us -> 5.64 us  [swap_all(): out.append(lax.ppermute(value, axis, pairs))]
    ppermute x6, waiting for transfers between devices: 5.99 us -> 6.97 us  [exchange(): lax.ppermute(value, axis, [(i, partner(i, number, count)) for i in range(...]
    ppermute x3 -> x5, waiting for transfers between devices: 5.13 us -> 4.3 us  [swap_all(): out.append(lax.ppermute(value, axis, pairs))]
    pallas_call x9 -> x8, Pallas kernels: 8.32 us -> 7.72 us  [call(): pl.pallas_call(kernel, out_shape=out_shape, in_specs=[pl.BlockSpec(memory...]
  transfers between devices with their start and end apart: 9 -> 11, of which waited for: 7 -> 7; matrix products, arithmetic and copies ran while one was open for 0% -> 0% of each run, Pallas kernels for 6% -> 2%
where the time goes in v5:
time: 35.6 us; the launch traced here: 35.4 us
  starting transfers between devices  15.7 us (44%)
  waiting for transfers between devices  11.3 us (32%)
  Pallas kernels  7.72 us (22%)
  between operations  0.69 us (2%)
    ppermute x6, starting transfers between devices, exchange(): lax.ppermute(value, axis, [(i, partner(i, number, count)) for i in range(...  10.1 us
    pallas_call x8, Pallas kernels, call(): pl.pallas_call(kernel, out_shape=out_shape, in_specs=[pl.BlockSpec(memory...  7.72 us
    ppermute x6, waiting for transfers between devices, exchange(): lax.ppermute(value, axis, [(i, partner(i, number, count)) for i in range(...  6.97 us
    ppermute x5, starting transfers between devices, swap_all(): out.append(lax.ppermute(value, axis, pairs))  5.64 us
    ppermute x5, waiting for transfers between devices, swap_all(): out.append(lax.ppermute(value, axis, pairs))  4.3 us
  transfers between devices with their start and end apart: 11, of which 7 were waited for; matrix products, arithmetic and copies ran while one was open for 0% of the time, Pallas kernels for 2%

profile of v5, /device:TPU:0, one launch (start us, length us, event | category | flops | bytes accessed | tf_op | source)
XLA Modules:
  0.0 35.4 jit_solution(13590631912497201715)
XLA Ops:
  0.6 1.0 %shard_map.86 = (f32[400,128]{1,0:T(8,128)S(1)}, f32[80,128]{1,0:T(8,128)S(1)}) custom-call(f32[2,64,128]{2,1,0:T(8,128)} %refs_0_.1, f32[64,128]{1,0:T(8,128)} %refs_1_.1, f32[64,128]{1,0:T(8,128)} %refs_2_.1, s32[64,128]{1,0:T(8,128)} %refs_3_.1, f32[64,128]{1,0:T(8,128)} %refs_4_.1, s32[8,128]{1,0:T(8,128)} %bitcast.2, f32[8,128]{1,0:T(8,128)} %bitcast.3), custom_call_target="tpu_custom_call" | custom-call | tf_op jit(solution)/shard_map/pallas_call | solution.py:74
  1.7 0.6 %collective-permute-start = (f32[80,128]{1,0:T(8,128)S(1)}, f32[80,128]{1,0:T(8,128)S(1)}, u32[]{:S(2)}, u32[]{:S(2)}) collective-permute-start(f32[80,128]{1,0:T(8,128)S(1)} %get-tuple-element.21), channel_id=1, source_target_pairs={{0,1},{1,0},{2,3},{3,2},{4,5},{5,4},{6,7},{7,6},{8,9},{9,8},{10,11... | collective-permute-start | bytes 122888 | tf_op jit(solution)/shard_map/ppermute | solution.py:68
  2.2 0.9 %collective-permute-done.refs_1_ = f32[80,128]{1,0:T(8,128)S(1)} collective-permute-done((f32[80,128]{1,0:T(8,128)S(1)}, f32[80,128]{1,0:T(8,128)S(1)}, u32[]{:S(2)}, u32[]{:S(2)}) %collective-permute-start) | collective-permute-done | bytes 40992 | tf_op jit(solution)/shard_map/ppermute | solution.py:68
  3.1 0.3 shard_map.87
  3.4 5.0 %collective-permute-start.1 = (f32[96,128]{1,0:T(8,128)S(1)}, f32[96,128]{1,0:T(8,128)S(1)}, u32[]{:S(2)}, u32[]{:S(2)}) collective-permute-start(f32[96,128]{1,0:T(8,128)S(1)} %get-tuple-element.23), channel_id=1, source_target_pairs={{0,24},{8,16},{16,8},{24,0},{1,25},{9,17},{17,9},{25,1},{2,26},{10... | collective-permute-start | bytes 147464 | tf_op jit(solution)/shard_map/ppermute | solution.py:37
  8.4 0.0 collective-permute-start.2
  8.4 0.6 %collective-permute-start.3 = (f32[96,128]{1,0:T(8,128)S(1)}, f32[96,128]{1,0:T(8,128)S(1)}, u32[]{:S(2)}, u32[]{:S(2)}) collective-permute-start(f32[96,128]{1,0:T(8,128)S(1)} %get-tuple-element.25), channel_id=1, source_target_pairs={{0,8},{8,0},{16,24},{24,16},{1,9},{9,1},{17,25},{25,17},{2,10},{10... | collective-permute-start | bytes 147464 | tf_op jit(solution)/shard_map/ppermute | solution.py:37
  9.0 1.5 %collective-permute-done.1.refs_0_.refs_1_ = f32[96,128]{1,0:T(8,128)S(1)} collective-permute-done((f32[96,128]{1,0:T(8,128)S(1)}, f32[96,128]{1,0:T(8,128)S(1)}, u32[]{:S(2)}, u32[]{:S(2)}) %collective-permute-start.1) | collective-permute-done | bytes 49184 | tf_op jit(solution)/shard_map/ppermute | solution.py:37
  10.6 2.8 %collective-permute-done.2.refs_1_.refs_2_ = f32[96,128]{1,0:T(8,128)S(1)} collective-permute-done((f32[96,128]{1,0:T(8,128)S(1)}, f32[96,128]{1,0:T(8,128)S(1)}, u32[]{:S(2)}, u32[]{:S(2)}) %collective-permute-start.2) | collective-permute-done | bytes 49184 | tf_op jit(solution)/shard_map/ppermute | solution.py:37
  13.4 1.3 %shard_map.89 = (f32[2,64,128]{2,1,0:T(8,128)S(1)}, f32[2,64,128]{2,1,0:T(8,128)S(1)}, f32[2,64,128]{2,1,0:T(8,128)S(1)}) custom-call(f32[96,128]{1,0:T(8,128)S(1)} %collective-permute-done.1.refs_0_.refs_1_, f32[96,128]{1,0:T(8,128)S(1)} %collective-permute-done.2.refs_1_.refs_2_, f32[96,128]{1,0:T(8,128)S(1)} %collective-permute-done.3.refs_2_.refs_3_), custom_call_target="tpu_custom_call" | custom-call | tf_op jit(solution)/shard_map/pallas_call | solution.py:74
  14.7 2.5 %collective-permute-start.6 = (f32[120,128]{1,0:T(8,128)S(1)}, f32[120,128]{1,0:T(8,128)S(1)}, u32[]{:S(2)}, u32[]{:S(2)}) collective-permute-start(f32[120,128]{1,0:T(8,128)S(1)} %get-tuple-element.32), channel_id=1, source_target_pairs={{2,4},{4,2},{6,0},{0,6},{3,5},{5,3},{7,1},{1,7},{10,12},{12,10},{1... | collective-permute-start | bytes 184328 | tf_op jit(solution)/shard_map/ppermute | solution.py:68
  17.2 0.5 %collective-permute-start.7 = (f32[120,128]{1,0:T(8,128)S(1)}, f32[120,128]{1,0:T(8,128)S(1)}, u32[]{:S(2)}, u32[]{:S(2)}) collective-permute-start(f32[120,128]{1,0:T(8,128)S(1)} %get-tuple-element.33), channel_id=1, source_target_pairs={{0,2},{2,0},{4,6},{6,4},{1,3},{3,1},{5,7},{7,5},{8,10},{10,8},{12,... | collective-permute-start | bytes 184328 | tf_op jit(solution)/shard_map/ppermute | solution.py:68
  17.8 0.7 %shard_map.88.refs_1_.refs_5_ = f32[2,64,128]{2,1,0:T(8,128)S(1)} custom-call(f32[96,128]{1,0:T(8,128)S(1)} %get-tuple-element.22.refs_0_), custom_call_target="tpu_custom_call" | custom-call | tf_op jit(solution)/shard_map/pallas_call | solution.py:74
  18.5 1.5 %collective-permute-start.4 = (f32[72,128]{1,0:T(8,128)S(1)}, f32[72,128]{1,0:T(8,128)S(1)}, u32[]{:S(2)}, u32[]{:S(2)}) collective-permute-start(f32[72,128]{1,0:T(8,128)S(1)} %get-tuple-element.30), channel_id=1, source_target_pairs={{2,4},{4,2},{6,0},{0,6},{3,5},{5,3},{7,1},{1,7},{10,12},{12,10},{1... | collective-permute-start | bytes 110600 | tf_op jit(solution)/shard_map/ppermute | solution.py:68
  20.0 0.5 %collective-permute-start.5 = (f32[72,128]{1,0:T(8,128)S(1)}, f32[72,128]{1,0:T(8,128)S(1)}, u32[]{:S(2)}, u32[]{:S(2)}) collective-permute-start(f32[72,128]{1,0:T(8,128)S(1)} %get-tuple-element.31), channel_id=1, source_target_pairs={{0,2},{2,0},{4,6},{6,4},{1,3},{3,1},{5,7},{7,5},{8,10},{10,8},{12,... | collective-permute-start | bytes 110600 | tf_op jit(solution)/shard_map/ppermute | solution.py:68
  20.5 2.9 %collective-permute-done.4.refs_9_ = f32[72,128]{1,0:T(8,128)S(1)} collective-permute-done((f32[72,128]{1,0:T(8,128)S(1)}, f32[72,128]{1,0:T(8,128)S(1)}, u32[]{:S(2)}, u32[]{:S(2)}) %collective-permute-start.4) | collective-permute-done | bytes 36896 | tf_op jit(solution)/shard_map/ppermute | solution.py:68
  23.4 0.5 %collective-permute-done.5.refs_10_ = f32[72,128]{1,0:T(8,128)S(1)} collective-permute-done((f32[72,128]{1,0:T(8,128)S(1)}, f32[72,128]{1,0:T(8,128)S(1)}, u32[]{:S(2)}, u32[]{:S(2)}) %collective-permute-start.5) | collective-permute-done | bytes 36896 | tf_op jit(solution)/shard_map/ppermute | solution.py:68
  23.9 3.6 %shard_map.92 = (f32[48,128]{1,0:T(8,128)S(1)}, f32[48,128]{1,0:T(8,128)S(1)}, f32[48,128]{1,0:T(8,128)S(1)}, f32[48,128]{1,0:T(8,128)S(1)}) custom-call(f32[96,128]{1,0:T(8,128)S(1)} %get-tuple-element.22.refs_0_, f32[96,128]{1,0:T(8,128)S(1)} %collective-permute-done.1.refs_0_.refs_1_, f32[96,128]{1,0:T(8,128)S(1)} %collective-permute-done.2.refs_1_.refs_2_, ...), custom_call_target="tpu_custom_call" | custom-call | tf_op jit(solution)/shard_map/pallas_call | solution.py:74
  27.5 2.3 %collective-permute-start.8 = (f32[48,128]{1,0:T(8,128)S(1)}, f32[48,128]{1,0:T(8,128)S(1)}, u32[]{:S(2)}, u32[]{:S(2)}) collective-permute-start(f32[48,128]{1,0:T(8,128)S(1)} %get-tuple-element.35), channel_id=1, source_target_pairs={{0,24},{8,16},{16,8},{24,0},{1,25},{9,17},{17,9},{25,1},{2,26},{10... | collective-permute-start | bytes 73736 | tf_op jit(solution)/shard_map/ppermute | solution.py:37
  29.8 0.2 collective-permute-start.9
  30.0 2.0 %collective-permute-start.10 = (f32[48,128]{1,0:T(8,128)S(1)}, f32[48,128]{1,0:T(8,128)S(1)}, u32[]{:S(2)}, u32[]{:S(2)}) collective-permute-start(f32[48,128]{1,0:T(8,128)S(1)} %get-tuple-element.37), channel_id=1, source_target_pairs={{0,8},{8,0},{16,24},{24,16},{1,9},{9,1},{17,25},{25,17},{2,10},{10... | collective-permute-start | bytes 73736 | tf_op jit(solution)/shard_map/ppermute | solution.py:37
  32.0 1.2 %collective-permute-done.8.refs_1_ = f32[48,128]{1,0:T(8,128)S(1)} collective-permute-done((f32[48,128]{1,0:T(8,128)S(1)}, f32[48,128]{1,0:T(8,128)S(1)}, u32[]{:S(2)}, u32[]{:S(2)}) %collective-permute-start.8) | collective-permute-done | bytes 24608 | tf_op jit(solution)/shard_map/ppermute | solution.py:37
  33.2 1.4 %collective-permute-done.9.refs_2_ = f32[48,128]{1,0:T(8,128)S(1)} collective-permute-done((f32[48,128]{1,0:T(8,128)S(1)}, f32[48,128]{1,0:T(8,128)S(1)}, u32[]{:S(2)}, u32[]{:S(2)}) %collective-permute-start.9) | collective-permute-done | bytes 24608 | tf_op jit(solution)/shard_map/ppermute | solution.py:37
  34.6 0.8 %shard_map.93 = (f32[2,64,128]{2,1,0:T(8,128)}, f32[64,128]{1,0:T(8,128)}) custom-call(f32[48,128]{1,0:T(8,128)S(1)} %get-tuple-element.34.refs_0_, f32[48,128]{1,0:T(8,128)S(1)} %collective-permute-done.8.refs_1_, f32[48,128]{1,0:T(8,128)S(1)} %collective-permute-done.9.refs_2_, f32[48,128]{1,0:T(8,128)S(1)} %collective-permute-done.10.refs_3_), custom_call_target="tpu_custom_call" | custom-call | tf_op jit(solution)/shard_map/pallas_call | solution.py:74
  (6 shorter events, 0.1 us)
Async XLA Ops:
  1.7 1.4 %collective-permute-start = (f32[80,128]{1,0:T(8,128)S(1)}, f32[80,128]{1,0:T(8,128)S(1)}, u32[]{:S(2)}, u32[]{:S(2)}) collective-permute-start(f32[80,128]{1,0:T(8,128)S(1)} %get-tuple-element.21), channel_id=1, source_target_pairs={{0,1},{1,0},{2,3},{3,2},{4,5},{5,4},{6,7},{7,6},{8,9},{9,8},{10,11... | collective-permute-start | bytes 122888 | tf_op jit(solution)/shard_map/ppermute | solution.py:68
  3.4 7.2 %collective-permute-start.1 = (f32[96,128]{1,0:T(8,128)S(1)}, f32[96,128]{1,0:T(8,128)S(1)}, u32[]{:S(2)}, u32[]{:S(2)}) collective-permute-start(f32[96,128]{1,0:T(8,128)S(1)} %get-tuple-element.23), channel_id=1, source_target_pairs={{0,24},{8,16},{16,8},{24,0},{1,25},{9,17},{17,9},{25,1},{2,26},{10... | collective-permute-start | bytes 147464 | tf_op jit(solution)/shard_map/ppermute | solution.py:37
  8.4 5.0 %collective-permute-start.2 = (f32[96,128]{1,0:T(8,128)S(1)}, f32[96,128]{1,0:T(8,128)S(1)}, u32[]{:S(2)}, u32[]{:S(2)}) collective-permute-start(f32[96,128]{1,0:T(8,128)S(1)} %get-tuple-element.24), channel_id=1, source_target_pairs={{0,16},{8,24},{16,0},{24,8},{1,17},{9,25},{17,1},{25,9},{2,18},{10... | collective-permute-start | bytes 147464 | tf_op jit(solution)/shard_map/ppermute | solution.py:37
  8.4 5.0 %collective-permute-start.3 = (f32[96,128]{1,0:T(8,128)S(1)}, f32[96,128]{1,0:T(8,128)S(1)}, u32[]{:S(2)}, u32[]{:S(2)}) collective-permute-start(f32[96,128]{1,0:T(8,128)S(1)} %get-tuple-element.25), channel_id=1, source_target_pairs={{0,8},{8,0},{16,24},{24,16},{1,9},{9,1},{17,25},{25,17},{2,10},{10... | collective-permute-start | bytes 147464 | tf_op jit(solution)/shard_map/ppermute | solution.py:37
  14.7 9.2 %collective-permute-start.6 = (f32[120,128]{1,0:T(8,128)S(1)}, f32[120,128]{1,0:T(8,128)S(1)}, u32[]{:S(2)}, u32[]{:S(2)}) collective-permute-start(f32[120,128]{1,0:T(8,128)S(1)} %get-tuple-element.32), channel_id=1, source_target_pairs={{2,4},{4,2},{6,0},{0,6},{3,5},{5,3},{7,1},{1,7},{10,12},{12,10},{1... | collective-permute-start | bytes 184328 | tf_op jit(solution)/shard_map/ppermute | solution.py:68
  17.2 6.7 %collective-permute-start.7 = (f32[120,128]{1,0:T(8,128)S(1)}, f32[120,128]{1,0:T(8,128)S(1)}, u32[]{:S(2)}, u32[]{:S(2)}) collective-permute-start(f32[120,128]{1,0:T(8,128)S(1)} %get-tuple-element.33), channel_id=1, source_target_pairs={{0,2},{2,0},{4,6},{6,4},{1,3},{3,1},{5,7},{7,5},{8,10},{10,8},{12,... | collective-permute-start | bytes 184328 | tf_op jit(solution)/shard_map/ppermute | solution.py:68
  18.5 4.9 %collective-permute-start.4 = (f32[72,128]{1,0:T(8,128)S(1)}, f32[72,128]{1,0:T(8,128)S(1)}, u32[]{:S(2)}, u32[]{:S(2)}) collective-permute-start(f32[72,128]{1,0:T(8,128)S(1)} %get-tuple-element.30), channel_id=1, source_target_pairs={{2,4},{4,2},{6,0},{0,6},{3,5},{5,3},{7,1},{1,7},{10,12},{12,10},{1... | collective-permute-start | bytes 110600 | tf_op jit(solution)/shard_map/ppermute | solution.py:68
  20.0 4.0 %collective-permute-start.5 = (f32[72,128]{1,0:T(8,128)S(1)}, f32[72,128]{1,0:T(8,128)S(1)}, u32[]{:S(2)}, u32[]{:S(2)}) collective-permute-start(f32[72,128]{1,0:T(8,128)S(1)} %get-tuple-element.31), channel_id=1, source_target_pairs={{0,2},{2,0},{4,6},{6,4},{1,3},{3,1},{5,7},{7,5},{8,10},{10,8},{12,... | collective-permute-start | bytes 110600 | tf_op jit(solution)/shard_map/ppermute | solution.py:68
  27.5 5.7 %collective-permute-start.8 = (f32[48,128]{1,0:T(8,128)S(1)}, f32[48,128]{1,0:T(8,128)S(1)}, u32[]{:S(2)}, u32[]{:S(2)}) collective-permute-start(f32[48,128]{1,0:T(8,128)S(1)} %get-tuple-element.35), channel_id=1, source_target_pairs={{0,24},{8,16},{16,8},{24,0},{1,25},{9,17},{17,9},{25,1},{2,26},{10... | collective-permute-start | bytes 73736 | tf_op jit(solution)/shard_map/ppermute | solution.py:37
  29.8 4.8 %collective-permute-start.9 = (f32[48,128]{1,0:T(8,128)S(1)}, f32[48,128]{1,0:T(8,128)S(1)}, u32[]{:S(2)}, u32[]{:S(2)}) collective-permute-start(f32[48,128]{1,0:T(8,128)S(1)} %get-tuple-element.36), channel_id=1, source_target_pairs={{0,16},{8,24},{16,0},{24,8},{1,17},{9,25},{17,1},{25,9},{2,18},{10... | collective-permute-start | bytes 73736 | tf_op jit(solution)/shard_map/ppermute | solution.py:37
  30.0 4.6 %collective-permute-start.10 = (f32[48,128]{1,0:T(8,128)S(1)}, f32[48,128]{1,0:T(8,128)S(1)}, u32[]{:S(2)}, u32[]{:S(2)}) collective-permute-start(f32[48,128]{1,0:T(8,128)S(1)} %get-tuple-element.37), channel_id=1, source_target_pairs={{0,8},{8,0},{16,24},{24,16},{1,9},{9,1},{17,25},{25,17},{2,10},{10... | collective-permute-start | bytes 73736 | tf_op jit(solution)/shard_map/ppermute | solution.py:37

commit v6 on v5

--- a/solution.py
+++ b/solution.py
@@ -197,7 +197,7 @@
             else:
                 row.append(cell // cols)
                 col.append(cell % cols + shift)
-            parts.append((part1, part2, value - part1 - part2))
+            parts.append((part1, part2))
 
         def line(arrays, s):
             return jnp.concatenate([v[j : j + 1] for v in arrays for j in range(s * each, (s + 1) * each)], axis=1)
@@ -207,13 +207,11 @@
             at_row = down == narrow(line(row, s))
             at_col = across == narrow(line(col, s))
             left = chosen(at_row, 1.0)
-            weights = [1.0] + [line([p[i] for p in parts], s) for i in range(3)]
+            weights = [1.0] + [line([p[i] for p in parts], s) for i in range(2)]
             right = jnp.concatenate([chosen(at_col, w) for w in weights], axis=0)
             out = lax.dot_general(left, right, (((1,), (1,)), ((), ())), preferred_element_type=jnp.float32)
             found[0].append(out[:, 0:width])
-            found[1].append(
-                out[:, width : 2 * width] + (out[:, 2 * width : 3 * width] + out[:, 3 * width : 4 * width])
-            )
+            found[1].append(out[:, width : 2 * width] + out[:, 2 * width : 3 * width])
         for i in range(2):
             pieces = found[i]
             if slices * width < LANES:

time: 35.6 us -> 35.2 us (0.989)
  Pallas kernels: 7.72 us -> 7.28 us
    pallas_call x8, Pallas kernels: 7.72 us -> 7.28 us  [call(): pl.pallas_call(kernel, out_shape=out_shape, in_specs=[pl.BlockSpec(memory...]
where the time goes in v6:
time: 35.2 us; the launch traced here: 35 us
  starting transfers between devices  15.7 us (45%)
  waiting for transfers between devices  11.3 us (32%)
  Pallas kernels  7.28 us (21%)
  between operations  0.68 us (2%)
    ppermute x6, starting transfers between devices, exchange(): lax.ppermute(value, axis, [(i, partner(i, number, count)) for i in range(...  10.1 us
    pallas_call x8, Pallas kernels, call(): pl.pallas_call(kernel, out_shape=out_shape, in_specs=[pl.BlockSpec(memory...  7.28 us
    ppermute x6, waiting for transfers between devices, exchange(): lax.ppermute(value, axis, [(i, partner(i, number, count)) for i in range(...  6.97 us
    ppermute x5, starting transfers between devices, swap_all(): out.append(lax.ppermute(value, axis, pairs))  5.64 us
    ppermute x5, waiting for transfers between devices, swap_all(): out.append(lax.ppermute(value, axis, pairs))  4.3 us
  transfers between devices with their start and end apart: 11, of which 7 were waited for; matrix products, arithmetic and copies ran while one was open for 0% of the time, Pallas kernels for 2%

profile of v6, /device:TPU:0, one launch (start us, length us, event | category | flops | bytes accessed | tf_op | source)
XLA Modules:
  0.0 35.0 jit_solution(8322042613443370706)
XLA Ops:
  0.6 1.0 %shard_map.86 = (f32[400,128]{1,0:T(8,128)S(1)}, f32[80,128]{1,0:T(8,128)S(1)}) custom-call(f32[2,64,128]{2,1,0:T(8,128)} %refs_0_.1, f32[64,128]{1,0:T(8,128)} %refs_1_.1, f32[64,128]{1,0:T(8,128)} %refs_2_.1, s32[64,128]{1,0:T(8,128)} %refs_3_.1, f32[64,128]{1,0:T(8,128)} %refs_4_.1, s32[8,128]{1,0:T(8,128)} %bitcast.2, f32[8,128]{1,0:T(8,128)} %bitcast.3), custom_call_target="tpu_custom_call" | custom-call | tf_op jit(solution)/shard_map/pallas_call | solution.py:74
  1.7 0.6 %collective-permute-start = (f32[80,128]{1,0:T(8,128)S(1)}, f32[80,128]{1,0:T(8,128)S(1)}, u32[]{:S(2)}, u32[]{:S(2)}) collective-permute-start(f32[80,128]{1,0:T(8,128)S(1)} %get-tuple-element.21), channel_id=1, source_target_pairs={{0,1},{1,0},{2,3},{3,2},{4,5},{5,4},{6,7},{7,6},{8,9},{9,8},{10,11... | collective-permute-start | bytes 122888 | tf_op jit(solution)/shard_map/ppermute | solution.py:68
  2.2 0.9 %collective-permute-done.refs_1_ = f32[80,128]{1,0:T(8,128)S(1)} collective-permute-done((f32[80,128]{1,0:T(8,128)S(1)}, f32[80,128]{1,0:T(8,128)S(1)}, u32[]{:S(2)}, u32[]{:S(2)}) %collective-permute-start) | collective-permute-done | bytes 40992 | tf_op jit(solution)/shard_map/ppermute | solution.py:68
  3.1 0.3 shard_map.87
  3.4 5.0 %collective-permute-start.1 = (f32[96,128]{1,0:T(8,128)S(1)}, f32[96,128]{1,0:T(8,128)S(1)}, u32[]{:S(2)}, u32[]{:S(2)}) collective-permute-start(f32[96,128]{1,0:T(8,128)S(1)} %get-tuple-element.23), channel_id=1, source_target_pairs={{0,24},{8,16},{16,8},{24,0},{1,25},{9,17},{17,9},{25,1},{2,26},{10... | collective-permute-start | bytes 147464 | tf_op jit(solution)/shard_map/ppermute | solution.py:37
  8.4 0.0 collective-permute-start.2
  8.4 0.6 %collective-permute-start.3 = (f32[96,128]{1,0:T(8,128)S(1)}, f32[96,128]{1,0:T(8,128)S(1)}, u32[]{:S(2)}, u32[]{:S(2)}) collective-permute-start(f32[96,128]{1,0:T(8,128)S(1)} %get-tuple-element.25), channel_id=1, source_target_pairs={{0,8},{8,0},{16,24},{24,16},{1,9},{9,1},{17,25},{25,17},{2,10},{10... | collective-permute-start | bytes 147464 | tf_op jit(solution)/shard_map/ppermute | solution.py:37
  9.0 1.5 %collective-permute-done.1.refs_0_.refs_1_ = f32[96,128]{1,0:T(8,128)S(1)} collective-permute-done((f32[96,128]{1,0:T(8,128)S(1)}, f32[96,128]{1,0:T(8,128)S(1)}, u32[]{:S(2)}, u32[]{:S(2)}) %collective-permute-start.1) | collective-permute-done | bytes 49184 | tf_op jit(solution)/shard_map/ppermute | solution.py:37
  10.6 2.8 %collective-permute-done.2.refs_1_.refs_2_ = f32[96,128]{1,0:T(8,128)S(1)} collective-permute-done((f32[96,128]{1,0:T(8,128)S(1)}, f32[96,128]{1,0:T(8,128)S(1)}, u32[]{:S(2)}, u32[]{:S(2)}) %collective-permute-start.2) | collective-permute-done | bytes 49184 | tf_op jit(solution)/shard_map/ppermute | solution.py:37
  13.4 1.0 %shard_map.89 = (f32[2,64,128]{2,1,0:T(8,128)S(1)}, f32[2,64,128]{2,1,0:T(8,128)S(1)}, f32[2,64,128]{2,1,0:T(8,128)S(1)}) custom-call(f32[96,128]{1,0:T(8,128)S(1)} %collective-permute-done.1.refs_0_.refs_1_, f32[96,128]{1,0:T(8,128)S(1)} %collective-permute-done.2.refs_1_.refs_2_, f32[96,128]{1,0:T(8,128)S(1)} %collective-permute-done.3.refs_2_.refs_3_), custom_call_target="tpu_custom_call" | custom-call | tf_op jit(solution)/shard_map/pallas_call | solution.py:74
  14.4 2.5 %collective-permute-start.6 = (f32[120,128]{1,0:T(8,128)S(1)}, f32[120,128]{1,0:T(8,128)S(1)}, u32[]{:S(2)}, u32[]{:S(2)}) collective-permute-start(f32[120,128]{1,0:T(8,128)S(1)} %get-tuple-element.32), channel_id=1, source_target_pairs={{2,4},{4,2},{6,0},{0,6},{3,5},{5,3},{7,1},{1,7},{10,12},{12,10},{1... | collective-permute-start | bytes 184328 | tf_op jit(solution)/shard_map/ppermute | solution.py:68
  16.9 0.5 %collective-permute-start.7 = (f32[120,128]{1,0:T(8,128)S(1)}, f32[120,128]{1,0:T(8,128)S(1)}, u32[]{:S(2)}, u32[]{:S(2)}) collective-permute-start(f32[120,128]{1,0:T(8,128)S(1)} %get-tuple-element.33), channel_id=1, source_target_pairs={{0,2},{2,0},{4,6},{6,4},{1,3},{3,1},{5,7},{7,5},{8,10},{10,8},{12,... | collective-permute-start | bytes 184328 | tf_op jit(solution)/shard_map/ppermute | solution.py:68
  17.5 0.5 %shard_map.88.refs_1_.refs_5_ = f32[2,64,128]{2,1,0:T(8,128)S(1)} custom-call(f32[96,128]{1,0:T(8,128)S(1)} %get-tuple-element.22.refs_0_), custom_call_target="tpu_custom_call" | custom-call | tf_op jit(solution)/shard_map/pallas_call | solution.py:74
  18.0 1.5 %collective-permute-start.4 = (f32[72,128]{1,0:T(8,128)S(1)}, f32[72,128]{1,0:T(8,128)S(1)}, u32[]{:S(2)}, u32[]{:S(2)}) collective-permute-start(f32[72,128]{1,0:T(8,128)S(1)} %get-tuple-element.30), channel_id=1, source_target_pairs={{2,4},{4,2},{6,0},{0,6},{3,5},{5,3},{7,1},{1,7},{10,12},{12,10},{1... | collective-permute-start | bytes 110600 | tf_op jit(solution)/shard_map/ppermute | solution.py:68
  19.5 0.5 %collective-permute-start.5 = (f32[72,128]{1,0:T(8,128)S(1)}, f32[72,128]{1,0:T(8,128)S(1)}, u32[]{:S(2)}, u32[]{:S(2)}) collective-permute-start(f32[72,128]{1,0:T(8,128)S(1)} %get-tuple-element.31), channel_id=1, source_target_pairs={{0,2},{2,0},{4,6},{6,4},{1,3},{3,1},{5,7},{7,5},{8,10},{10,8},{12,... | collective-permute-start | bytes 110600 | tf_op jit(solution)/shard_map/ppermute | solution.py:68
  20.1 2.9 %collective-permute-done.4.refs_9_ = f32[72,128]{1,0:T(8,128)S(1)} collective-permute-done((f32[72,128]{1,0:T(8,128)S(1)}, f32[72,128]{1,0:T(8,128)S(1)}, u32[]{:S(2)}, u32[]{:S(2)}) %collective-permute-start.4) | collective-permute-done | bytes 36896 | tf_op jit(solution)/shard_map/ppermute | solution.py:68
  22.9 0.5 %collective-permute-done.5.refs_10_ = f32[72,128]{1,0:T(8,128)S(1)} collective-permute-done((f32[72,128]{1,0:T(8,128)S(1)}, f32[72,128]{1,0:T(8,128)S(1)}, u32[]{:S(2)}, u32[]{:S(2)}) %collective-permute-start.5) | collective-permute-done | bytes 36896 | tf_op jit(solution)/shard_map/ppermute | solution.py:68
  23.5 3.6 %shard_map.92 = (f32[48,128]{1,0:T(8,128)S(1)}, f32[48,128]{1,0:T(8,128)S(1)}, f32[48,128]{1,0:T(8,128)S(1)}, f32[48,128]{1,0:T(8,128)S(1)}) custom-call(f32[96,128]{1,0:T(8,128)S(1)} %get-tuple-element.22.refs_0_, f32[96,128]{1,0:T(8,128)S(1)} %collective-permute-done.1.refs_0_.refs_1_, f32[96,128]{1,0:T(8,128)S(1)} %collective-permute-done.2.refs_1_.refs_2_, ...), custom_call_target="tpu_custom_call" | custom-call | tf_op jit(solution)/shard_map/pallas_call | solution.py:74
  27.1 2.3 %collective-permute-start.8 = (f32[48,128]{1,0:T(8,128)S(1)}, f32[48,128]{1,0:T(8,128)S(1)}, u32[]{:S(2)}, u32[]{:S(2)}) collective-permute-start(f32[48,128]{1,0:T(8,128)S(1)} %get-tuple-element.35), channel_id=1, source_target_pairs={{0,24},{8,16},{16,8},{24,0},{1,25},{9,17},{17,9},{25,1},{2,26},{10... | collective-permute-start | bytes 73736 | tf_op jit(solution)/shard_map/ppermute | solution.py:37
  29.3 0.2 collective-permute-start.9
  29.5 2.0 %collective-permute-start.10 = (f32[48,128]{1,0:T(8,128)S(1)}, f32[48,128]{1,0:T(8,128)S(1)}, u32[]{:S(2)}, u32[]{:S(2)}) collective-permute-start(f32[48,128]{1,0:T(8,128)S(1)} %get-tuple-element.37), channel_id=1, source_target_pairs={{0,8},{8,0},{16,24},{24,16},{1,9},{9,1},{17,25},{25,17},{2,10},{10... | collective-permute-start | bytes 73736 | tf_op jit(solution)/shard_map/ppermute | solution.py:37
  31.5 1.2 %collective-permute-done.8.refs_1_ = f32[48,128]{1,0:T(8,128)S(1)} collective-permute-done((f32[48,128]{1,0:T(8,128)S(1)}, f32[48,128]{1,0:T(8,128)S(1)}, u32[]{:S(2)}, u32[]{:S(2)}) %collective-permute-start.8) | collective-permute-done | bytes 24608 | tf_op jit(solution)/shard_map/ppermute | solution.py:37
  32.8 1.4 %collective-permute-done.9.refs_2_ = f32[48,128]{1,0:T(8,128)S(1)} collective-permute-done((f32[48,128]{1,0:T(8,128)S(1)}, f32[48,128]{1,0:T(8,128)S(1)}, u32[]{:S(2)}, u32[]{:S(2)}) %collective-permute-start.9) | collective-permute-done | bytes 24608 | tf_op jit(solution)/shard_map/ppermute | solution.py:37
  34.2 0.8 %shard_map.93 = (f32[2,64,128]{2,1,0:T(8,128)}, f32[64,128]{1,0:T(8,128)}) custom-call(f32[48,128]{1,0:T(8,128)S(1)} %get-tuple-element.34.refs_0_, f32[48,128]{1,0:T(8,128)S(1)} %collective-permute-done.8.refs_1_, f32[48,128]{1,0:T(8,128)S(1)} %collective-permute-done.9.refs_2_, f32[48,128]{1,0:T(8,128)S(1)} %collective-permute-done.10.refs_3_), custom_call_target="tpu_custom_call" | custom-call | tf_op jit(solution)/shard_map/pallas_call | solution.py:74
  (6 shorter events, 0.0 us)
Async XLA Ops:
  1.7 1.4 %collective-permute-start = (f32[80,128]{1,0:T(8,128)S(1)}, f32[80,128]{1,0:T(8,128)S(1)}, u32[]{:S(2)}, u32[]{:S(2)}) collective-permute-start(f32[80,128]{1,0:T(8,128)S(1)} %get-tuple-element.21), channel_id=1, source_target_pairs={{0,1},{1,0},{2,3},{3,2},{4,5},{5,4},{6,7},{7,6},{8,9},{9,8},{10,11... | collective-permute-start | bytes 122888 | tf_op jit(solution)/shard_map/ppermute | solution.py:68
  3.4 7.2 %collective-permute-start.1 = (f32[96,128]{1,0:T(8,128)S(1)}, f32[96,128]{1,0:T(8,128)S(1)}, u32[]{:S(2)}, u32[]{:S(2)}) collective-permute-start(f32[96,128]{1,0:T(8,128)S(1)} %get-tuple-element.23), channel_id=1, source_target_pairs={{0,24},{8,16},{16,8},{24,0},{1,25},{9,17},{17,9},{25,1},{2,26},{10... | collective-permute-start | bytes 147464 | tf_op jit(solution)/shard_map/ppermute | solution.py:37
  8.4 5.0 %collective-permute-start.2 = (f32[96,128]{1,0:T(8,128)S(1)}, f32[96,128]{1,0:T(8,128)S(1)}, u32[]{:S(2)}, u32[]{:S(2)}) collective-permute-start(f32[96,128]{1,0:T(8,128)S(1)} %get-tuple-element.24), channel_id=1, source_target_pairs={{0,16},{8,24},{16,0},{24,8},{1,17},{9,25},{17,1},{25,9},{2,18},{10... | collective-permute-start | bytes 147464 | tf_op jit(solution)/shard_map/ppermute | solution.py:37
  8.4 5.0 %collective-permute-start.3 = (f32[96,128]{1,0:T(8,128)S(1)}, f32[96,128]{1,0:T(8,128)S(1)}, u32[]{:S(2)}, u32[]{:S(2)}) collective-permute-start(f32[96,128]{1,0:T(8,128)S(1)} %get-tuple-element.25), channel_id=1, source_target_pairs={{0,8},{8,0},{16,24},{24,16},{1,9},{9,1},{17,25},{25,17},{2,10},{10... | collective-permute-start | bytes 147464 | tf_op jit(solution)/shard_map/ppermute | solution.py:37
  14.4 9.1 %collective-permute-start.6 = (f32[120,128]{1,0:T(8,128)S(1)}, f32[120,128]{1,0:T(8,128)S(1)}, u32[]{:S(2)}, u32[]{:S(2)}) collective-permute-start(f32[120,128]{1,0:T(8,128)S(1)} %get-tuple-element.32), channel_id=1, source_target_pairs={{2,4},{4,2},{6,0},{0,6},{3,5},{5,3},{7,1},{1,7},{10,12},{12,10},{1... | collective-permute-start | bytes 184328 | tf_op jit(solution)/shard_map/ppermute | solution.py:68
  16.9 6.5 %collective-permute-start.7 = (f32[120,128]{1,0:T(8,128)S(1)}, f32[120,128]{1,0:T(8,128)S(1)}, u32[]{:S(2)}, u32[]{:S(2)}) collective-permute-start(f32[120,128]{1,0:T(8,128)S(1)} %get-tuple-element.33), channel_id=1, source_target_pairs={{0,2},{2,0},{4,6},{6,4},{1,3},{3,1},{5,7},{7,5},{8,10},{10,8},{12,... | collective-permute-start | bytes 184328 | tf_op jit(solution)/shard_map/ppermute | solution.py:68
  18.0 4.9 %collective-permute-start.4 = (f32[72,128]{1,0:T(8,128)S(1)}, f32[72,128]{1,0:T(8,128)S(1)}, u32[]{:S(2)}, u32[]{:S(2)}) collective-permute-start(f32[72,128]{1,0:T(8,128)S(1)} %get-tuple-element.30), channel_id=1, source_target_pairs={{2,4},{4,2},{6,0},{0,6},{3,5},{5,3},{7,1},{1,7},{10,12},{12,10},{1... | collective-permute-start | bytes 110600 | tf_op jit(solution)/shard_map/ppermute | solution.py:68
  19.5 4.0 %collective-permute-start.5 = (f32[72,128]{1,0:T(8,128)S(1)}, f32[72,128]{1,0:T(8,128)S(1)}, u32[]{:S(2)}, u32[]{:S(2)}) collective-permute-start(f32[72,128]{1,0:T(8,128)S(1)} %get-tuple-element.31), channel_id=1, source_target_pairs={{0,2},{2,0},{4,6},{6,4},{1,3},{3,1},{5,7},{7,5},{8,10},{10,8},{12,... | collective-permute-start | bytes 110600 | tf_op jit(solution)/shard_map/ppermute | solution.py:68
  27.1 5.7 %collective-permute-start.8 = (f32[48,128]{1,0:T(8,128)S(1)}, f32[48,128]{1,0:T(8,128)S(1)}, u32[]{:S(2)}, u32[]{:S(2)}) collective-permute-start(f32[48,128]{1,0:T(8,128)S(1)} %get-tuple-element.35), channel_id=1, source_target_pairs={{0,24},{8,16},{16,8},{24,0},{1,25},{9,17},{17,9},{25,1},{2,26},{10... | collective-permute-start | bytes 73736 | tf_op jit(solution)/shard_map/ppermute | solution.py:37
  29.3 4.8 %collective-permute-start.9 = (f32[48,128]{1,0:T(8,128)S(1)}, f32[48,128]{1,0:T(8,128)S(1)}, u32[]{:S(2)}, u32[]{:S(2)}) collective-permute-start(f32[48,128]{1,0:T(8,128)S(1)} %get-tuple-element.36), channel_id=1, source_target_pairs={{0,16},{8,24},{16,0},{24,8},{1,17},{9,25},{17,1},{25,9},{2,18},{10... | collective-permute-start | bytes 73736 | tf_op jit(solution)/shard_map/ppermute | solution.py:37
  29.5 4.6 %collective-permute-start.10 = (f32[48,128]{1,0:T(8,128)S(1)}, f32[48,128]{1,0:T(8,128)S(1)}, u32[]{:S(2)}, u32[]{:S(2)}) collective-permute-start(f32[48,128]{1,0:T(8,128)S(1)} %get-tuple-element.37), channel_id=1, source_target_pairs={{0,8},{8,0},{16,24},{24,16},{1,9},{9,1},{17,25},{25,17},{2,10},{10... | collective-permute-start | bytes 73736 | tf_op jit(solution)/shard_map/ppermute | solution.py:37

commit v7 on v6

--- a/solution.py
+++ b/solution.py
@@ -117,11 +117,10 @@
 
 
 def pack_kernel(dims, *refs):
-    slices, rows, cols, lists, group, sides, cut, width = dims
+    slices, rows, cols, lists, group, sides, cut, width, numbers = dims
     own = refs[0]
     near = refs[1 : 1 + sides]
-    blocks = refs[1 + sides : 1 + sides + group]
-    statics = refs[1 + sides + group]
+    blocks = dict(zip(numbers, refs[1 + sides :]))
     me = lax.axis_index("tm")
     y = lax.axis_index("gy")
     last_y = lax.axis_size("gy") - 1
@@ -152,13 +151,16 @@
             out = jnp.where(lane >= s * width, placed(number, start, s * width), out)
         return out
 
-    for k in range(group):
+    for k in numbers:
         start = partner(me, k, group) * cut - HALO
         blocks[k][0:rows] = packed(list(range(slices)), start)
         blocks[k][rows : rows + 2 * lists] = own[top : top + 2 * lists]
         for i, ref in enumerate(near):
             low = rows + 2 * lists * (i + 1)
             blocks[k][low : low + 2 * lists] = ref[rows : rows + 2 * lists]
+    if 0 not in numbers:
+        return
+    statics = refs[-1]
     start = me * cut - HALO
     statics[0] = packed([slices, slices + 1], start)
     statics[1] = packed([slices + 2, slices + 3], start)
@@ -447,11 +449,16 @@
     )
     near = swap_all(sends, "gy")
     dims = (slices, rows, cols, lists, group, sides, cut, width)
-    *blocks, statics = call(
-        functools.partial(pack_kernel, dims),
-        [f32(rows + 2 * lists * (1 + sides), LANES)] * group + [f32(2, rows, LANES)],
-        [own, *near],
+    block = f32(rows + 2 * lists * (1 + sides), LANES)
+    far = tuple(range(1, min(group, 2)))
+    rest = (0, *range(2, group))
+    first = []
+    if far:
+        first = call(functools.partial(pack_kernel, (*dims, far)), [block], [own, *near])
+    *others, statics = call(
+        functools.partial(pack_kernel, (*dims, rest)), [block] * len(rest) + [f32(2, rows, LANES)], [own, *near]
     )
+    blocks = [others[0], *first, *others[1:]]
     blocks = exchange_all(blocks)
     maps = []
     for part in (blocks[:1], blocks[1:]):

time: 35.2 us -> 35.9 us (1.020)
  waiting for transfers between devices: 11.3 us -> 12 us
    ppermute x6, waiting for transfers between devices: 6.97 us -> 7.68 us  [exchange(): lax.ppermute(value, axis, [(i, partner(i, number, count)) for i in range(...]
    pallas_call x8 -> x9, Pallas kernels: 7.28 us -> 7.34 us  [call(): pl.pallas_call(kernel, out_shape=out_shape, in_specs=[pl.BlockSpec(memory...]
  transfers between devices with their start and end apart: 11 -> 11, of which waited for: 7 -> 8; matrix products, arithmetic and copies ran while one was open for 0% -> 0% of each run, Pallas kernels for 2% -> 2%
where the time goes in v7:
time: 35.9 us; the launch traced here: 35.7 us
  starting transfers between devices  15.7 us (44%)
  waiting for transfers between devices  12 us (33%)
  Pallas kernels  7.34 us (20%)
  between operations  0.7 us (2%)
    ppermute x6, starting transfers between devices, exchange(): lax.ppermute(value, axis, [(i, partner(i, number, count)) for i in range(...  10.1 us
    ppermute x6, waiting for transfers between devices, exchange(): lax.ppermute(value, axis, [(i, partner(i, number, count)) for i in range(...  7.68 us
    pallas_call x9, Pallas kernels, call(): pl.pallas_call(kernel, out_shape=out_shape, in_specs=[pl.BlockSpec(memory...  7.34 us
    ppermute x5, starting transfers between devices, swap_all(): out.append(lax.ppermute(value, axis, pairs))  5.64 us
    ppermute x5, waiting for transfers between devices, swap_all(): out.append(lax.ppermute(value, axis, pairs))  4.29 us
  transfers between devices with their start and end apart: 11, of which 8 were waited for; matrix products, arithmetic and copies ran while one was open for 0% of the time, Pallas kernels for 2%

profile of v7, /device:TPU:0, one launch (start us, length us, event | category | flops | bytes accessed | tf_op | source)
XLA Modules:
  0.0 35.7 jit_solution(11278842745345800380)
XLA Ops:
  0.6 1.0 %shard_map.86 = (f32[400,128]{1,0:T(8,128)S(1)}, f32[80,128]{1,0:T(8,128)S(1)}) custom-call(f32[2,64,128]{2,1,0:T(8,128)} %refs_0_.1, f32[64,128]{1,0:T(8,128)} %refs_1_.1, f32[64,128]{1,0:T(8,128)} %refs_2_.1, s32[64,128]{1,0:T(8,128)} %refs_3_.1, f32[64,128]{1,0:T(8,128)} %refs_4_.1, s32[8,128]{1,0:T(8,128)} %bitcast.2, f32[8,128]{1,0:T(8,128)} %bitcast.3), custom_call_target="tpu_custom_call" | custom-call | tf_op jit(solution)/shard_map/pallas_call | solution.py:74
  1.7 0.6 %collective-permute-start = (f32[80,128]{1,0:T(8,128)S(1)}, f32[80,128]{1,0:T(8,128)S(1)}, u32[]{:S(2)}, u32[]{:S(2)}) collective-permute-start(f32[80,128]{1,0:T(8,128)S(1)} %get-tuple-element.20), channel_id=1, source_target_pairs={{0,1},{1,0},{2,3},{3,2},{4,5},{5,4},{6,7},{7,6},{8,9},{9,8},{10,11... | collective-permute-start | bytes 122888 | tf_op jit(solution)/shard_map/ppermute | solution.py:68
  2.2 0.9 %collective-permute-done.refs_1_ = f32[80,128]{1,0:T(8,128)S(1)} collective-permute-done((f32[80,128]{1,0:T(8,128)S(1)}, f32[80,128]{1,0:T(8,128)S(1)}, u32[]{:S(2)}, u32[]{:S(2)}) %collective-permute-start) | collective-permute-done | bytes 40992 | tf_op jit(solution)/shard_map/ppermute | solution.py:68
  3.1 0.2 shard_map.87
  3.4 4.0 %collective-permute-start.2 = (f32[96,128]{1,0:T(8,128)S(1)}, f32[96,128]{1,0:T(8,128)S(1)}, u32[]{:S(2)}, u32[]{:S(2)}) collective-permute-start(f32[96,128]{1,0:T(8,128)S(1)} %get-tuple-element.22), channel_id=1, source_target_pairs={{0,16},{8,24},{16,0},{24,8},{1,17},{9,25},{17,1},{25,9},{2,18},{10... | collective-permute-start | bytes 147464 | tf_op jit(solution)/shard_map/ppermute | solution.py:37
  7.3 1.6 %collective-permute-start.3 = (f32[96,128]{1,0:T(8,128)S(1)}, f32[96,128]{1,0:T(8,128)S(1)}, u32[]{:S(2)}, u32[]{:S(2)}) collective-permute-start(f32[96,128]{1,0:T(8,128)S(1)} %get-tuple-element.23), channel_id=1, source_target_pairs={{0,8},{8,0},{16,24},{24,16},{1,9},{9,1},{17,25},{25,17},{2,10},{10... | collective-permute-start | bytes 147464 | tf_op jit(solution)/shard_map/ppermute | solution.py:37
  8.9 0.1 shard_map.88
  9.1 0.3 collective-permute-done.2.refs_1_.refs_2_
  9.4 2.0 %collective-permute-done.3.refs_2_.refs_3_ = f32[96,128]{1,0:T(8,128)S(1)} collective-permute-done((f32[96,128]{1,0:T(8,128)S(1)}, f32[96,128]{1,0:T(8,128)S(1)}, u32[]{:S(2)}, u32[]{:S(2)}) %collective-permute-start.3) | collective-permute-done | bytes 49184 | tf_op jit(solution)/shard_map/ppermute | solution.py:37
  11.4 3.5 %collective-permute-done.1.refs_0_.refs_1_ = f32[96,128]{1,0:T(8,128)S(1)} collective-permute-done((f32[96,128]{1,0:T(8,128)S(1)}, f32[96,128]{1,0:T(8,128)S(1)}, u32[]{:S(2)}, u32[]{:S(2)}) %collective-permute-start.1) | collective-permute-done | bytes 49184 | tf_op jit(solution)/shard_map/ppermute | solution.py:37
  15.0 1.0 %shard_map.90 = (f32[2,64,128]{2,1,0:T(8,128)S(1)}, f32[2,64,128]{2,1,0:T(8,128)S(1)}, f32[2,64,128]{2,1,0:T(8,128)S(1)}) custom-call(f32[96,128]{1,0:T(8,128)S(1)} %collective-permute-done.1.refs_0_.refs_1_, f32[96,128]{1,0:T(8,128)S(1)} %collective-permute-done.2.refs_1_.refs_2_, f32[96,128]{1,0:T(8,128)S(1)} %collective-permute-done.3.refs_2_.refs_3_), custom_call_target="tpu_custom_call" | custom-call | tf_op jit(solution)/shard_map/pallas_call | solution.py:74
  16.0 2.5 %collective-permute-start.6 = (f32[120,128]{1,0:T(8,128)S(1)}, f32[120,128]{1,0:T(8,128)S(1)}, u32[]{:S(2)}, u32[]{:S(2)}) collective-permute-start(f32[120,128]{1,0:T(8,128)S(1)} %get-tuple-element.30), channel_id=1, source_target_pairs={{2,4},{4,2},{6,0},{0,6},{3,5},{5,3},{7,1},{1,7},{10,12},{12,10},{1... | collective-permute-start | bytes 184328 | tf_op jit(solution)/shard_map/ppermute | solution.py:68
  18.5 0.5 %collective-permute-start.7 = (f32[120,128]{1,0:T(8,128)S(1)}, f32[120,128]{1,0:T(8,128)S(1)}, u32[]{:S(2)}, u32[]{:S(2)}) collective-permute-start(f32[120,128]{1,0:T(8,128)S(1)} %get-tuple-element.31), channel_id=1, source_target_pairs={{0,2},{2,0},{4,6},{6,4},{1,3},{3,1},{5,7},{7,5},{8,10},{10,8},{12,... | collective-permute-start | bytes 184328 | tf_op jit(solution)/shard_map/ppermute | solution.py:68
  19.1 0.5 %shard_map.89.refs_1_.refs_5_ = f32[2,64,128]{2,1,0:T(8,128)S(1)} custom-call(f32[96,128]{1,0:T(8,128)S(1)} %get-tuple-element.21.refs_0_), custom_call_target="tpu_custom_call" | custom-call | tf_op jit(solution)/shard_map/pallas_call | solution.py:74
  19.6 1.5 %collective-permute-start.4 = (f32[72,128]{1,0:T(8,128)S(1)}, f32[72,128]{1,0:T(8,128)S(1)}, u32[]{:S(2)}, u32[]{:S(2)}) collective-permute-start(f32[72,128]{1,0:T(8,128)S(1)} %get-tuple-element.28), channel_id=1, source_target_pairs={{2,4},{4,2},{6,0},{0,6},{3,5},{5,3},{7,1},{1,7},{10,12},{12,10},{1... | collective-permute-start | bytes 110600 | tf_op jit(solution)/shard_map/ppermute | solution.py:68
  21.1 0.5 %collective-permute-start.5 = (f32[72,128]{1,0:T(8,128)S(1)}, f32[72,128]{1,0:T(8,128)S(1)}, u32[]{:S(2)}, u32[]{:S(2)}) collective-permute-start(f32[72,128]{1,0:T(8,128)S(1)} %get-tuple-element.29), channel_id=1, source_target_pairs={{0,2},{2,0},{4,6},{6,4},{1,3},{3,1},{5,7},{7,5},{8,10},{10,8},{12,... | collective-permute-start | bytes 110600 | tf_op jit(solution)/shard_map/ppermute | solution.py:68
  21.6 2.9 %collective-permute-done.4.refs_9_ = f32[72,128]{1,0:T(8,128)S(1)} collective-permute-done((f32[72,128]{1,0:T(8,128)S(1)}, f32[72,128]{1,0:T(8,128)S(1)}, u32[]{:S(2)}, u32[]{:S(2)}) %collective-permute-start.4) | collective-permute-done | bytes 36896 | tf_op jit(solution)/shard_map/ppermute | solution.py:68
  24.5 0.5 %collective-permute-done.5.refs_10_ = f32[72,128]{1,0:T(8,128)S(1)} collective-permute-done((f32[72,128]{1,0:T(8,128)S(1)}, f32[72,128]{1,0:T(8,128)S(1)}, u32[]{:S(2)}, u32[]{:S(2)}) %collective-permute-start.5) | collective-permute-done | bytes 36896 | tf_op jit(solution)/shard_map/ppermute | solution.py:68
  25.1 3.6 %shard_map.93 = (f32[48,128]{1,0:T(8,128)S(1)}, f32[48,128]{1,0:T(8,128)S(1)}, f32[48,128]{1,0:T(8,128)S(1)}, f32[48,128]{1,0:T(8,128)S(1)}) custom-call(f32[96,128]{1,0:T(8,128)S(1)} %get-tuple-element.21.refs_0_, f32[96,128]{1,0:T(8,128)S(1)} %collective-permute-done.1.refs_0_.refs_1_, f32[96,128]{1,0:T(8,128)S(1)} %collective-permute-done.2.refs_1_.refs_2_, ...), custom_call_target="tpu_custom_call" | custom-call | tf_op jit(solution)/shard_map/pallas_call | solution.py:74
  28.7 0.4 %collective-permute-start.8 = (f32[48,128]{1,0:T(8,128)S(1)}, f32[48,128]{1,0:T(8,128)S(1)}, u32[]{:S(2)}, u32[]{:S(2)}) collective-permute-start(f32[48,128]{1,0:T(8,128)S(1)} %get-tuple-element.33), channel_id=1, source_target_pairs={{0,24},{8,16},{16,8},{24,0},{1,25},{9,17},{17,9},{25,1},{2,26},{10... | collective-permute-start | bytes 73736 | tf_op jit(solution)/shard_map/ppermute | solution.py:37
  29.1 4.0 %collective-permute-start.10 = (f32[48,128]{1,0:T(8,128)S(1)}, f32[48,128]{1,0:T(8,128)S(1)}, u32[]{:S(2)}, u32[]{:S(2)}) collective-permute-start(f32[48,128]{1,0:T(8,128)S(1)} %get-tuple-element.35), channel_id=1, source_target_pairs={{0,8},{8,0},{16,24},{24,16},{1,9},{9,1},{17,25},{25,17},{2,10},{10... | collective-permute-start | bytes 73736 | tf_op jit(solution)/shard_map/ppermute | solution.py:37
  33.1 1.2 %collective-permute-done.8.refs_1_ = f32[48,128]{1,0:T(8,128)S(1)} collective-permute-done((f32[48,128]{1,0:T(8,128)S(1)}, f32[48,128]{1,0:T(8,128)S(1)}, u32[]{:S(2)}, u32[]{:S(2)}) %collective-permute-start.8) | collective-permute-done | bytes 24608 | tf_op jit(solution)/shard_map/ppermute | solution.py:37
  34.4 0.6 %collective-permute-done.10.refs_3_ = f32[48,128]{1,0:T(8,128)S(1)} collective-permute-done((f32[48,128]{1,0:T(8,128)S(1)}, f32[48,128]{1,0:T(8,128)S(1)}, u32[]{:S(2)}, u32[]{:S(2)}) %collective-permute-start.10) | collective-permute-done | bytes 24608 | tf_op jit(solution)/shard_map/ppermute | solution.py:37
  34.9 0.8 %shard_map.94 = (f32[2,64,128]{2,1,0:T(8,128)}, f32[64,128]{1,0:T(8,128)}) custom-call(f32[48,128]{1,0:T(8,128)S(1)} %get-tuple-element.32.refs_0_, f32[48,128]{1,0:T(8,128)S(1)} %collective-permute-done.8.refs_1_, f32[48,128]{1,0:T(8,128)S(1)} %collective-permute-done.9.refs_2_, f32[48,128]{1,0:T(8,128)S(1)} %collective-permute-done.10.refs_3_), custom_call_target="tpu_custom_call" | custom-call | tf_op jit(solution)/shard_map/pallas_call | solution.py:74
  (7 shorter events, 0.1 us)
Async XLA Ops:
  1.7 1.4 %collective-permute-start = (f32[80,128]{1,0:T(8,128)S(1)}, f32[80,128]{1,0:T(8,128)S(1)}, u32[]{:S(2)}, u32[]{:S(2)}) collective-permute-start(f32[80,128]{1,0:T(8,128)S(1)} %get-tuple-element.20), channel_id=1, source_target_pairs={{0,1},{1,0},{2,3},{3,2},{4,5},{5,4},{6,7},{7,6},{8,9},{9,8},{10,11... | collective-permute-start | bytes 122888 | tf_op jit(solution)/shard_map/ppermute | solution.py:68
  3.4 6.1 %collective-permute-start.2 = (f32[96,128]{1,0:T(8,128)S(1)}, f32[96,128]{1,0:T(8,128)S(1)}, u32[]{:S(2)}, u32[]{:S(2)}) collective-permute-start(f32[96,128]{1,0:T(8,128)S(1)} %get-tuple-element.22), channel_id=1, source_target_pairs={{0,16},{8,24},{16,0},{24,8},{1,17},{9,25},{17,1},{25,9},{2,18},{10... | collective-permute-start | bytes 147464 | tf_op jit(solution)/shard_map/ppermute | solution.py:37
  7.3 4.1 %collective-permute-start.3 = (f32[96,128]{1,0:T(8,128)S(1)}, f32[96,128]{1,0:T(8,128)S(1)}, u32[]{:S(2)}, u32[]{:S(2)}) collective-permute-start(f32[96,128]{1,0:T(8,128)S(1)} %get-tuple-element.23), channel_id=1, source_target_pairs={{0,8},{8,0},{16,24},{24,16},{1,9},{9,1},{17,25},{25,17},{2,10},{10... | collective-permute-start | bytes 147464 | tf_op jit(solution)/shard_map/ppermute | solution.py:37
  9.0 6.0 %collective-permute-start.1 = (f32[96,128]{1,0:T(8,128)S(1)}, f32[96,128]{1,0:T(8,128)S(1)}, u32[]{:S(2)}, u32[]{:S(2)}) collective-permute-start(f32[96,128]{1,0:T(8,128)S(1)} %shard_map.88), channel_id=1, source_target_pairs={{0,24},{8,16},{16,8},{24,0},{1,25},{9,17},{17,9},{25,1},{2,26},{10... | collective-permute-start | bytes 147464 | tf_op jit(solution)/shard_map/ppermute | solution.py:37
  16.0 9.0 %collective-permute-start.6 = (f32[120,128]{1,0:T(8,128)S(1)}, f32[120,128]{1,0:T(8,128)S(1)}, u32[]{:S(2)}, u32[]{:S(2)}) collective-permute-start(f32[120,128]{1,0:T(8,128)S(1)} %get-tuple-element.30), channel_id=1, source_target_pairs={{2,4},{4,2},{6,0},{0,6},{3,5},{5,3},{7,1},{1,7},{10,12},{12,10},{1... | collective-permute-start | bytes 184328 | tf_op jit(solution)/shard_map/ppermute | solution.py:68
  18.5 6.5 %collective-permute-start.7 = (f32[120,128]{1,0:T(8,128)S(1)}, f32[120,128]{1,0:T(8,128)S(1)}, u32[]{:S(2)}, u32[]{:S(2)}) collective-permute-start(f32[120,128]{1,0:T(8,128)S(1)} %get-tuple-element.31), channel_id=1, source_target_pairs={{0,2},{2,0},{4,6},{6,4},{1,3},{3,1},{5,7},{7,5},{8,10},{10,8},{12,... | collective-permute-start | bytes 184328 | tf_op jit(solution)/shard_map/ppermute | solution.py:68
  19.6 4.9 %collective-permute-start.4 = (f32[72,128]{1,0:T(8,128)S(1)}, f32[72,128]{1,0:T(8,128)S(1)}, u32[]{:S(2)}, u32[]{:S(2)}) collective-permute-start(f32[72,128]{1,0:T(8,128)S(1)} %get-tuple-element.28), channel_id=1, source_target_pairs={{2,4},{4,2},{6,0},{0,6},{3,5},{5,3},{7,1},{1,7},{10,12},{12,10},{1... | collective-permute-start | bytes 110600 | tf_op jit(solution)/shard_map/ppermute | solution.py:68
  21.1 4.0 %collective-permute-start.5 = (f32[72,128]{1,0:T(8,128)S(1)}, f32[72,128]{1,0:T(8,128)S(1)}, u32[]{:S(2)}, u32[]{:S(2)}) collective-permute-start(f32[72,128]{1,0:T(8,128)S(1)} %get-tuple-element.29), channel_id=1, source_target_pairs={{0,2},{2,0},{4,6},{6,4},{1,3},{3,1},{5,7},{7,5},{8,10},{10,8},{12,... | collective-permute-start | bytes 110600 | tf_op jit(solution)/shard_map/ppermute | solution.py:68
  28.7 5.7 %collective-permute-start.8 = (f32[48,128]{1,0:T(8,128)S(1)}, f32[48,128]{1,0:T(8,128)S(1)}, u32[]{:S(2)}, u32[]{:S(2)}) collective-permute-start(f32[48,128]{1,0:T(8,128)S(1)} %get-tuple-element.33), channel_id=1, source_target_pairs={{0,24},{8,16},{16,8},{24,0},{1,25},{9,17},{17,9},{25,1},{2,26},{10... | collective-permute-start | bytes 73736 | tf_op jit(solution)/shard_map/ppermute | solution.py:37
  29.1 5.3 %collective-permute-start.9 = (f32[48,128]{1,0:T(8,128)S(1)}, f32[48,128]{1,0:T(8,128)S(1)}, u32[]{:S(2)}, u32[]{:S(2)}) collective-permute-start(f32[48,128]{1,0:T(8,128)S(1)} %get-tuple-element.34), channel_id=1, source_target_pairs={{0,16},{8,24},{16,0},{24,8},{1,17},{9,25},{17,1},{25,9},{2,18},{10... | collective-permute-start | bytes 73736 | tf_op jit(solution)/shard_map/ppermute | solution.py:37
  29.1 5.8 %collective-permute-start.10 = (f32[48,128]{1,0:T(8,128)S(1)}, f32[48,128]{1,0:T(8,128)S(1)}, u32[]{:S(2)}, u32[]{:S(2)}) collective-permute-start(f32[48,128]{1,0:T(8,128)S(1)} %get-tuple-element.35), channel_id=1, source_target_pairs={{0,8},{8,0},{16,24},{24,16},{1,9},{9,1},{17,25},{25,17},{2,10},{10... | collective-permute-start | bytes 73736 | tf_op jit(solution)/shard_map/ppermute | solution.py:37
